TPU v7x, 32 devices: a whole 2x2x4 slice. The times are simulated.
32 devices in a mesh: dp: 16 (over z, x, core), tensor: 2 (over y).
Axes of the slice: x: 2, y: 2, z: 4, core: 2. Of those that a mesh axis runs over, the one named last changes fastest.
Arguments:
- hidden_in: bfloat16 [16, 561, 1024], P('dp', None, 'tensor'), may hold values from -6 to 6
- lengths: int32 [16], P('dp'), may hold values from 52 to 512, as said below
- boxes: int32 [16, 561, 2], P('dp'), may hold values from 0 to 1000
- w_qkv: bfloat16 [1024, 3, 1024], P(None, None, 'tensor'), may hold values from -0.1875 to 0.1875
- w_out: bfloat16 [1024, 1024], P('tensor'), may hold values from -1 to 1
- w_up: bfloat16 [1024, 4096], P(None, 'tensor'), may hold values from -0.1875 to 0.1875
- w_down: bfloat16 [4096, 1024], P('tensor'), may hold values from -0.09375 to 0.09375
- rel_keys: bfloat16 [3, 128, 1024], P(None, None, 'tensor'), may hold values from -6 to 6
- rel_queries: bfloat16 [3, 128, 1024], P(None, None, 'tensor'), may hold values from -6 to 6
- norm_gains: float32 [2, 1024], P(None, 'tensor'), may hold values from 0.25 to 1.75
- norm_shifts: float32 [2, 1024], P(None, 'tensor'), may hold values from -3 to 3
- out_grad: bfloat16 [16, 561, 1024], P('dp', None, 'tensor'), may hold values from -6 to 6
Outputs:
- hidden_out: bfloat16 [16, 561, 1024], P('dp', None, 'tensor')
- input_grad: bfloat16 [16, 561, 1024], P('dp', None, 'tensor')
- qkv_grad: float32 [1024, 3, 1024], P(None, None, 'tensor')
- out_weight_grad: float32 [1024, 1024], P('tensor')
- up_grad: float32 [1024, 4096], P(None, 'tensor')
- down_grad: float32 [4096, 1024], P('tensor')
- rel_keys_grad: float32 [3, 128, 1024], P(None, None, 'tensor')
- rel_queries_grad: float32 [3, 128, 1024], P(None, None, 'tensor')
- gains_grad: float32 [2, 1024], P(None, 'tensor')
- shifts_grad: float32 [2, 1024], P(None, 'tensor')
Inputs may be any that keep to these rules, and one draw needn't show every extreme that they name: `lengths`: text slot s of a document holds a real token when s is under its count; in every draw some document has all 512 text slots real.
All inputs are finite; a program needn't handle non-finite values.
Results may differ from a plain program's by a relative error of at most 0.02.
Values may be sent and summed in bfloat16 or wider, within the bound.
No kernel may reach another device: no remote copies, remote signals or barrier semaphores. Data moves between devices by JAX's collectives and lax.ppermute only.
A program may use at most 512 MiB of HBM per device.

v0:
```python
import math

import jax
import jax.numpy as jnp
from jax import lax
from jax.sharding import PartitionSpec as P

HEAD_DIM = 64
BUCKETS = 128
TEXT = 512
BOX_STEP = 16


NEG_LARGE = -1e30
EPSILON = 1e-05


def relative_buckets(box_doc):
    slot_count = box_doc.shape[0]
    middle = BUCKETS // 2
    places = jnp.arange(slot_count, dtype=jnp.int32)
    linear = jnp.clip(places[None, :] - places[:, None], -middle, middle - 1) + middle
    across = (
        jnp.clip((box_doc[None, :, 0] - box_doc[:, None, 0]) // BOX_STEP, -middle, middle - 1)
        + middle
    )
    upward = (
        jnp.clip((box_doc[None, :, 1] - box_doc[:, None, 1]) // BOX_STEP, -middle, middle - 1)
        + middle
    )
    return jnp.stack([linear, across, upward])


def pick_buckets(table, buckets):
    labels = jnp.arange(BUCKETS, dtype=jnp.int32)

    def pick_one_kind(inputs):
        kind_table, kind_buckets = inputs
        chosen = kind_buckets[None, :, :, None] == labels
        return jnp.sum(jnp.where(chosen, kind_table[:, :, None, :], 0.0), axis=-1)

    return jnp.sum(lax.map(pick_one_kind, (table, buckets)), axis=0)


def spread_buckets(grad_scores, buckets):
    labels = jnp.arange(BUCKETS, dtype=jnp.int32)

    def spread_one_kind(kind_buckets):
        chosen = kind_buckets[None, :, :, None] == labels
        return jnp.sum(jnp.where(chosen, grad_scores[:, :, :, None], 0.0), axis=2)

    return lax.map(spread_one_kind, buckets)


def score_block(queries, keys_doc, rel_k, rel_q, box_doc, length, score_scale):
    slot_count = queries.shape[0]
    buckets = relative_buckets(box_doc)
    content = jnp.einsum("ihe,jhe->hij", queries, keys_doc, preferred_element_type=jnp.float32)
    near_query = jnp.einsum("ihe,tbhe->thib", queries, rel_k, preferred_element_type=jnp.float32)
    near_key = jnp.einsum("jhe,tbhe->thjb", keys_doc, rel_q, preferred_element_type=jnp.float32)
    raw = (
        content
        + pick_buckets(near_query, buckets)
        + jnp.swapaxes(pick_buckets(near_key, buckets), 1, 2)
    )
    places = jnp.arange(slot_count, dtype=jnp.int32)
    valid = (places < length) | (places >= TEXT)
    return (jnp.where(valid[None, None, :], score_scale * raw, NEG_LARGE), buckets)


def norm_forward(values_in, gain, shift, model_width):
    row_total, row_square = lax.psum(
        (jnp.sum(values_in, axis=1), jnp.sum(values_in * values_in, axis=1)), "tensor"
    )
    mean_row = row_total / model_width
    scale_row = lax.rsqrt(row_square / model_width - mean_row * mean_row + EPSILON)
    normed = (values_in - mean_row[:, None]) * scale_row[:, None]
    return (normed * gain + shift, normed, scale_row)


def norm_backward(upstream, normed, scale_row, gain, model_width):
    scaled_up = upstream * gain
    first_sum, second_sum = lax.psum(
        (jnp.sum(scaled_up, axis=1), jnp.sum(scaled_up * normed, axis=1)), "tensor"
    )
    centered = (
        scaled_up - first_sum[:, None] / model_width - normed * second_sum[:, None] / model_width
    )
    return scale_row[:, None] * centered


def on_device(
    hidden_in,
    lengths,
    boxes,
    w_qkv,
    w_out,
    w_up,
    w_down,
    rel_keys,
    rel_queries,
    norm_gains,
    norm_shifts,
    out_grad,
):
    doc_count, slot_count, local_width = hidden_in.shape
    row_count = doc_count * slot_count
    model_width = w_qkv.shape[0]
    heads_here = local_width // HEAD_DIM
    score_scale = 1.0 / math.sqrt(3 * HEAD_DIM)
    rel_k = rel_keys.reshape(3, BUCKETS, heads_here, HEAD_DIM)
    rel_q = rel_queries.reshape(3, BUCKETS, heads_here, HEAD_DIM)
    local_rows = hidden_in.reshape(row_count, local_width)
    full_rows = lax.all_gather(local_rows, "tensor", axis=1, tiled=True)
    weight_qkv = w_qkv.reshape(model_width, 3 * local_width)
    projected = jnp.dot(full_rows, weight_qkv, preferred_element_type=jnp.float32).astype(
        jnp.bfloat16
    )
    projected = projected.reshape(doc_count, slot_count, 3, heads_here, HEAD_DIM)
    queries_all, keys_all, values_all = (projected[:, :, 0], projected[:, :, 1], projected[:, :, 2])

    def forward_doc(inputs):
        queries, keys_doc, values_doc, box_doc, length = inputs
        scores, _ = score_block(queries, keys_doc, rel_k, rel_q, box_doc, length, score_scale)
        top_score = jnp.max(scores, axis=-1, keepdims=True)
        log_total = top_score[..., 0] + jnp.log(jnp.sum(jnp.exp(scores - top_score), axis=-1))
        probs = jnp.exp(scores - log_total[..., None]).astype(jnp.bfloat16)
        context = jnp.einsum("hij,jhe->ihe", probs, values_doc, preferred_element_type=jnp.float32)
        return (context.astype(jnp.bfloat16), log_total)

    context, log_totals = lax.map(forward_doc, (queries_all, keys_all, values_all, boxes, lengths))
    context_rows = context.reshape(row_count, local_width)
    attn_terms = jnp.dot(context_rows, w_out, preferred_element_type=jnp.float32)
    attn_out = lax.psum_scatter(attn_terms, "tensor", scatter_dimension=1, tiled=True)
    first_sum_in = local_rows.astype(jnp.float32) + attn_out
    normed_first, unit_first, scale_first = norm_forward(
        first_sum_in, norm_gains[0], norm_shifts[0], model_width
    )
    normed_full = lax.all_gather(normed_first.astype(jnp.bfloat16), "tensor", axis=1, tiled=True)
    upper = jnp.dot(normed_full, w_up, preferred_element_type=jnp.float32)
    active = jax.nn.gelu(upper, approximate=False).astype(jnp.bfloat16)
    ffn_out = lax.psum_scatter(
        jnp.dot(active, w_down, preferred_element_type=jnp.float32).astype(jnp.bfloat16),
        "tensor",
        scatter_dimension=1,
        tiled=True,
    ).astype(jnp.float32)
    result, unit_second, scale_second = norm_forward(
        normed_first + ffn_out, norm_gains[1], norm_shifts[1], model_width
    )
    hidden_out = result.astype(jnp.bfloat16).reshape(doc_count, slot_count, local_width)
    upstream = out_grad.reshape(row_count, local_width).astype(jnp.float32)
    gain_second = jnp.sum(upstream * unit_second, axis=0)
    shift_second = jnp.sum(upstream, axis=0)
    grad_second = norm_backward(upstream, unit_second, scale_second, norm_gains[1], model_width)
    ffn_grad_full = lax.all_gather(grad_second.astype(jnp.bfloat16), "tensor", axis=1, tiled=True)
    down_grad = jnp.einsum("rf,rd->fd", active, ffn_grad_full, preferred_element_type=jnp.float32)
    grad_active = jnp.einsum("rd,fd->rf", ffn_grad_full, w_down, preferred_element_type=jnp.float32)
    _, gelu_pull = jax.vjp(lambda entry: jax.nn.gelu(entry, approximate=False), upper)
    grad_upper = gelu_pull(grad_active)[0].astype(jnp.bfloat16)
    up_grad = jnp.einsum("rd,rf->df", normed_full, grad_upper, preferred_element_type=jnp.float32)
    hidden_terms = jnp.einsum("rf,df->rd", grad_upper, w_up, preferred_element_type=jnp.float32)
    grad_hidden = grad_second + lax.psum_scatter(
        hidden_terms.astype(jnp.bfloat16), "tensor", scatter_dimension=1, tiled=True
    ).astype(jnp.float32)
    gain_first = jnp.sum(grad_hidden * unit_first, axis=0)
    shift_first = jnp.sum(grad_hidden, axis=0)
    grad_first = norm_backward(grad_hidden, unit_first, scale_first, norm_gains[0], model_width)
    attn_grad_full = lax.all_gather(grad_first.astype(jnp.bfloat16), "tensor", axis=1, tiled=True)
    out_weight_grad = jnp.einsum(
        "rc,rd->cd", context_rows, attn_grad_full, preferred_element_type=jnp.float32
    )
    grad_context = jnp.einsum(
        "rd,cd->rc", attn_grad_full, w_out, preferred_element_type=jnp.float32
    ).astype(jnp.bfloat16)
    grad_context = grad_context.reshape(doc_count, slot_count, heads_here, HEAD_DIM)

    def backward_doc(carry, inputs):
        queries, keys_doc, values_doc, box_doc, length, log_total, grad_ctx = inputs
        scores, buckets = score_block(queries, keys_doc, rel_k, rel_q, box_doc, length, score_scale)
        probs = jnp.exp(scores - log_total[..., None])
        grad_values = jnp.einsum(
            "hij,ihe->jhe", probs.astype(jnp.bfloat16), grad_ctx, preferred_element_type=jnp.float32
        )
        grad_probs = jnp.einsum(
            "ihe,jhe->hij", grad_ctx, values_doc, preferred_element_type=jnp.float32
        )
        inner = jnp.sum(probs * grad_probs, axis=-1, keepdims=True)
        grad_scores = (probs * (grad_probs - inner)).astype(jnp.bfloat16)
        scaled_grad = grad_scores.astype(jnp.float32) * score_scale
        grad_near_q = spread_buckets(scaled_grad, buckets).astype(jnp.bfloat16)
        grad_near_k = spread_buckets(jnp.swapaxes(scaled_grad, 1, 2), buckets).astype(jnp.bfloat16)
        grad_queries = score_scale * jnp.einsum(
            "hij,jhe->ihe", grad_scores, keys_doc, preferred_element_type=jnp.float32
        )
        grad_queries = grad_queries + jnp.einsum(
            "thib,tbhe->ihe", grad_near_q, rel_k, preferred_element_type=jnp.float32
        )
        grad_keys = score_scale * jnp.einsum(
            "hij,ihe->jhe", grad_scores, queries, preferred_element_type=jnp.float32
        )
        grad_keys = grad_keys + jnp.einsum(
            "thjb,tbhe->jhe", grad_near_k, rel_q, preferred_element_type=jnp.float32
        )
        rel_k_sum = carry[0] + jnp.einsum(
            "thib,ihe->tbhe", grad_near_q, queries, preferred_element_type=jnp.float32
        )
        rel_q_sum = carry[1] + jnp.einsum(
            "thjb,jhe->tbhe", grad_near_k, keys_doc, preferred_element_type=jnp.float32
        )
        grads_doc = jnp.stack(
            [
                grad_queries.astype(jnp.bfloat16),
                grad_keys.astype(jnp.bfloat16),
                grad_values.astype(jnp.bfloat16),
            ],
            axis=1,
        )
        return ((rel_k_sum, rel_q_sum), grads_doc)

    start_sums = (jnp.zeros(rel_k.shape, jnp.float32), jnp.zeros(rel_q.shape, jnp.float32))
    rel_sums, grad_projected = lax.scan(
        backward_doc,
        start_sums,
        (queries_all, keys_all, values_all, boxes, lengths, log_totals, grad_context),
    )
    rel_keys_grad = rel_sums[0].reshape(3, BUCKETS, local_width)
    rel_queries_grad = rel_sums[1].reshape(3, BUCKETS, local_width)
    grad_rows = grad_projected.reshape(row_count, 3 * local_width)
    qkv_grad = jnp.einsum(
        "rd,rc->dc", full_rows, grad_rows, preferred_element_type=jnp.float32
    ).reshape(model_width, 3, local_width)
    input_terms = jnp.einsum("rc,dc->rd", grad_rows, weight_qkv, preferred_element_type=jnp.float32)
    input_grad = grad_first + lax.psum_scatter(
        input_terms.astype(jnp.bfloat16), "tensor", scatter_dimension=1, tiled=True
    ).astype(jnp.float32)
    input_grad = input_grad.astype(jnp.bfloat16).reshape(doc_count, slot_count, local_width)
    (
        qkv_grad,
        out_weight_grad,
        up_grad,
        down_grad,
        rel_keys_grad,
        rel_queries_grad,
        gain_first,
        shift_first,
        gain_second,
        shift_second,
    ) = (
        lax.psum(qkv_grad.astype(jnp.bfloat16), "dp").astype(jnp.float32),
        lax.psum(out_weight_grad.astype(jnp.bfloat16), "dp").astype(jnp.float32),
        lax.psum(up_grad.astype(jnp.bfloat16), "dp").astype(jnp.float32),
        lax.psum(down_grad.astype(jnp.bfloat16), "dp").astype(jnp.float32),
        lax.psum(rel_keys_grad.astype(jnp.bfloat16), "dp").astype(jnp.float32),
        lax.psum(rel_queries_grad.astype(jnp.bfloat16), "dp").astype(jnp.float32),
        lax.psum(gain_first.astype(jnp.bfloat16), "dp").astype(jnp.float32),
        lax.psum(shift_first.astype(jnp.bfloat16), "dp").astype(jnp.float32),
        lax.psum(gain_second.astype(jnp.bfloat16), "dp").astype(jnp.float32),
        lax.psum(shift_second.astype(jnp.bfloat16), "dp").astype(jnp.float32),
    )
    gains_grad = jnp.stack([gain_first, gain_second])
    shifts_grad = jnp.stack([shift_first, shift_second])
    return (
        hidden_out,
        input_grad,
        qkv_grad,
        out_weight_grad,
        up_grad,
        down_grad,
        rel_keys_grad,
        rel_queries_grad,
        gains_grad,
        shifts_grad,
    )


def solution(mesh):
    in_specs = (
        P("dp", None, "tensor"),
        P("dp"),
        P("dp", None, None),
        P(None, None, "tensor"),
        P("tensor", None),
        P(None, "tensor"),
        P("tensor", None),
        P(None, None, "tensor"),
        P(None, None, "tensor"),
        P(None, "tensor"),
        P(None, "tensor"),
        P("dp", None, "tensor"),
    )
    out_specs = (
        P("dp", None, "tensor"),
        P("dp", None, "tensor"),
        P(None, None, "tensor"),
        P("tensor", None),
        P(None, "tensor"),
        P("tensor", None),
        P(None, None, "tensor"),
        P(None, None, "tensor"),
        P(None, "tensor"),
        P(None, "tensor"),
    )
    return jax.shard_map(
        on_device, mesh=mesh, in_specs=in_specs, out_specs=out_specs, check_vma=False
    )
```

profile of v0, /device:TPU:0, one launch (start us, length us, event | category | flops | bytes accessed | tf_op | source)
XLA Modules:
  0.0 7121.7 jit_solution(11558817213116256360)
XLA Ops:
  60.1 1785.7 %while.81 = (s32[]{:T(128)}, f32[3,8,561,561]{3,2,1,0:T(8,128)}, s32[3,561,561]{2,1,0:T(8,128)}, f32[3,8,561,128]{3,1,2,0:T(8,128)}, s32[]{:T(128)}) while((s32[]{:T(128)}, f32[3,8,561,561]{3,2,1,0:T(8,128)}, s32[3,561,561]{2,1,0:T(8,128)}, f32[3,8,561,128]{3,1,2,0:T(8,128)}, s32[]{:T(128)}) %tuple.116), condition=%wide.region_2.3_spmd.clone, body=%wide.region_0.2_spmd.clone.sunk | while | flops 682315136 | bytes 144717392 | solution.py:42
  112.5 441.5 %select_reduce_fusion.8 = f32[8,561,561]{0,2,1:T(8,128)} fusion(f32[8,561,128]{2,0,1:T(8,128)S(1)} %dynamic-slice_bitcast_fusion.12, pred[561,561,128]{2,1,0:T(8,128)(4,1)} %iota_compare_fusion.10), kind=kLoop, calls=%fused_computation.4.clone.1 | loop fusion | flops 642030848 | bytes 52653216 | tf_op jit(solution)/shard_map/while/body/eval_jaxpr/while/body/eval_jaxpr/reduce_sum | solution.py:40
  554.0 92.0 %copy.176 = f32[1,8,561,561]{3,2,1,0:T(8,128)} copy(f32[1,8,561,561]{1,3,2,0:T(8,128)} %bitcast.195) | data formatting | bytes 20142144 | tf_op jit(solution)/shard_map/while/body/eval_jaxpr/while/body/jit(dynamic_update_index_in_dim)/dynamic_update_slice | solution.py:42
  707.8 441.5 %select_reduce_fusion.8 = f32[8,561,561]{0,2,1:T(8,128)} fusion(f32[8,561,128]{2,0,1:T(8,128)S(1)} %dynamic-slice_bitcast_fusion.12, pred[561,561,128]{2,1,0:T(8,128)(4,1)} %iota_compare_fusion.10), kind=kLoop, calls=%fused_computation.4.clone.1 | loop fusion | flops 642030848 | bytes 52653216 | tf_op jit(solution)/shard_map/while/body/eval_jaxpr/while/body/eval_jaxpr/reduce_sum | solution.py:40
  1149.3 92.0 %copy.176 = f32[1,8,561,561]{3,2,1,0:T(8,128)} copy(f32[1,8,561,561]{1,3,2,0:T(8,128)} %bitcast.195) | data formatting | bytes 20142144 | tf_op jit(solution)/shard_map/while/body/eval_jaxpr/while/body/jit(dynamic_update_index_in_dim)/dynamic_update_slice | solution.py:42
  1253.9 49.1 iota_compare_fusion.10
  1303.0 441.5 %select_reduce_fusion.8 = f32[8,561,561]{0,2,1:T(8,128)} fusion(f32[8,561,128]{2,0,1:T(8,128)S(1)} %dynamic-slice_bitcast_fusion.12, pred[561,561,128]{2,1,0:T(8,128)(4,1)} %iota_compare_fusion.10), kind=kLoop, calls=%fused_computation.4.clone.1 | loop fusion | flops 642030848 | bytes 52653216 | tf_op jit(solution)/shard_map/while/body/eval_jaxpr/while/body/eval_jaxpr/reduce_sum | solution.py:40
  1744.5 92.0 %copy.176 = f32[1,8,561,561]{3,2,1,0:T(8,128)} copy(f32[1,8,561,561]{1,3,2,0:T(8,128)} %bitcast.195) | data formatting | bytes 20142144 | tf_op jit(solution)/shard_map/while/body/eval_jaxpr/while/body/jit(dynamic_update_index_in_dim)/dynamic_update_slice | solution.py:42
  1915.9 1785.7 %while.82 = (s32[]{:T(128)}, f32[3,8,561,561]{3,2,1,0:T(8,128)}, s32[3,561,561]{2,1,0:T(8,128)}, f32[3,8,561,128]{3,1,2,0:T(8,128)}, s32[]{:T(128)}) while((s32[]{:T(128)}, f32[3,8,561,561]{3,2,1,0:T(8,128)}, s32[3,561,561]{2,1,0:T(8,128)}, f32[3,8,561,128]{3,1,2,0:T(8,128)}, s32[]{:T(128)}) %tuple.147), condition=%wide.region_6.7_spmd.clone, body=%wide.region_4.6_spmd.clone.sunk | while | flops 682315136 | bytes 144717392 | solution.py:42
  1919.2 49.1 iota_compare_fusion.11
  1968.3 441.5 %select_reduce_fusion.9 = f32[8,561,561]{0,2,1:T(8,128)} fusion(f32[8,561,128]{2,0,1:T(8,128)S(1)} %dynamic-slice_bitcast_fusion.14, pred[561,561,128]{2,1,0:T(8,128)(4,1)} %iota_compare_fusion.11), kind=kLoop, calls=%fused_computation.9.clone.1 | loop fusion | flops 642030848 | bytes 52653216 | tf_op jit(solution)/shard_map/while/body/eval_jaxpr/while/body/eval_jaxpr/reduce_sum | solution.py:40
  2409.8 92.0 %copy.177 = f32[1,8,561,561]{3,2,1,0:T(8,128)} copy(f32[1,8,561,561]{1,3,2,0:T(8,128)} %bitcast.198) | data formatting | bytes 20142144 | tf_op jit(solution)/shard_map/while/body/eval_jaxpr/while/body/jit(dynamic_update_index_in_dim)/dynamic_update_slice | solution.py:42
  2514.5 49.1 iota_compare_fusion.11
  2563.6 441.5 %select_reduce_fusion.9 = f32[8,561,561]{0,2,1:T(8,128)} fusion(f32[8,561,128]{2,0,1:T(8,128)S(1)} %dynamic-slice_bitcast_fusion.14, pred[561,561,128]{2,1,0:T(8,128)(4,1)} %iota_compare_fusion.11), kind=kLoop, calls=%fused_computation.9.clone.1 | loop fusion | flops 642030848 | bytes 52653216 | tf_op jit(solution)/shard_map/while/body/eval_jaxpr/while/body/eval_jaxpr/reduce_sum | solution.py:40
  3005.1 92.0 %copy.177 = f32[1,8,561,561]{3,2,1,0:T(8,128)} copy(f32[1,8,561,561]{1,3,2,0:T(8,128)} %bitcast.198) | data formatting | bytes 20142144 | tf_op jit(solution)/shard_map/while/body/eval_jaxpr/while/body/jit(dynamic_update_index_in_dim)/dynamic_update_slice | solution.py:42
  3158.8 441.5 %select_reduce_fusion.9 = f32[8,561,561]{0,2,1:T(8,128)} fusion(f32[8,561,128]{2,0,1:T(8,128)S(1)} %dynamic-slice_bitcast_fusion.14, pred[561,561,128]{2,1,0:T(8,128)(4,1)} %iota_compare_fusion.11), kind=kLoop, calls=%fused_computation.9.clone.1 | loop fusion | flops 642030848 | bytes 52653216 | tf_op jit(solution)/shard_map/while/body/eval_jaxpr/while/body/eval_jaxpr/reduce_sum | solution.py:40
  3600.3 92.0 %copy.177 = f32[1,8,561,561]{3,2,1,0:T(8,128)} copy(f32[1,8,561,561]{1,3,2,0:T(8,128)} %bitcast.198) | data formatting | bytes 20142144 | tf_op jit(solution)/shard_map/while/body/eval_jaxpr/while/body/jit(dynamic_update_index_in_dim)/dynamic_update_slice | solution.py:42
  4047.5 77.2 %copy.109 = f32[8,561,561]{0,2,1:T(8,128)} copy(f32[8,561,561]{2,1,0:T(8,128)} %convert_multiply_fusion) | data formatting | bytes 20142144
  4126.9 1299.0 %while.84 = (s32[]{:T(128)}, bf16[3,8,561,128]{3,1,2,0:T(8,128)(2,1)}, s32[3,561,561]{2,1,0:T(8,128)}, f32[8,561,561]{0,2,1:T(8,128)}, s32[]{:T(128)}) while((s32[]{:T(128)}, bf16[3,8,561,128]{3,1,2,0:T(8,128)(2,1)}, s32[3,561,561]{2,1,0:T(8,128)}, f32[8,561,561]{0,2,1:T(8,128)}, s32[]{:T(128)}) %tuple.148), condition=%wide.region_35.36_spmd.clone, body=%wide.region_33.35_spmd.clone.sunk | while | flops 684258432 | bytes 97863152 | solution.py:52
  4128.4 49.1 iota_compare_fusion.13
  4177.5 381.4 %select_reduce_fusion.11 = bf16[8,561,128]{2,0,1:T(8,128)(2,1)S(1)} fusion(f32[8,561,561]{0,2,1:T(8,128)} %get-tuple-element.554, pred[561,561,128]{2,1,0:T(8,128)(4,1)} %iota_compare_fusion.13), kind=kLoop, calls=%fused_computation.18.clone.1 | loop fusion | flops 643974144 | bytes 51504288 | tf_op jit(solution)/shard_map/while/body/eval_jaxpr/while/body/eval_jaxpr/reduce_sum | solution.py:50
  4561.4 49.1 iota_compare_fusion.13
  4610.5 381.4 %select_reduce_fusion.11 = bf16[8,561,128]{2,0,1:T(8,128)(2,1)S(1)} fusion(f32[8,561,561]{0,2,1:T(8,128)} %get-tuple-element.554, pred[561,561,128]{2,1,0:T(8,128)(4,1)} %iota_compare_fusion.13), kind=kLoop, calls=%fused_computation.18.clone.1 | loop fusion | flops 643974144 | bytes 51504288 | tf_op jit(solution)/shard_map/while/body/eval_jaxpr/while/body/eval_jaxpr/reduce_sum | solution.py:50
  5043.5 381.4 %select_reduce_fusion.11 = bf16[8,561,128]{2,0,1:T(8,128)(2,1)S(1)} fusion(f32[8,561,561]{0,2,1:T(8,128)} %get-tuple-element.554, pred[561,561,128]{2,1,0:T(8,128)(4,1)} %iota_compare_fusion.13), kind=kLoop, calls=%fused_computation.18.clone.1 | loop fusion | flops 643974144 | bytes 51504288 | tf_op jit(solution)/shard_map/while/body/eval_jaxpr/while/body/eval_jaxpr/reduce_sum | solution.py:50
  5430.3 77.2 %copy.106 = f32[8,561,561]{0,2,1:T(8,128)} copy(f32[8,561,561]{2,1,0:T(8,128)} %get-tuple-element.384) | data formatting | bytes 20142144
  5509.8 1299.2 %while.83 = (s32[]{:T(128)}, bf16[3,8,561,128]{3,1,2,0:T(8,128)(2,1)}, s32[3,561,561]{2,1,0:T(8,128)}, f32[8,561,561]{0,2,1:T(8,128)}, s32[]{:T(128)}) while((s32[]{:T(128)}, bf16[3,8,561,128]{3,1,2,0:T(8,128)(2,1)}, s32[3,561,561]{2,1,0:T(8,128)}, f32[8,561,561]{0,2,1:T(8,128)}, s32[]{:T(128)}) %tuple.149), condition=%wide.region_32.33_spmd.clone, body=%wide.region_30.32_spmd.clone.sunk | while | flops 684258432 | bytes 97863152 | solution.py:52
  5511.5 49.1 iota_compare_fusion.12
  5560.6 381.4 %select_reduce_fusion.10 = bf16[8,561,128]{2,0,1:T(8,128)(2,1)S(1)} fusion(f32[8,561,561]{0,2,1:T(8,128)} %get-tuple-element.569, pred[561,561,128]{2,1,0:T(8,128)(4,1)} %iota_compare_fusion.12), kind=kLoop, calls=%fused_computation.14.clone.1 | loop fusion | flops 643974144 | bytes 51504288 | tf_op jit(solution)/shard_map/while/body/eval_jaxpr/while/body/eval_jaxpr/reduce_sum | solution.py:50
  5944.5 49.1 iota_compare_fusion.12
  5993.6 381.4 %select_reduce_fusion.10 = bf16[8,561,128]{2,0,1:T(8,128)(2,1)S(1)} fusion(f32[8,561,561]{0,2,1:T(8,128)} %get-tuple-element.569, pred[561,561,128]{2,1,0:T(8,128)(4,1)} %iota_compare_fusion.12), kind=kLoop, calls=%fused_computation.14.clone.1 | loop fusion | flops 643974144 | bytes 51504288 | tf_op jit(solution)/shard_map/while/body/eval_jaxpr/while/body/eval_jaxpr/reduce_sum | solution.py:50
  6426.6 381.4 %select_reduce_fusion.10 = bf16[8,561,128]{2,0,1:T(8,128)(2,1)S(1)} fusion(f32[8,561,561]{0,2,1:T(8,128)} %get-tuple-element.569, pred[561,561,128]{2,1,0:T(8,128)(4,1)} %iota_compare_fusion.12), kind=kLoop, calls=%fused_computation.14.clone.1 | loop fusion | flops 643974144 | bytes 51504288 | tf_op jit(solution)/shard_map/while/body/eval_jaxpr/while/body/eval_jaxpr/reduce_sum | solution.py:50
  6891.5 205.2 %all-reduce.8.cloned.1.call-done = (bf16[3,128,512]{1,2,0:T(8,128)(2,1)}, bf16[3,128,512]{1,2,0:T(8,128)(2,1)}, bf16[1024,3,512]{2,0,1:T(8,128)(2,1)}, bf16[512,...) async-done(((bf16[3,128,512]{1,2,0:T(8,128)(2,1)}, bf16[3,128,512]{1,2,0:T(8,128)(2,1)}, bf16[1024,3,512]{2,0,1:T(8,128)(2,1)}, ...) | async-done | bytes 13369360 | tf_op jit(solution)/shard_map/psum | solution.py:254
  (245 shorter events, 913.7 us)
Async XLA Ops:
  7.2 3751.5 %copy-start = (bf16[512,1024]{1,0:T(8,128)(2,1)S(1)}, bf16[512,1024]{1,0:T(8,128)(2,1)}, u32[]{:S(2)}) copy-start(bf16[512,1024]{1,0:T(8,128)(2,1)} %param.24) | copy-start | bytes 3145732
  7.2 5.6 copy-start.26
  7.2 27.7 all-gather.12.cloned.1.call-start
  7.9 3787.6 %reduce-scatter.5.cloned.1.call-start = ((), (), s32[]{:S(2)}) async-start(), calls=%async_computation.4 | async-start | bytes 3489792 | tf_op jit(solution)/shard_map/reduce_scatter | solution.py:134
  8.0 5.0 copy-start.27
  8.0 7.2 copy-start.30
  13.0 30.1 copy-start.21
  1863.7 12.3 copy-start.4
  1886.7 12.2 copy-start.23
  3719.3 12.2 copy-start.31
  3760.9 67.2 all-gather.6.cloned.1.call-start
  3805.4 65.8 reduce-scatter.7.cloned.1.call-start
  3828.1 17.5 copy-start.37
  3849.3 63.3 all-gather.8.cloned.1.call-start
  3889.9 58.8 reduce-scatter.9.cloned.1.call-start
  3912.7 10.6 copy-start.38
  3926.9 55.9 all-gather.10.cloned.1.call-start
  3960.1 2929.3 %reduce-scatter.11.cloned.1.call-start = ((), (), s32[]{:S(2)}) async-start(), calls=%async_computation.10 | async-start | bytes 1744896 | tf_op jit(solution)/shard_map/reduce_scatter | solution.py:234
  3987.8 7.7 copy-start.7
  3987.8 17.0 slice-start
  3987.8 17.0 slice-start.1
  3995.5 9.3 slice-start.2
  4126.9 1299.1 %copy-start.24 = (bf16[3,128,512]{1,2,0:T(8,128)(2,1)S(1)}, bf16[3,128,512]{1,2,0:T(8,128)(2,1)}, u32[]{:S(2)}) copy-start(bf16[3,128,512]{1,2,0:T(8,128)(2,1)} %copy.97) | copy-start | bytes 1179652
  5509.8 1299.2 %copy-start.22 = (bf16[3,128,512]{1,2,0:T(8,128)(2,1)S(1)}, bf16[3,128,512]{1,2,0:T(8,128)(2,1)}, u32[]{:S(2)}) copy-start(bf16[3,128,512]{1,2,0:T(8,128)(2,1)} %copy-done.21) | copy-start | bytes 1179652
  6823.1 273.6 %all-reduce.8.cloned.1.call-start = ((), (), s32[]{:S(2)}) async-start(), calls=%async_computation.12 | async-start | bytes 26738688 | tf_op jit(solution)/shard_map/psum | solution.py:254
  6823.2 7.7 copy-start.40
  6823.2 7.7 copy-start.44
  6830.9 5.3 copy-start.15
  6851.1 38.3 copy-start.9
  7096.7 5.6 copy-start.25
  7096.7 7.2 copy-start.13
  7108.4 5.5 copy-start.28
  (25 other events, 64.3 us)
Sparse Core Ops, SparseCore 0:
  9.6 25.2 all-gather.11
  3761.1 34.4 reduce-scatter.4
  3805.5 22.5 all-gather.5
  3849.4 21.6 reduce-scatter.6
  3890.1 22.5 all-gather.7
  3927.0 21.6 reduce-scatter.8
  3960.2 22.5 all-gather.9
  6823.2 21.6 reduce-scatter.10
  6851.2 245.4 all-reduce.7
where the time goes:
time: 7140 us; the launch traced here: 7120 us
  other arithmetic  5660 us (79%)
  local copies, waits for them, and re-layouts  910 us (13%)
  waiting for transfers between devices  367 us (5%)
  matrix products  113 us (2%)
    reduce_sum x6, other arithmetic, pick_one_kind(): return jnp.sum(jnp.where(chosen, kind_table[:, :, None, :], 0.0), axis=-1)  2650 us
    reduce_sum x6, other arithmetic, spread_one_kind(): return jnp.sum(jnp.where(chosen, grad_scores[:, :, :, None], 0.0), axis=2)  2290 us
    dynamic_update_slice x12, local copies, waits for them, and re-layouts, pick_buckets(): return jnp.sum(lax.map(pick_one_kind, (table, buckets)), axis=0)  608 us
    eq x6, other arithmetic, spread_one_kind(): chosen = kind_buckets[None, :, :, None] == labels  295 us
    eq x6, other arithmetic, pick_one_kind(): chosen = kind_buckets[None, :, :, None] == labels  295 us
    psum x1, waiting for transfers between devices, on_device(): lax.psum(rel_keys_grad.astype(jnp.bfloat16), 'dp').astype(jnp.float32)  205 us
    unnamed x105, local copies, waits for them, and re-layouts  180 us
  transfers between devices with their start and end apart: 9, of which 8 were waited for; matrix products, arithmetic and copies ran while one was open for 1% of the time, Pallas kernels for 0%

commit v1 on v0

v1 whole, which is shorter than its diff:
```python
import math, functools
import jax, jax.numpy as jnp
from jax import lax
from jax.sharding import PartitionSpec as P
from jax.experimental import pallas as pl
from jax.experimental.pallas import tpu as pltpu

HEAD_DIM = 64
BUCKETS = 128
TEXT = 512
NEG = -1e30
SCALE = 1.0 / math.sqrt(3 * HEAD_DIM)
F32 = jnp.float32
BF16 = jnp.bfloat16


def nt(a, b):
    return lax.dot_general(a, b, (((1,), (1,)), ((), ())), preferred_element_type=F32)


def nn(a, b):
    return lax.dot_general(a, b, (((1,), (0,)), ((), ())), preferred_element_type=F32)


def iota(shape, d):
    return lax.broadcasted_iota(jnp.int32, shape, d)


def lane_pick(table, index):
    return jnp.take_along_axis(table, index, axis=1, mode="promise_in_bounds")


def fwd_kernel(slots, sp, len_ref, q_ref, k_ref, v_ref, relk_ref, relq_ref, bc_ref, br_ref,
               ctx_ref, p_ref, qs, ks, vs, idx, nq, nk, fk):
    pair = pl.program_id(1)
    nb = sp // 128

    @pl.when(pair == 0)
    def _():
        qs[...] = jnp.zeros_like(qs)
        ks[...] = jnp.zeros_like(ks)
        vs[...] = jnp.zeros_like(vs)

        def rows(b, c):
            r0 = pl.multiple_of(b * 128, 128)
            row = iota((128, sp), 0) + r0
            col = iota((128, sp), 1)
            idx[0, pl.ds(r0, 128), :] = jnp.clip(col - row, -64, 63) + 64
            for t in range(2):
                x_i = bc_ref[pl.ds(r0, 128), t:t + 1]
                x_j = br_ref[t:t + 1, :]
                idx[t + 1, pl.ds(r0, 128), :] = jnp.clip((x_j - x_i) >> 4, -64, 63) + 64
            return c
        lax.fori_loop(0, nb, rows, 0)

    qs[0:slots, :] = q_ref[...]
    ks[0:slots, :] = k_ref[...]
    vs[0:slots, :] = v_ref[...]
    place = iota((1, sp), 1)
    length = len_ref[pl.program_id(0)]
    valid = (place < length) | ((place >= TEXT) & (place < slots))
    half = iota((1, 128), 1) < 64

    for h in range(2):
        mine = half if h == 0 else jnp.logical_not(half)
        qm = jnp.where(mine, qs[...], 0)
        km = jnp.where(mine, ks[...], 0)
        nq[...] = nt(qm, relk_ref[...])
        nk[...] = nt(km, relq_ref[...])

        def key_side(b, c):
            r0 = pl.multiple_of(b * 128, 128)
            for ib in range(nb):
                g = None
                for t in range(3):
                    e = lane_pick(nk[pl.ds(r0, 128), t * 128:(t + 1) * 128],
                                  idx[t, pl.ds(r0, 128), ib * 128:(ib + 1) * 128])
                    g = e if g is None else g + e
                fk[ib * 128:(ib + 1) * 128, pl.ds(r0, 128)] = g.T
            return c
        lax.fori_loop(0, nb, key_side, 0)

        def query_side(b, c):
            r0 = pl.multiple_of(b * 128, 128)
            q_b = jnp.where(mine, qs[pl.ds(r0, 128), :], 0)
            s = nt(q_b, ks[...]) + fk[pl.ds(r0, 128), :]
            parts = []
            for jb in range(nb):
                g = s[:, jb * 128:(jb + 1) * 128]
                for t in range(3):
                    g = g + lane_pick(nq[pl.ds(r0, 128), t * 128:(t + 1) * 128],
                                      idx[t, pl.ds(r0, 128), jb * 128:(jb + 1) * 128])
                parts.append(g)
            s = jnp.concatenate(parts, axis=1)
            s = jnp.where(valid, s * SCALE, NEG)
            m = jnp.max(s, axis=1, keepdims=True)
            e = jnp.exp(s - m)
            tot = jnp.sum(e, axis=1, keepdims=True)
            p = (e * (1.0 / tot)).astype(BF16)
            p_ref[h, pl.ds(r0, 128), :] = p
            c_b = nn(p, vs[...])
            fk[pl.ds(r0, 128), 0:128] = c_b
            return c
        lax.fori_loop(0, nb, query_side, 0)
        if h == 0:
            ctx_ref[...] = fk[0:slots, 0:128].astype(BF16)
        else:
            ctx_ref[...] = jnp.where(mine, fk[0:slots, 0:128].astype(BF16), ctx_ref[...])


def attend_forward(lengths, qkv, relk, relq, boxes_col, boxes_row, heads):
    docs, slots, width = qkv.shape
    width = width // 3
    sp = boxes_row.shape[2]
    pairs = heads // 2

    def part(t):
        return pl.BlockSpec((None, slots, 128), lambda d, p, ln: (d, 0, t * pairs + p))
    grid_spec = pltpu.PrefetchScalarGridSpec(
        num_scalar_prefetch=1, grid=(docs, pairs),
        in_specs=[part(0), part(1), part(2),
                  pl.BlockSpec((3 * BUCKETS, 128), lambda d, p, ln: (0, p)),
                  pl.BlockSpec((3 * BUCKETS, 128), lambda d, p, ln: (0, p)),
                  pl.BlockSpec((None, sp, 2), lambda d, p, ln: (d, 0, 0)),
                  pl.BlockSpec((None, 2, sp), lambda d, p, ln: (d, 0, 0))],
        out_specs=[pl.BlockSpec((None, slots, 128), lambda d, p, ln: (d, 0, p)),
                   pl.BlockSpec((None, 2, sp, sp), lambda d, p, ln: (d, p, 0, 0))],
        scratch_shapes=[pltpu.VMEM((sp, 128), BF16)] * 3
        + [pltpu.VMEM((3, sp, sp), jnp.int32), pltpu.VMEM((sp, 384), F32), pltpu.VMEM((sp, 384), F32),
           pltpu.VMEM((sp, sp), F32)])
    return pl.pallas_call(
        functools.partial(fwd_kernel, slots, sp),
        out_shape=[jax.ShapeDtypeStruct((docs, slots, width), BF16),
                   jax.ShapeDtypeStruct((docs, heads, sp, sp), BF16)],
        grid_spec=grid_spec, name="attend_forward",
        compiler_params=pltpu.CompilerParams(vmem_limit_bytes=56 << 20),
    )(lengths, qkv, qkv, qkv, relk, relq, boxes_col, boxes_row)


def bwd_kernel(slots, sp, width, q_ref, k_ref, v_ref, dc_ref, p_ref, relk_ref, relq_ref, bc_ref, br_ref,
               dqkv_ref, gk_ref, gq_ref,
               qs, ks, vs, dcs, base, ex, ey, mx, my, ds, dst, gt, acc):
    pair = pl.program_id(1)
    nb = sp // 128

    @pl.when(pair == 0)
    def _():
        for r in (qs, ks, vs, dcs, ds, dst):
            r[...] = jnp.zeros_like(r)
        lane = iota((sp, 128), 1)
        ax = bc_ref[:, 0:1] >> 4
        ay = bc_ref[:, 1:2] >> 4
        left = lane < 64
        c = lane & 63
        a = jnp.where(left, ax, ay)
        one = jnp.where(c == a, 1.0, 0.0)
        nxt = jnp.where(c == a + 1, 1.0, 0.0)
        base[...] = one.astype(BF16)
        e = nxt - one
        ex[...] = jnp.where(left, e, 0.0).astype(BF16)
        ey[...] = jnp.where(left, 0.0, e).astype(BF16)

        def rows(b, c):
            r0 = pl.multiple_of(b * 128, 128)
            for t, m in ((0, mx), (1, my)):
                r_i = bc_ref[pl.ds(r0, 128), t:t + 1] & 15
                r_j = br_ref[t:t + 1, :] & 15
                m[pl.ds(r0, 128), :] = jnp.where(r_j >= r_i, 1.0, 0.0).astype(BF16)
            return c
        lax.fori_loop(0, nb, rows, 0)

    qs[0:slots, :] = q_ref[...]
    ks[0:slots, :] = k_ref[...]
    vs[0:slots, :] = v_ref[...]
    dcs[0:slots, :] = dc_ref[...]
    half = iota((1, 128), 1) < 64
    lane1 = iota((128, 128), 1)
    row1 = iota((128, 128), 0)

    for h in range(2):
        mine = half if h == 0 else jnp.logical_not(half)

        def grad_scores(b, c):
            r0 = pl.multiple_of(b * 128, 128)
            d_b = jnp.where(mine, dcs[pl.ds(r0, 128), :], 0)
            dp = nt(d_b, vs[...])
            p = p_ref[h, pl.ds(r0, 128), :].astype(F32)
            inner = jnp.sum(p * dp, axis=1, keepdims=True)
            d = p * (dp - inner)
            ds[pl.ds(r0, 128), 128:128 + sp] = d.astype(BF16)
            for jb in range(nb):
                dst[jb * 128:(jb + 1) * 128, pl.ds(pl.multiple_of(r0 + 128, 128), 128)] = \
                    d[:, jb * 128:(jb + 1) * 128].T.astype(BF16)
            return c
        lax.fori_loop(0, nb, grad_scores, 0)

        dct = jnp.where(mine, dcs[...], 0).astype(F32).T.astype(BF16)
        dvt = nn(dct, p_ref[h, :, :])
        if h == 0:
            gt[...] = dvt
        else:
            gt[...] += dvt

        for side in range(2):
            mat = ds if side == 0 else dst
            other = ks if side == 0 else qs
            own = qs if side == 0 else ks
            rel_ref = relk_ref if side == 0 else relq_ref
            g_ref = gk_ref if side == 0 else gq_ref
            blk = iota((sp, 128), 0) >> 7
            lane_sp = iota((sp, 128), 1) & 63
            w = jnp.where(mine, other[...].astype(F32), jnp.where(blk == lane_sp, 1.0, 0.0)).astype(BF16)
            w2 = jnp.concatenate([w, base[...]], axis=1)
            relm = jnp.where(mine, rel_ref[...], 0)
            acc[...] = jnp.zeros_like(acc)

            def rows(b, c):
                r0 = pl.multiple_of(b * 128, 128)
                d_b = mat[pl.ds(r0, 128), 128:128 + sp]
                out = nn(d_b, w2)
                hist = out[:, 128:] + nn(d_b * mx[pl.ds(r0, 128), :], ex[...]) \
                    + nn(d_b * my[pl.ds(r0, 128), :], ey[...])
                before = mat[pl.ds(r0, 128), pl.ds(r0, 128)].astype(F32)
                here = mat[pl.ds(r0, 128), pl.ds(pl.multiple_of(r0 + 128, 128), 128)].astype(F32)
                after = mat[pl.ds(r0, 128), pl.ds(pl.multiple_of(r0 + 256, 128), 128)].astype(F32)
                sums = jnp.where(mine, 0.0, out[:, :128])
                blkno = lane1 & 63
                low = jnp.where(blkno <= b - 2, sums, 0.0) + jnp.where(lane1 <= row1 + 64, before, 0.0) \
                    + jnp.where(lane1 <= row1 - 64, here, 0.0)
                high = jnp.where(blkno >= b + 2, sums, 0.0) + jnp.where(lane1 >= row1 + 63, here, 0.0) \
                    + jnp.where(lane1 >= row1 - 65, after, 0.0)
                low = jnp.sum(low, axis=1, keepdims=True)
                high = jnp.sum(high, axis=1, keepdims=True)
                at = lane1 + row1 + 64
                place = at & 127
                mid = jnp.where(at < 128, lane_pick(before, place),
                                jnp.where(at < 256, lane_pick(here, place), lane_pick(after, place)))
                dn0 = jnp.where(lane1 == 0, low, jnp.where(lane1 == 127, high, mid))
                ax = bc_ref[pl.ds(r0, 128), 0:1] >> 4
                ay = bc_ref[pl.ds(r0, 128), 1:2] >> 4
                c1 = lane1 + ax - 63
                c2 = lane1 + ay - 63
                dn1 = jnp.where((c1 >= 0) & (c1 < 64), lane_pick(hist, c1 & 127), 0.0)
                dn2 = jnp.where((c2 >= 0) & (c2 < 64), lane_pick(hist, (c2 + 64) & 127), 0.0)
                dn = jnp.concatenate([dn0, dn1, dn2], axis=1).astype(BF16)
                g = (out[:, :128] + nn(dn, relm)) * SCALE
                o_b = jnp.where(mine, own[pl.ds(r0, 128), :], 0)
                acc[...] += nn(o_b.astype(F32).T.astype(BF16), dn)
                return c, g
            for b in range(nb):
                _, g = rows(b, 0)
                n = min(128, slots - b * 128)
                at = pl.ds(pl.multiple_of(side * width + pair * 128, 128), 128)
                if h == 0:
                    dqkv_ref[b * 128:b * 128 + n, at] = g[0:n].astype(BF16)
                else:
                    dqkv_ref[b * 128:b * 128 + n, at] = jnp.where(
                        mine, g[0:n].astype(BF16), dqkv_ref[b * 128:b * 128 + n, at])
            if h == 0:
                g_ref[...] = acc[...] * SCALE
            else:
                g_ref[...] += acc[...] * SCALE
    dv = gt[...].T
    dqkv_ref[:, pl.ds(pl.multiple_of(2 * width + pair * 128, 128), 128)] = dv[0:slots, :].astype(BF16)


def attend_backward(qkv, dctx, probs, relk, relq, boxes_col, boxes_row, heads):
    docs, slots, width = qkv.shape
    width = width // 3
    sp = boxes_row.shape[2]
    pairs = heads // 2

    def part(t):
        return pl.BlockSpec((None, slots, 128), lambda d, p: (d, 0, t * pairs + p))
    rel = pl.BlockSpec((3 * BUCKETS, 128), lambda d, p: (0, p))
    grel = pl.BlockSpec((None, 128, 3 * BUCKETS), lambda d, p: (d, p, 0))
    return pl.pallas_call(
        functools.partial(bwd_kernel, slots, sp, width),
        grid=(docs, pairs),
        in_specs=[part(0), part(1), part(2),
                  pl.BlockSpec((None, slots, 128), lambda d, p: (d, 0, p)),
                  pl.BlockSpec((None, 2, sp, sp), lambda d, p: (d, p, 0, 0)),
                  rel, rel,
                  pl.BlockSpec((None, sp, 2), lambda d, p: (d, 0, 0)),
                  pl.BlockSpec((None, 2, sp), lambda d, p: (d, 0, 0))],
        out_specs=[pl.BlockSpec((None, slots, 3 * width), lambda d, p: (d, 0, 0)), grel, grel],
        out_shape=[jax.ShapeDtypeStruct((docs, slots, 3 * width), BF16),
                   jax.ShapeDtypeStruct((docs, width, 3 * BUCKETS), F32),
                   jax.ShapeDtypeStruct((docs, width, 3 * BUCKETS), F32)],
        scratch_shapes=[pltpu.VMEM((sp, 128), BF16)] * 7
        + [pltpu.VMEM((sp, sp), BF16)] * 2 + [pltpu.VMEM((sp, sp + 256), BF16)] * 2
        + [pltpu.VMEM((128, sp), F32), pltpu.VMEM((128, 384), F32)],
        name="attend_backward",
        compiler_params=pltpu.CompilerParams(vmem_limit_bytes=56 << 20),
    )(qkv, qkv, qkv, dctx, probs, relk, relq, boxes_col, boxes_row)


def norm_forward(values_in, gain, shift, model_width):
    row_total, row_square = lax.psum(
        (jnp.sum(values_in, axis=1), jnp.sum(values_in * values_in, axis=1)), "tensor"
    )
    mean_row = row_total / model_width
    scale_row = lax.rsqrt(row_square / model_width - mean_row * mean_row + 1e-05)
    normed = (values_in - mean_row[:, None]) * scale_row[:, None]
    return (normed * gain + shift, normed, scale_row)


def norm_backward(upstream, normed, scale_row, gain, model_width):
    scaled_up = upstream * gain
    first_sum, second_sum = lax.psum(
        (jnp.sum(scaled_up, axis=1), jnp.sum(scaled_up * normed, axis=1)), "tensor"
    )
    centered = (
        scaled_up - first_sum[:, None] / model_width - normed * second_sum[:, None] / model_width
    )
    return scale_row[:, None] * centered


def on_device(
    hidden_in,
    lengths,
    boxes,
    w_qkv,
    w_out,
    w_up,
    w_down,
    rel_keys,
    rel_queries,
    norm_gains,
    norm_shifts,
    out_grad,
):
    doc_count, slot_count, local_width = hidden_in.shape
    row_count = doc_count * slot_count
    model_width = w_qkv.shape[0]
    heads_here = local_width // HEAD_DIM
    rel_k = rel_keys.reshape(3 * BUCKETS, local_width)
    rel_q = rel_queries.reshape(3 * BUCKETS, local_width)
    padded = -(-slot_count // 128) * 128
    boxes_col = jnp.pad(boxes, ((0, 0), (0, padded - slot_count), (0, 0)))
    boxes_row = jnp.swapaxes(boxes_col, 1, 2)
    local_rows = hidden_in.reshape(row_count, local_width)
    full_rows = lax.all_gather(local_rows, "tensor", axis=1, tiled=True)
    weight_qkv = w_qkv.reshape(model_width, 3 * local_width)
    projected = jnp.dot(full_rows, weight_qkv, preferred_element_type=jnp.float32).astype(
        jnp.bfloat16
    )
    projected = projected.reshape(doc_count, slot_count, 3 * local_width)
    context, probs = attend_forward(lengths, projected, rel_k, rel_q, boxes_col, boxes_row, heads_here)
    context_rows = context.reshape(row_count, local_width)
    attn_terms = jnp.dot(context_rows, w_out, preferred_element_type=jnp.float32)
    attn_out = lax.psum_scatter(attn_terms, "tensor", scatter_dimension=1, tiled=True)
    first_sum_in = local_rows.astype(jnp.float32) + attn_out
    normed_first, unit_first, scale_first = norm_forward(
        first_sum_in, norm_gains[0], norm_shifts[0], model_width
    )
    normed_full = lax.all_gather(normed_first.astype(jnp.bfloat16), "tensor", axis=1, tiled=True)
    upper = jnp.dot(normed_full, w_up, preferred_element_type=jnp.float32)
    active = jax.nn.gelu(upper, approximate=False).astype(jnp.bfloat16)
    ffn_out = lax.psum_scatter(
        jnp.dot(active, w_down, preferred_element_type=jnp.float32).astype(jnp.bfloat16),
        "tensor",
        scatter_dimension=1,
        tiled=True,
    ).astype(jnp.float32)
    result, unit_second, scale_second = norm_forward(
        normed_first + ffn_out, norm_gains[1], norm_shifts[1], model_width
    )
    hidden_out = result.astype(jnp.bfloat16).reshape(doc_count, slot_count, local_width)
    upstream = out_grad.reshape(row_count, local_width).astype(jnp.float32)
    gain_second = jnp.sum(upstream * unit_second, axis=0)
    shift_second = jnp.sum(upstream, axis=0)
    grad_second = norm_backward(upstream, unit_second, scale_second, norm_gains[1], model_width)
    ffn_grad_full = lax.all_gather(grad_second.astype(jnp.bfloat16), "tensor", axis=1, tiled=True)
    down_grad = jnp.einsum("rf,rd->fd", active, ffn_grad_full, preferred_element_type=jnp.float32)
    grad_active = jnp.einsum("rd,fd->rf", ffn_grad_full, w_down, preferred_element_type=jnp.float32)
    _, gelu_pull = jax.vjp(lambda entry: jax.nn.gelu(entry, approximate=False), upper)
    grad_upper = gelu_pull(grad_active)[0].astype(jnp.bfloat16)
    up_grad = jnp.einsum("rd,rf->df", normed_full, grad_upper, preferred_element_type=jnp.float32)
    hidden_terms = jnp.einsum("rf,df->rd", grad_upper, w_up, preferred_element_type=jnp.float32)
    grad_hidden = grad_second + lax.psum_scatter(
        hidden_terms.astype(jnp.bfloat16), "tensor", scatter_dimension=1, tiled=True
    ).astype(jnp.float32)
    gain_first = jnp.sum(grad_hidden * unit_first, axis=0)
    shift_first = jnp.sum(grad_hidden, axis=0)
    grad_first = norm_backward(grad_hidden, unit_first, scale_first, norm_gains[0], model_width)
    attn_grad_full = lax.all_gather(grad_first.astype(jnp.bfloat16), "tensor", axis=1, tiled=True)
    out_weight_grad = jnp.einsum(
        "rc,rd->cd", context_rows, attn_grad_full, preferred_element_type=jnp.float32
    )
    grad_context = jnp.einsum(
        "rd,cd->rc", attn_grad_full, w_out, preferred_element_type=jnp.float32
    ).astype(jnp.bfloat16)
    grad_context = grad_context.reshape(doc_count, slot_count, local_width)
    grad_projected, rel_k_sum, rel_q_sum = attend_backward(
        projected, grad_context, probs, rel_k, rel_q, boxes_col, boxes_row, heads_here
    )
    rel_keys_grad = jnp.sum(rel_k_sum, axis=0).T.reshape(3, BUCKETS, local_width)
    rel_queries_grad = jnp.sum(rel_q_sum, axis=0).T.reshape(3, BUCKETS, local_width)
    grad_rows = grad_projected.reshape(row_count, 3 * local_width)
    qkv_grad = jnp.einsum(
        "rd,rc->dc", full_rows, grad_rows, preferred_element_type=jnp.float32
    ).reshape(model_width, 3, local_width)
    input_terms = jnp.einsum("rc,dc->rd", grad_rows, weight_qkv, preferred_element_type=jnp.float32)
    input_grad = grad_first + lax.psum_scatter(
        input_terms.astype(jnp.bfloat16), "tensor", scatter_dimension=1, tiled=True
    ).astype(jnp.float32)
    input_grad = input_grad.astype(jnp.bfloat16).reshape(doc_count, slot_count, local_width)
    (
        qkv_grad,
        out_weight_grad,
        up_grad,
        down_grad,
        rel_keys_grad,
        rel_queries_grad,
        gain_first,
        shift_first,
        gain_second,
        shift_second,
    ) = (
        lax.psum(qkv_grad.astype(jnp.bfloat16), "dp").astype(jnp.float32),
        lax.psum(out_weight_grad.astype(jnp.bfloat16), "dp").astype(jnp.float32),
        lax.psum(up_grad.astype(jnp.bfloat16), "dp").astype(jnp.float32),
        lax.psum(down_grad.astype(jnp.bfloat16), "dp").astype(jnp.float32),
        lax.psum(rel_keys_grad.astype(jnp.bfloat16), "dp").astype(jnp.float32),
        lax.psum(rel_queries_grad.astype(jnp.bfloat16), "dp").astype(jnp.float32),
        lax.psum(gain_first.astype(jnp.bfloat16), "dp").astype(jnp.float32),
        lax.psum(shift_first.astype(jnp.bfloat16), "dp").astype(jnp.float32),
        lax.psum(gain_second.astype(jnp.bfloat16), "dp").astype(jnp.float32),
        lax.psum(shift_second.astype(jnp.bfloat16), "dp").astype(jnp.float32),
    )
    gains_grad = jnp.stack([gain_first, gain_second])
    shifts_grad = jnp.stack([shift_first, shift_second])
    return (
        hidden_out,
        input_grad,
        qkv_grad,
        out_weight_grad,
        up_grad,
        down_grad,
        rel_keys_grad,
        rel_queries_grad,
        gains_grad,
        shifts_grad,
    )


def solution(mesh):
    in_specs = (
        P("dp", None, "tensor"),
        P("dp"),
        P("dp", None, None),
        P(None, None, "tensor"),
        P("tensor", None),
        P(None, "tensor"),
        P("tensor", None),
        P(None, None, "tensor"),
        P(None, None, "tensor"),
        P(None, "tensor"),
        P(None, "tensor"),
        P("dp", None, "tensor"),
    )
    out_specs = (
        P("dp", None, "tensor"),
        P("dp", None, "tensor"),
        P(None, None, "tensor"),
        P("tensor", None),
        P(None, "tensor"),
        P("tensor", None),
        P(None, None, "tensor"),
        P(None, None, "tensor"),
        P(None, "tensor"),
        P(None, "tensor"),
    )
    return jax.shard_map(
        on_device, mesh=mesh, in_specs=in_specs, out_specs=out_specs, check_vma=False
    )
```

time: 7140 us -> 726 us (0.10)
  other arithmetic: 5660 us -> 35.5 us
  local copies, waits for them, and re-layouts: 910 us -> 17.4 us
  Pallas kernels: 0 us -> 155 us
    reduce_sum x15 -> x0, other arithmetic: 4980 us -> none  [the longest x6 2650 us: pick_one_kind(): return jnp.sum(jnp.where(chosen, kind_table[:, :, None, :], 0.0), axis=-1)]
    dynamic_update_slice x18 -> x0, local copies, waits for them, and re-layouts: 614 us -> none  [the longest x12 608 us: pick_buckets(): return jnp.sum(lax.map(pick_one_kind, (table, buckets)), axis=0)]
    eq x12 -> x0, other arithmetic: 589 us -> none  [the longest x6 295 us: spread_one_kind(): chosen = kind_buckets[None, :, :, None] == labels]
    unnamed x105 -> x52, local copies, waits for them, and re-layouts: 180 us -> 9.38 us
    pallas_call x0 -> x2, Pallas kernels: none -> 155 us  [the longest x1 82.4 us: attend_forward(): pl.pallas_call(functools.partial(fwd_kernel, slots, sp), out_shape=[jax.S...]
  transfers between devices with their start and end apart: 9 -> 9, of which waited for: 8 -> 8; matrix products, arithmetic and copies ran while one was open for 1% -> 5% of each run, Pallas kernels for 0% -> 0%
where the time goes in v1:
time: 726 us; the launch traced here: 719 us
  waiting for transfers between devices  371 us (51%)
  Pallas kernels  155 us (21%)
  matrix products  67.9 us (9%)
  blocking collectives  55.8 us (8%)
  other arithmetic  35.5 us (5%)
  local copies, waits for them, and re-layouts  17.4 us (2%)
  between operations  14.9 us (2%)
    psum x1, waiting for transfers between devices, on_device(): lax.psum(qkv_grad.astype(jnp.bfloat16), 'dp').astype(jnp.float32)  206 us
    pallas_call x1, Pallas kernels, attend_forward(): pl.pallas_call(functools.partial(fwd_kernel, slots, sp), out_shape=[jax.S...  82.4 us
    pallas_call x1, Pallas kernels, attend_backward(): pl.pallas_call(functools.partial(bwd_kernel, slots, sp, width), grid=(doc...  72.7 us
    psum x1, blocking collectives, on_device(): lax.psum(gain_second.astype(jnp.bfloat16), 'dp').astype(jnp.float32)  35.8 us
    reduce_scatter x1, waiting for transfers between devices, on_device(): lax.psum_scatter(attn_terms, 'tensor', scatter_dimension=1, tiled=True)  33.9 us
    all_gather x1, waiting for transfers between devices, on_device(): lax.all_gather(grad_first.astype(jnp.bfloat16), 'tensor', axis=1, tiled=T...  22.5 us
    all_gather x1, waiting for transfers between devices, on_device(): lax.all_gather(normed_first.astype(jnp.bfloat16), 'tensor', axis=1, tiled...  22.4 us
    all_gather x1, waiting for transfers between devices, on_device(): lax.all_gather(grad_second.astype(jnp.bfloat16), 'tensor', axis=1, tiled=...  22.2 us
  transfers between devices with their start and end apart: 9, of which 8 were waited for; matrix products, arithmetic and copies ran while one was open for 5% of the time, Pallas kernels for 0%

profile of v1, /device:TPU:0, one launch (start us, length us, event | category | flops | bytes accessed | tf_op | source)
XLA Modules:
  0.0 719.4 jit_solution(11509705416890955327)
XLA Ops:
  8.6 4.7 copy.27
  14.8 20.1 %all-gather.12.cloned.1.call-done = bf16[1,561,1024]{2,1,0:T(8,128)(2,1)} async-done(((bf16[1,561,512]{2,1,0:T(8,128)(2,1)}), bf16[1,561,1024]{2,1,0:T(8,128)(2,1)}) %all-gather.12.cloned.1.call-update) | async-done | bytes 1148944 | tf_op jit(solution)/shard_map/all_gather | solution.py:343
  34.9 5.5 fusion.6.q_ref.k_ref.v_ref
  40.3 82.4 %attend_forward.1 = (bf16[1,561,512]{2,1,0:T(8,128)(2,1)}, bf16[1,8,640,640]{3,2,1,0:T(8,128)(2,1)}) custom-call(s32[1]{0:T(128)S(6)} %copy.40.len_ref, bf16[1,561,1536]{2,1,0:T(8,128)(2,1)} %fusion.6.q_ref.k_ref.v_ref, bf16[1,561,1536]{2,1,0:T(8,128)(2,1)} %fusion.6.q_ref.k_ref.v_ref, bf16[1,561,1536]{2,1,0:T(8,128)(2,1)} %fusion.6.q_ref.k_ref.v_ref, ...), custom_call_target="tpu_custom_call" | custom-call | tf_op jit(solution)/shard_map/attend_forward/pallas_call | solution.py:131
  122.7 3.2 fusion.27
  126.7 33.9 %reduce-scatter.5.cloned.1.call-done = f32[561,512]{1,0:T(8,128)} async-done(((f32[561,1024]{1,0:T(8,128)}), f32[561,512]{1,0:T(8,128)}) %reduce-scatter.5.cloned.1.call-update) | async-done | bytes 1148944 | tf_op jit(solution)/shard_map/reduce_scatter | solution.py:352
  162.1 5.0 all-reduce.4
  168.6 22.4 %all-gather.6.cloned.1.call-done = bf16[561,1024]{1,0:T(8,128)(2,1)} async-done(((bf16[561,512]{1,0:T(8,128)(2,1)}), bf16[561,1024]{1,0:T(8,128)(2,1)}) %all-gather.6.cloned.1.call-update) | async-done | bytes 1148944 | tf_op jit(solution)/shard_map/all_gather | solution.py:357
  191.0 16.2 %multiply_convert_fusion = (bf16[561,2048]{1,0:T(8,128)(2,1)S(1)}, f32[561,2048]{1,0:T(8,128)}, f32[561,2048]{1,0:T(8,128)}) fusion(bf16[561,1024]{1,0:T(8,128)(2,1)} %all-gather.6.cloned.1.call-done, bf16[1024,2048]{1,0:T(8,128)(2,1)} %param.17), kind=kOutput, calls=%fused_computation.3 | convolution fusion | flops 2427684864 | bytes 16832512 | tf_op jit(solution)/shard_map/dot_general | solution.py:358
  208.6 3.6 convolution_convert_fusion.5
  212.3 21.8 %reduce-scatter.7.cloned.1.call-done = bf16[561,512]{1,0:T(8,128)(2,1)} async-done(((bf16[561,1024]{1,0:T(8,128)(2,1)}), bf16[561,512]{1,0:T(8,128)(2,1)}) %reduce-scatter.7.cloned.1.call-update) | async-done | bytes 574480 | tf_op jit(solution)/shard_map/reduce_scatter | solution.py:360
  235.6 5.0 all-reduce.3
  242.4 5.0 all-reduce.2
  247.4 3.0 fusion.33
  250.9 22.2 %all-gather.8.cloned.1.call-done = bf16[561,1024]{1,0:T(8,128)(2,1)} async-done(((bf16[561,512]{1,0:T(8,128)(2,1)}), bf16[561,1024]{1,0:T(8,128)(2,1)}) %all-gather.8.cloned.1.call-update) | async-done | bytes 1148944 | tf_op jit(solution)/shard_map/all_gather | solution.py:374
  273.1 9.2 %add_convert_fusion = bf16[561,2048]{1,0:T(8,128)(2,1)S(1)} fusion(f32[561,2048]{1,0:T(8,128)} %get-tuple-element.55, f32[561,2048]{1,0:T(8,128)} %get-tuple-element.66, bf16[561,1024]{1,0:T(8,128)(2,1)} %all-gather.8.cloned.1.call-done, bf16[2048,1024]{1,0:T(8,128)(2,1)} %param.18), kind=kOutput, calls=%fused_computation.2 | convolution fusion | flops 2369089536 | bytes 16832512 | tf_op jit(solution)/shard_map/rd,fd->rf/dot_general | solution.py:376
  283.7 3.6 convolution_convert_fusion.4
  287.4 21.8 %reduce-scatter.9.cloned.1.call-done = bf16[561,512]{1,0:T(8,128)(2,1)} async-done(((bf16[561,1024]{1,0:T(8,128)(2,1)}), bf16[561,512]{1,0:T(8,128)(2,1)}) %reduce-scatter.9.cloned.1.call-update) | async-done | bytes 574480 | tf_op jit(solution)/shard_map/reduce_scatter | solution.py:381
  310.9 5.0 all-reduce.1
  318.8 22.5 %all-gather.10.cloned.1.call-done = bf16[561,1024]{1,0:T(8,128)(2,1)} async-done(((bf16[561,512]{1,0:T(8,128)(2,1)}), bf16[561,1024]{1,0:T(8,128)(2,1)}) %all-gather.10.cloned.1.call-update) | async-done | bytes 1148944 | tf_op jit(solution)/shard_map/all_gather | solution.py:387
  344.2 72.7 %attend_backward.1 = (bf16[1,561,1536]{2,1,0:T(8,128)(2,1)}, f32[1,512,384]{2,1,0:T(8,128)}, f32[1,512,384]{2,1,0:T(8,128)}) custom-call(bf16[1,561,1536]{2,1,0:T(8,128)(2,1)} %fusion.6.q_ref.k_ref.v_ref, bf16[1,561,1536]{2,1,0:T(8,128)(2,1)} %fusion.6.q_ref.k_ref.v_ref, bf16[1,561,1536]{2,1,0:T(8,128)(2,1)} %fusion.6.q_ref.k_ref.v_ref, ...), custom_call_target="tpu_custom_call" | custom-call | tf_op jit(solution)/shard_map/attend_backward/pallas_call | solution.py:277
  417.0 4.5 fusion.10
  421.6 6.9 convolution_convert_fusion.2
  428.5 5.1 convolution_convert_fusion.1
  433.6 4.0 convolution_convert_fusion
  437.6 4.8 copy.30
  445.6 3.2 convolution_convert_fusion.6
  450.1 35.8 %all-reduce.5 = (bf16[1,512]{1,0:T(2,128)(2,1)S(1)}, bf16[1,512]{1,0:T(2,128)(2,1)S(1)}, bf16[1,512]{1,0:T(2,128)(2,1)S(1)}, bf16[1,512]{1,0:T(2,128)(2,1)S(1)}) all-reduce(bf16[1,512]{1,0:T(2,128)(2,1)S(1)} %stack.29, bf16[1,512]{1,0:T(2,128)(2,1)S(1)} %stack.28, ...), channel_id=1, replica_groups=mesh['dp'=16,'tensor'=2] {'dp'}, use_global_device_ids=true, to_apply=%region_29.30 | all-reduce | flops 2048 | bytes 8192 | tf_op jit(solution)/shard_map/psum | solution.py:429
  488.6 206.0 %all-reduce.9.cloned.1.call-done = (bf16[1024,3,512]{2,0,1:T(8,128)(2,1)}, bf16[512,1024]{1,0:T(8,128)(2,1)}, bf16[1024,2048]{1,0:T(8,128)(2,1)}, bf16[2048,1024...) async-done(((bf16[1024,3,512]{2,0,1:T(8,128)(2,1)}, bf16[512,1024]{1,0:T(8,128)(2,1)}, bf16[1024,2048]{1,0:T(8,128)(2,1)}, ...) | async-done | bytes 13369360 | tf_op jit(solution)/shard_map/psum | solution.py:421
  694.6 5.6 convert_element_type.149
  701.8 4.4 convert_element_type.153
  706.2 4.4 convert_element_type.155
  (98 shorter events, 31.0 us)
Async XLA Ops:
  7.2 115.6 %copy-start = (bf16[512,1024]{1,0:T(8,128)(2,1)S(1)}, bf16[512,1024]{1,0:T(8,128)(2,1)}, u32[]{:S(2)}) copy-start(bf16[512,1024]{1,0:T(8,128)(2,1)} %param.16) | copy-start | bytes 3145732
  7.2 27.7 %all-gather.12.cloned.1.call-start = ((), (), s32[]{:S(2)}) async-start(), calls=%async_computation.11 | async-start | bytes 1744896 | tf_op jit(solution)/shard_map/all_gather | solution.py:343
  7.9 152.6 %reduce-scatter.5.cloned.1.call-start = ((), (), s32[]{:S(2)}) async-start(), calls=%async_computation.4 | async-start | bytes 3489792 | tf_op jit(solution)/shard_map/reduce_scatter | solution.py:352
  8.6 4.7 copy-start.13
  126.0 34.6 %copy-start.7 = (bf16[1,561,512]{2,1,0:T(8,128)(2,1)S(1)}, bf16[1,561,512]{2,1,0:T(8,128)(2,1)}, u32[]{:S(2)}) copy-start(bf16[1,561,512]{2,1,0:T(8,128)(2,1)} %param.12) | copy-start | bytes 1723396
  126.0 65.0 %all-gather.6.cloned.1.call-start = ((), (), s32[]{:S(2)}) async-start(), calls=%async_computation.5 | async-start | bytes 1744896 | tf_op jit(solution)/shard_map/all_gather | solution.py:357
  168.2 65.8 %reduce-scatter.7.cloned.1.call-start = ((), (), s32[]{:S(2)}) async-start(), calls=%async_computation.6 | async-start | bytes 1744896 | tf_op jit(solution)/shard_map/reduce_scatter | solution.py:360
  191.0 17.6 %copy-start.16 = (bf16[2048,1024]{1,0:T(8,128)(2,1)S(1)}, bf16[2048,1024]{1,0:T(8,128)(2,1)}, u32[]{:S(2)}) copy-start(bf16[2048,1024]{1,0:T(8,128)(2,1)} %param.18) | copy-start | bytes 12582916
  207.1 1.4 copy-start.23
  212.2 60.9 %all-gather.8.cloned.1.call-start = ((), (), s32[]{:S(2)}) async-start(), calls=%async_computation.7 | async-start | bytes 1744896 | tf_op jit(solution)/shard_map/all_gather | solution.py:374
  250.4 58.8 %reduce-scatter.9.cloned.1.call-start = ((), (), s32[]{:S(2)}) async-start(), calls=%async_computation.8 | async-start | bytes 1744896 | tf_op jit(solution)/shard_map/reduce_scatter | solution.py:381
  273.1 10.6 %copy-start.17 = (bf16[1024,2048]{1,0:T(8,128)(2,1)S(1)}, bf16[1024,2048]{1,0:T(8,128)(2,1)}, u32[]{:S(2)}) copy-start(bf16[1024,2048]{1,0:T(8,128)(2,1)} %param.17) | copy-start | bytes 12582916
  282.3 1.4 copy-start.22
  283.7 25.5 %copy-start.1 = (f32[561,512]{1,0:T(8,128)S(1)}, f32[561,512]{1,0:T(8,128)}, u32[]{:S(2)}) copy-start(f32[561,512]{1,0:T(8,128)} %get-tuple-element.52) | copy-start | bytes 3446788
  287.4 54.0 %all-gather.10.cloned.1.call-start = ((), (), s32[]{:S(2)}) async-start(), calls=%async_computation.9 | async-start | bytes 1744896 | tf_op jit(solution)/shard_map/all_gather | solution.py:387
  318.6 167.9 %reduce-scatter.11.cloned.1.call-start = ((), (), s32[]{:S(2)}) async-start(), calls=%async_computation.10 | async-start | bytes 1744896 | tf_op jit(solution)/shard_map/reduce_scatter | solution.py:405
  344.2 72.7 %copy-start.6 = (bf16[1024,3,512]{0,2,1:T(8,128)(2,1)S(1)}, bf16[1024,3,512]{0,2,1:T(8,128)(2,1)}, u32[]{:S(2)}) copy-start(bf16[1024,3,512]{0,2,1:T(8,128)(2,1)} %copy.27) | copy-start | bytes 9437188
  416.9 4.6 copy-start.20
  421.5 6.9 copy-start.21
  421.5 273.0 %all-reduce.9.cloned.1.call-start = ((), (), s32[]{:S(2)}) async-start(), calls=%async_computation.12 | async-start | bytes 26738688 | tf_op jit(solution)/shard_map/psum | solution.py:421
  421.6 6.9 copy-start.24
  428.5 5.1 copy-start.18
  428.5 5.1 copy-start.19
  437.6 4.8 copy-start.10
  442.4 3.2 copy-start.8
  448.8 1.1 copy-start.2
  448.8 37.7 %copy-start.3 = (f32[561,512]{1,0:T(8,128)S(1)}, f32[561,512]{1,0:T(8,128)}, u32[]{:S(2)}) copy-start(f32[561,512]{1,0:T(8,128)} %get-tuple-element.50) | copy-start | bytes 3446788
  694.5 5.6 copy-start.9
  694.5 7.2 %copy-start.5 = (bf16[1024,2048]{1,0:T(8,128)(2,1)S(1)}, bf16[1024,2048]{1,0:T(8,128)(2,1)}, u32[]{:S(2)}) copy-start(bf16[1024,2048]{1,0:T(8,128)(2,1)} %get-tuple-element.45) | copy-start | bytes 12582916
  701.8 4.5 copy-start.4
  706.2 4.4 copy-start.12
  706.2 5.4 copy-start.11
  (2 other events, 1.4 us)
Sparse Core Ops, SparseCore 0:
  9.5 25.2 all-gather.11
  126.1 34.4 reduce-scatter.4
  168.3 22.5 all-gather.5
  212.3 21.6 reduce-scatter.6
  250.5 22.5 all-gather.7
  287.5 21.6 reduce-scatter.8
  318.7 22.5 all-gather.9
  421.6 21.6 reduce-scatter.10
  449.1 245.3 all-reduce.8

commit v2 on v1

--- a/solution.py
+++ b/solution.py
@@ -256,10 +256,11 @@
                 else:
                     dqkv_ref[b * 128:b * 128 + n, at] = jnp.where(
                         mine, g[0:n].astype(BF16), dqkv_ref[b * 128:b * 128 + n, at])
+            turned = acc[...].T * SCALE
             if h == 0:
-                g_ref[...] = acc[...] * SCALE
+                g_ref[...] = turned
             else:
-                g_ref[...] += acc[...] * SCALE
+                g_ref[...] += turned
     dv = gt[...].T
     dqkv_ref[:, pl.ds(pl.multiple_of(2 * width + pair * 128, 128), 128)] = dv[0:slots, :].astype(BF16)
 
@@ -273,7 +274,7 @@
     def part(t):
         return pl.BlockSpec((None, slots, 128), lambda d, p: (d, 0, t * pairs + p))
     rel = pl.BlockSpec((3 * BUCKETS, 128), lambda d, p: (0, p))
-    grel = pl.BlockSpec((None, 128, 3 * BUCKETS), lambda d, p: (d, p, 0))
+    grel = pl.BlockSpec((None, 3 * BUCKETS, 128), lambda d, p: (d, 0, p))
     return pl.pallas_call(
         functools.partial(bwd_kernel, slots, sp, width),
         grid=(docs, pairs),
@@ -285,8 +286,8 @@
                   pl.BlockSpec((None, 2, sp), lambda d, p: (d, 0, 0))],
         out_specs=[pl.BlockSpec((None, slots, 3 * width), lambda d, p: (d, 0, 0)), grel, grel],
         out_shape=[jax.ShapeDtypeStruct((docs, slots, 3 * width), BF16),
-                   jax.ShapeDtypeStruct((docs, width, 3 * BUCKETS), F32),
-                   jax.ShapeDtypeStruct((docs, width, 3 * BUCKETS), F32)],
+                   jax.ShapeDtypeStruct((docs, 3 * BUCKETS, width), F32),
+                   jax.ShapeDtypeStruct((docs, 3 * BUCKETS, width), F32)],
         scratch_shapes=[pltpu.VMEM((sp, 128), BF16)] * 7
         + [pltpu.VMEM((sp, sp), BF16)] * 2 + [pltpu.VMEM((sp, sp + 256), BF16)] * 2
         + [pltpu.VMEM((128, sp), F32), pltpu.VMEM((128, 384), F32)],
@@ -295,28 +296,75 @@
     )(qkv, qkv, qkv, dctx, probs, relk, relq, boxes_col, boxes_row)
 
 
-def norm_forward(values_in, gain, shift, model_width):
-    row_total, row_square = lax.psum(
-        (jnp.sum(values_in, axis=1), jnp.sum(values_in * values_in, axis=1)), "tensor"
-    )
-    mean_row = row_total / model_width
-    scale_row = lax.rsqrt(row_square / model_width - mean_row * mean_row + 1e-05)
-    normed = (values_in - mean_row[:, None]) * scale_row[:, None]
-    return (normed * gain + shift, normed, scale_row)
-
-
-def norm_backward(upstream, normed, scale_row, gain, model_width):
-    scaled_up = upstream * gain
-    first_sum, second_sum = lax.psum(
-        (jnp.sum(scaled_up, axis=1), jnp.sum(scaled_up * normed, axis=1)), "tensor"
-    )
-    centered = (
-        scaled_up - first_sum[:, None] / model_width - normed * second_sum[:, None] / model_width
-    )
-    return scale_row[:, None] * centered
+EPSILON = 1e-05
+ROOT_HALF = math.sqrt(0.5)
+PDF_SCALE = 1.0 / math.sqrt(2.0 * math.pi)
+
+
+def dot_nt(a, b):
+    return lax.dot_general(a, b, (((1,), (1,)), ((), ())), preferred_element_type=F32)
+
+
+def dot_tn(a, b):
+    return lax.dot_general(a, b, (((0,), (0,)), ((), ())), preferred_element_type=F32)
+
+
+def norm_rows(values, gain, shift):
+    mean = jnp.mean(values, axis=1, keepdims=True)
+    scale = lax.rsqrt(jnp.mean(values * values, axis=1, keepdims=True) - mean * mean + EPSILON)
+    unit = (values - mean) * scale
+    return unit * gain + shift, unit, scale
+
+
+def norm_pull(upstream, unit, scale, gain):
+    scaled = upstream * gain
+    first = jnp.mean(scaled, axis=1, keepdims=True)
+    second = jnp.mean(scaled * unit, axis=1, keepdims=True)
+    return scale * (scaled - first - unit * second)
+
+
+def exchange_sum(parts, bits, size):
+    place = lax.axis_index("dp")
+
+    def swap(array, bit):
+        return lax.ppermute(array, "dp", [(i, i ^ bit) for i in range(size)])
+
+    def fold(array, bit):
+        half = array.shape[0] // 2
+        low = (place & bit) == 0
+        keep = jnp.where(low, array[:half], array[half:])
+        send = jnp.where(low, array[half:], array[:half])
+        return (keep.astype(F32) + swap(send, bit).astype(F32)).astype(BF16)
+
+    def unfold(array, bit):
+        low = (place & bit) == 0
+        other = swap(array, bit)
+        return jnp.concatenate([jnp.where(low, array, other), jnp.where(low, other, array)], axis=0)
+
+    arrays = [a for a, _ in parts]
+    for step in range(len(bits)):
+        arrays = [fold(a, order[step]) for a, (_, order) in zip(arrays, parts)]
+    for step in reversed(range(len(bits))):
+        arrays = [unfold(a, order[step]) for a, (_, order) in zip(arrays, parts)]
+    return arrays
+
+
+def sum_over_documents(table, size):
+    if size != 16:
+        return lax.psum(table, "dp")
+    rows = table.shape[0]
+    grain = 256
+    pieces = 4
+    step = -(-rows // (pieces * grain)) * grain
+    padded = jnp.pad(table, ((0, pieces * step - rows), (0, 0)))
+    orders = ((1, 2, 4, 8), (1, 4, 8, 2))
+    parts = [(padded[i * step:(i + 1) * step], orders[i % 2]) for i in range(pieces)]
+    return jnp.concatenate(exchange_sum(parts, orders[0], size), axis=0)[:rows]
 
 
 def on_device(
+    documents,
+    shards,
     hidden_in,
     lengths,
     boxes,
@@ -330,118 +378,129 @@
     norm_shifts,
     out_grad,
 ):
-    doc_count, slot_count, local_width = hidden_in.shape
+    doc_count, slot_count, width = hidden_in.shape
     row_count = doc_count * slot_count
     model_width = w_qkv.shape[0]
-    heads_here = local_width // HEAD_DIM
-    rel_k = rel_keys.reshape(3 * BUCKETS, local_width)
-    rel_q = rel_queries.reshape(3 * BUCKETS, local_width)
+    heads_here = width // HEAD_DIM
+    me = lax.axis_index("tensor")
+    pair = [(0, 1), (1, 0)]
+
+    def join(array, axis):
+        if shards != 2:
+            return lax.all_gather(array, "tensor", axis=axis, tiled=True)
+        other = lax.ppermute(array, "tensor", pair)
+        first = me == 0
+        return jnp.concatenate(
+            [jnp.where(first, array, other), jnp.where(first, other, array)], axis=axis)
+
+    def total(partial):
+        if shards != 2:
+            return lax.psum(partial, "tensor").astype(F32)
+        return partial.astype(F32) + lax.ppermute(partial, "tensor", pair).astype(F32)
+
+    def own(array):
+        return lax.dynamic_slice_in_dim(array, me * width, width, axis=array.ndim - 1)
+
+    def own_total(partial):
+        if shards != 2:
+            return lax.psum_scatter(partial, "tensor", scatter_dimension=1, tiled=True).astype(F32)
+        send = lax.dynamic_slice_in_dim(partial, (1 - me) * width, width, axis=1)
+        return own(partial).astype(F32) + lax.ppermute(send, "tensor", pair).astype(F32)
+
+    rel_k = rel_keys.reshape(3 * BUCKETS, width)
+    rel_q = rel_queries.reshape(3 * BUCKETS, width)
     padded = -(-slot_count // 128) * 128
     boxes_col = jnp.pad(boxes, ((0, 0), (0, padded - slot_count), (0, 0)))
     boxes_row = jnp.swapaxes(boxes_col, 1, 2)
-    local_rows = hidden_in.reshape(row_count, local_width)
-    full_rows = lax.all_gather(local_rows, "tensor", axis=1, tiled=True)
-    weight_qkv = w_qkv.reshape(model_width, 3 * local_width)
-    projected = jnp.dot(full_rows, weight_qkv, preferred_element_type=jnp.float32).astype(
-        jnp.bfloat16
-    )
-    projected = projected.reshape(doc_count, slot_count, 3 * local_width)
+
+    rows = join(hidden_in.reshape(row_count, width), 1)
+    weight_qkv = w_qkv.reshape(model_width, 3 * width)
+    projected = jnp.dot(rows, weight_qkv, preferred_element_type=F32).astype(BF16)
+    norms = join(jnp.concatenate([norm_gains, norm_shifts], axis=0), 1)
+    upstream = join(out_grad.reshape(row_count, width), 1)
+    out_whole = join(w_out, 0)
+    projected = projected.reshape(doc_count, slot_count, 3 * width)
     context, probs = attend_forward(lengths, projected, rel_k, rel_q, boxes_col, boxes_row, heads_here)
-    context_rows = context.reshape(row_count, local_width)
-    attn_terms = jnp.dot(context_rows, w_out, preferred_element_type=jnp.float32)
-    attn_out = lax.psum_scatter(attn_terms, "tensor", scatter_dimension=1, tiled=True)
-    first_sum_in = local_rows.astype(jnp.float32) + attn_out
-    normed_first, unit_first, scale_first = norm_forward(
-        first_sum_in, norm_gains[0], norm_shifts[0], model_width
-    )
-    normed_full = lax.all_gather(normed_first.astype(jnp.bfloat16), "tensor", axis=1, tiled=True)
-    upper = jnp.dot(normed_full, w_up, preferred_element_type=jnp.float32)
-    active = jax.nn.gelu(upper, approximate=False).astype(jnp.bfloat16)
-    ffn_out = lax.psum_scatter(
-        jnp.dot(active, w_down, preferred_element_type=jnp.float32).astype(jnp.bfloat16),
-        "tensor",
-        scatter_dimension=1,
-        tiled=True,
-    ).astype(jnp.float32)
-    result, unit_second, scale_second = norm_forward(
-        normed_first + ffn_out, norm_gains[1], norm_shifts[1], model_width
-    )
-    hidden_out = result.astype(jnp.bfloat16).reshape(doc_count, slot_count, local_width)
-    upstream = out_grad.reshape(row_count, local_width).astype(jnp.float32)
-    gain_second = jnp.sum(upstream * unit_second, axis=0)
-    shift_second = jnp.sum(upstream, axis=0)
-    grad_second = norm_backward(upstream, unit_second, scale_second, norm_gains[1], model_width)
-    ffn_grad_full = lax.all_gather(grad_second.astype(jnp.bfloat16), "tensor", axis=1, tiled=True)
-    down_grad = jnp.einsum("rf,rd->fd", active, ffn_grad_full, preferred_element_type=jnp.float32)
-    grad_active = jnp.einsum("rd,fd->rf", ffn_grad_full, w_down, preferred_element_type=jnp.float32)
-    _, gelu_pull = jax.vjp(lambda entry: jax.nn.gelu(entry, approximate=False), upper)
-    grad_upper = gelu_pull(grad_active)[0].astype(jnp.bfloat16)
-    up_grad = jnp.einsum("rd,rf->df", normed_full, grad_upper, preferred_element_type=jnp.float32)
-    hidden_terms = jnp.einsum("rf,df->rd", grad_upper, w_up, preferred_element_type=jnp.float32)
-    grad_hidden = grad_second + lax.psum_scatter(
-        hidden_terms.astype(jnp.bfloat16), "tensor", scatter_dimension=1, tiled=True
-    ).astype(jnp.float32)
-    gain_first = jnp.sum(grad_hidden * unit_first, axis=0)
-    shift_first = jnp.sum(grad_hidden, axis=0)
-    grad_first = norm_backward(grad_hidden, unit_first, scale_first, norm_gains[0], model_width)
-    attn_grad_full = lax.all_gather(grad_first.astype(jnp.bfloat16), "tensor", axis=1, tiled=True)
-    out_weight_grad = jnp.einsum(
-        "rc,rd->cd", context_rows, attn_grad_full, preferred_element_type=jnp.float32
-    )
-    grad_context = jnp.einsum(
-        "rd,cd->rc", attn_grad_full, w_out, preferred_element_type=jnp.float32
-    ).astype(jnp.bfloat16)
-    grad_context = grad_context.reshape(doc_count, slot_count, local_width)
+    context = context.reshape(row_count, width)
+
+    attn = jnp.dot(join(context, 1), out_whole, preferred_element_type=F32)
+    h1, unit_first, scale_first = norm_rows(rows.astype(F32) + attn, norms[0:1], norms[2:3])
+    h1_low = h1.astype(BF16)
+    upper = jnp.dot(h1_low, w_up, preferred_element_type=F32)
+    chance = 0.5 * (1.0 + lax.erf(upper * ROOT_HALF))
+    active = (upper * chance).astype(BF16)
+    slope = (chance + upper * (PDF_SCALE * jnp.exp(-0.5 * upper * upper))).astype(BF16)
+    ffn = total(jnp.dot(active, w_down, preferred_element_type=F32).astype(BF16))
+    result, unit_second, scale_second = norm_rows(h1 + ffn, norms[1:2], norms[3:4])
+    hidden_out = own(result.astype(BF16)).reshape(doc_count, slot_count, width)
+
+    upstream = upstream.astype(F32)
+    grad_second = norm_pull(upstream, unit_second, scale_second, norms[1:2])
+    ffn_grad = grad_second.astype(BF16)
+    grad_upper = (dot_nt(ffn_grad, w_down) * slope.astype(F32)).astype(BF16)
+    hidden_part = dot_nt(grad_upper, w_up).astype(BF16)
+    units = w_up.shape[1]
+    down_grad = dot_tn(active, ffn_grad).astype(BF16)
+    early = documents == 16 and units % model_width == 0
+    if early:
+        ffn_table = jnp.concatenate([down_grad] + [
+            dot_tn(h1_low, grad_upper[:, t:t + model_width]).astype(BF16)
+            for t in range(0, units, model_width)], axis=0)
+        ffn_shard = lax.psum_scatter(ffn_table, "dp", scatter_dimension=0, tiled=True)
+    else:
+        up_grad = dot_tn(h1_low, grad_upper).astype(BF16)
+        down_grad, up_grad = lax.psum((down_grad, up_grad), "dp")
+    grad_hidden = grad_second + total(hidden_part)
+    grad_first = norm_pull(grad_hidden, unit_first, scale_first, norms[0:1])
+    attn_grad = grad_first.astype(BF16)
+    norm_grads = own(jnp.stack([
+        jnp.sum(grad_hidden * unit_first, axis=0),
+        jnp.sum(upstream * unit_second, axis=0),
+        jnp.sum(grad_hidden, axis=0),
+        jnp.sum(upstream, axis=0)]))
+
+    out_weight_grad = dot_tn(context, attn_grad)
+    grad_context = dot_nt(attn_grad, w_out).astype(BF16).reshape(doc_count, slot_count, width)
     grad_projected, rel_k_sum, rel_q_sum = attend_backward(
         projected, grad_context, probs, rel_k, rel_q, boxes_col, boxes_row, heads_here
     )
-    rel_keys_grad = jnp.sum(rel_k_sum, axis=0).T.reshape(3, BUCKETS, local_width)
-    rel_queries_grad = jnp.sum(rel_q_sum, axis=0).T.reshape(3, BUCKETS, local_width)
-    grad_rows = grad_projected.reshape(row_count, 3 * local_width)
-    qkv_grad = jnp.einsum(
-        "rd,rc->dc", full_rows, grad_rows, preferred_element_type=jnp.float32
-    ).reshape(model_width, 3, local_width)
-    input_terms = jnp.einsum("rc,dc->rd", grad_rows, weight_qkv, preferred_element_type=jnp.float32)
-    input_grad = grad_first + lax.psum_scatter(
-        input_terms.astype(jnp.bfloat16), "tensor", scatter_dimension=1, tiled=True
-    ).astype(jnp.float32)
-    input_grad = input_grad.astype(jnp.bfloat16).reshape(doc_count, slot_count, local_width)
-    (
-        qkv_grad,
-        out_weight_grad,
-        up_grad,
-        down_grad,
-        rel_keys_grad,
-        rel_queries_grad,
-        gain_first,
-        shift_first,
-        gain_second,
-        shift_second,
-    ) = (
-        lax.psum(qkv_grad.astype(jnp.bfloat16), "dp").astype(jnp.float32),
-        lax.psum(out_weight_grad.astype(jnp.bfloat16), "dp").astype(jnp.float32),
-        lax.psum(up_grad.astype(jnp.bfloat16), "dp").astype(jnp.float32),
-        lax.psum(down_grad.astype(jnp.bfloat16), "dp").astype(jnp.float32),
-        lax.psum(rel_keys_grad.astype(jnp.bfloat16), "dp").astype(jnp.float32),
-        lax.psum(rel_queries_grad.astype(jnp.bfloat16), "dp").astype(jnp.float32),
-        lax.psum(gain_first.astype(jnp.bfloat16), "dp").astype(jnp.float32),
-        lax.psum(shift_first.astype(jnp.bfloat16), "dp").astype(jnp.float32),
-        lax.psum(gain_second.astype(jnp.bfloat16), "dp").astype(jnp.float32),
-        lax.psum(shift_second.astype(jnp.bfloat16), "dp").astype(jnp.float32),
-    )
-    gains_grad = jnp.stack([gain_first, gain_second])
-    shifts_grad = jnp.stack([shift_first, shift_second])
+    if early:
+        grad_projected, ffn_shard = lax.optimization_barrier((grad_projected, ffn_shard))
+        ffn_table = lax.all_gather(ffn_shard, "dp", axis=0, tiled=True)
+        down_grad = ffn_table[:units]
+        up_grad = jnp.concatenate([
+            ffn_table[units + t:units + t + model_width] for t in range(0, units, model_width)], axis=1)
+    grad_rows = grad_projected.reshape(row_count, 3 * width)
+    input_part = dot_nt(grad_rows, weight_qkv).astype(BF16)
+    input_grad = own(grad_first) + own_total(input_part)
+    input_grad = input_grad.astype(BF16).reshape(doc_count, slot_count, width)
+    qkv_grads = [dot_tn(rows, grad_rows[:, t * width:(t + 1) * width]) for t in range(3)]
+    pieces = qkv_grads + [jnp.sum(rel_k_sum, axis=0), jnp.sum(rel_q_sum, axis=0)]
+    pieces += [out_weight_grad[:, t * width:(t + 1) * width] for t in range(shards)]
+    pieces += [norm_grads]
+    table = sum_over_documents(jnp.concatenate([p.astype(BF16) for p in pieces], axis=0), documents)
+    table = table.astype(F32)
+    found = []
+    at = 0
+    for p in pieces:
+        found.append(table[at:at + p.shape[0]])
+        at += p.shape[0]
+    qkv_grad = jnp.stack(found[0:3], axis=1)
+    rel_keys_grad = found[3].reshape(3, BUCKETS, width)
+    rel_queries_grad = found[4].reshape(3, BUCKETS, width)
+    out_weight_grad = jnp.concatenate(found[5:5 + shards], axis=1)
+    norm_grads = found[5 + shards]
     return (
         hidden_out,
         input_grad,
         qkv_grad,
         out_weight_grad,
-        up_grad,
-        down_grad,
+        up_grad.astype(F32),
+        down_grad.astype(F32),
         rel_keys_grad,
         rel_queries_grad,
-        gains_grad,
-        shifts_grad,
+        norm_grads[0:2],
+        norm_grads[2:4],
     )
 
 
@@ -472,6 +531,5 @@
         P(None, "tensor"),
         P(None, "tensor"),
     )
-    return jax.shard_map(
-        on_device, mesh=mesh, in_specs=in_specs, out_specs=out_specs, check_vma=False
-    )
+    body = functools.partial(on_device, mesh.shape["dp"], mesh.shape["tensor"])
+    return jax.shard_map(body, mesh=mesh, in_specs=in_specs, out_specs=out_specs, check_vma=False)

time: 726 us -> 503 us (0.69)
  waiting for transfers between devices: 371 us -> 176 us
  blocking collectives: 55.8 us -> 0 us
  starting transfers between devices: 1.36 us -> 47.5 us
  matrix products: 67.9 us -> 43.3 us
  other arithmetic: 35.5 us -> 43.6 us
    psum x1 -> x0, waiting for transfers between devices: 206 us -> none  [on_device(): lax.psum(qkv_grad.astype(jnp.bfloat16), 'dp').astype(jnp.float32)]
    ppermute x0 -> x40, waiting for transfers between devices: none -> 176 us  [the longest x32 103 us: swap(): return lax.ppermute(array, 'dp', [(i, i ^ bit) for i in range(size)])]
    all_gather x4 -> x1, waiting for transfers between devices: 87.2 us -> 0.01 us  [on_device(): ffn_table = lax.all_gather(ffn_shard, 'dp', axis=0, tiled=True)]
    reduce_scatter x4 -> x1, waiting for transfers between devices: 77.4 us -> 0.01 us  [on_device(): lax.psum_scatter(ffn_table, 'dp', scatter_dimension=0, tiled=True)]
    psum x5 -> x0, blocking collectives: 55.8 us -> none  [the longest x1 35.8 us: on_device(): lax.psum(gain_second.astype(jnp.bfloat16), 'dp').astype(jnp.float32)]
    ppermute x0 -> x40, starting transfers between devices: none -> 35.8 us  [the longest x32 25.1 us: swap(): return lax.ppermute(array, 'dp', [(i, i ^ bit) for i in range(size)])]
    dot_general x12 -> x15, matrix products: 67.9 us -> 43.3 us  [the longest x4 18.4 us: dot_nt(): lax.dot_general(a, b, (((1,), (1,)), ((), ())), preferred_element_type=F32)]
    convert_element_type x10 -> x20, other arithmetic: 26.1 us -> 13.7 us  [the longest x1 4.44 us: on_device(): down_grad.astype(F32)]
  transfers between devices with their start and end apart: 9 -> 42, of which waited for: 8 -> 22; matrix products, arithmetic and copies ran while one was open for 5% -> 11% of each run, Pallas kernels for 0% -> 31%
where the time goes in v2:
time: 503 us; the launch traced here: 496 us
  waiting for transfers between devices  176 us (35%)
  Pallas kernels  152 us (30%)
  starting transfers between devices  47.5 us (9%)
  other arithmetic  43.6 us (9%)
  matrix products  43.3 us (9%)
  local copies, waits for them, and re-layouts  17 us (3%)
  between operations  16.2 us (3%)
    ppermute x32, waiting for transfers between devices, swap(): return lax.ppermute(array, 'dp', [(i, i ^ bit) for i in range(size)])  103 us
    pallas_call x1, Pallas kernels, attend_forward(): pl.pallas_call(functools.partial(fwd_kernel, slots, sp), out_shape=[jax.S...  82.5 us
    pallas_call x1, Pallas kernels, attend_backward(): pl.pallas_call(functools.partial(bwd_kernel, slots, sp, width), grid=(doc...  69.8 us
    ppermute x5, waiting for transfers between devices, join(): other = lax.ppermute(array, 'tensor', pair)  51.1 us
    ppermute x32, starting transfers between devices, swap(): return lax.ppermute(array, 'dp', [(i, i ^ bit) for i in range(size)])  25.1 us
    ppermute x2, waiting for transfers between devices, total(): lax.ppermute(partial, 'tensor', pair).astype(F32)  22.3 us
    dot_general x4, matrix products, dot_nt(): lax.dot_general(a, b, (((1,), (1,)), ((), ())), preferred_element_type=F32)  18.4 us
    dot_general x7, matrix products, dot_tn(): lax.dot_general(a, b, (((0,), (0,)), ((), ())), preferred_element_type=F32)  14.1 us
  transfers between devices with their start and end apart: 42, of which 22 were waited for; matrix products, arithmetic and copies ran while one was open for 11% of the time, Pallas kernels for 31%

profile of v2, /device:TPU:0, one launch (start us, length us, event | category | flops | bytes accessed | tf_op | source)
XLA Modules:
  0.0 496.2 jit_solution(14363065626248578656)
XLA Ops:
  7.2 3.1 collective-permute-start
  15.3 3.2 copy.24
  19.2 5.4 %collective-permute-done = bf16[561,512]{1,0:T(8,128)(2,1)} collective-permute-done((bf16[561,512]{1,0:T(8,128)(2,1)}, bf16[561,512]{1,0:T(8,128)(2,1)}, u32[]{:S(2)}, u32[]{:S(2)}) %collective-permute-start) | collective-permute-done | bytes 574496 | tf_op jit(solution)/shard_map/ppermute | solution.py:391
  25.9 3.2 fusion.8.q_ref.k_ref.v_ref
  29.2 82.5 %attend_forward.1 = (bf16[1,561,512]{2,1,0:T(8,128)(2,1)}, bf16[1,8,640,640]{3,2,1,0:T(8,128)(2,1)}) custom-call(s32[1]{0:T(128)S(6)} %copy.42.len_ref, bf16[1,561,1536]{2,1,0:T(8,128)(2,1)} %fusion.8.q_ref.k_ref.v_ref, bf16[1,561,1536]{2,1,0:T(8,128)(2,1)} %fusion.8.q_ref.k_ref.v_ref, bf16[1,561,1536]{2,1,0:T(8,128)(2,1)} %fusion.8.q_ref.k_ref.v_ref, ...), custom_call_target="tpu_custom_call" | custom-call | tf_op jit(solution)/shard_map/attend_forward/pallas_call | solution.py:131
  115.2 10.2 %collective-permute-done.1 = bf16[561,512]{1,0:T(8,128)(2,1)S(1)} collective-permute-done((bf16[561,512]{1,0:T(8,128)(2,1)}, bf16[561,512]{1,0:T(8,128)(2,1)S(1)}, u32[]{:S(2)}, u32[]{:S(2)}) %collective-permute-start.1) | collective-permute-done | bytes 574496 | tf_op jit(solution)/shard_map/ppermute | solution.py:391
  127.7 3.4 multiply_convert_fusion.1
  135.8 35.5 %collective-permute-done.5 = bf16[561,512]{1,0:T(8,128)(2,1)S(1)} collective-permute-done((bf16[561,512]{1,0:T(8,128)(2,1)S(1)}, bf16[561,512]{1,0:T(8,128)(2,1)S(1)}, u32[]{:S(2)}, u32[]{:S(2)}) %collective-permute-start.5) | collective-permute-done | bytes 574496 | tf_op jit(solution)/shard_map/ppermute | solution.py:391
  173.7 4.4 convolution_convert_fusion
  178.1 6.0 %multiply_convert_fusion = bf16[561,2048]{1,0:T(8,128)(2,1)S(1)} fusion(bf16[2048,1024]{1,0:T(8,128)(2,1)S(1)} %copy-done.28, f32[561,2048]{1,0:T(8,128)S(1)} %get-tuple-element.108, f32[561,1024]{1,0:T(8,128)S(1)} %get-tuple-element.45, f32[561]{0:T(1024)S(1)} %get-tuple-element.115, f32[561]{0:T(1024)S(1)} %get-tuple-element.116, f32[1024]{0:T(1024)S(1)} %bitcast.83, ...), kind=kOutput, calls=%fused_computation.10 | convolution fusion | flops 2372536320 | bytes 14545484 | tf_op jit(solution)/shard_map/dot_general | solution.py:305
  187.9 3.9 pad_maximum_fusion
  191.8 11.7 %all-gather.2.cloned.1.call-start = ((), (), s32[]{:S(2)}) async-start(), calls=%async_computation.2 | async-start | bytes 8912896 | tf_op jit(solution)/shard_map/all_gather | solution.py:469
  203.5 7.2 %convolution_convert_fusion.4 = bf16[561,1024]{1,0:T(8,128)(2,1)} fusion(bf16[561,2048]{1,0:T(8,128)(2,1)} %copy-done.31, bf16[1024,2048]{1,0:T(8,128)(2,1)} %param.17), kind=kOutput, calls=%fused_computation.51 | convolution fusion | flops 2353579008 | bytes 7641088 | tf_op jit(solution)/shard_map/dot_general | solution.py:305
  212.8 22.3 %collective-permute-done.6 = bf16[561,1024]{1,0:T(8,128)(2,1)} collective-permute-done((bf16[561,1024]{1,0:T(8,128)(2,1)}, bf16[561,1024]{1,0:T(8,128)(2,1)}, u32[]{:S(2)}, u32[]{:S(2)}) %collective-permute-start.6) | collective-permute-done | bytes 1148960 | tf_op jit(solution)/shard_map/ppermute | solution.py:399
  235.2 4.4 multiply_reduce_fusion
  242.5 69.8 %attend_backward.1 = (bf16[1,561,1536]{2,1,0:T(8,128)(2,1)}, f32[1,384,512]{2,1,0:T(8,128)}, f32[1,384,512]{2,1,0:T(8,128)}) custom-call(bf16[1,561,1536]{2,1,0:T(8,128)(2,1)} %fusion.8.q_ref.k_ref.v_ref, bf16[1,561,1536]{2,1,0:T(8,128)(2,1)} %fusion.8.q_ref.k_ref.v_ref, bf16[1,561,1536]{2,1,0:T(8,128)(2,1)} %fusion.8.q_ref.k_ref.v_ref, ...), custom_call_target="tpu_custom_call" | custom-call | tf_op jit(solution)/shard_map/attend_backward/pallas_call | solution.py:278
  314.4 3.6 convolution_convert_fusion.6
  341.3 16.6 %collective-permute-done.33 = bf16[320,512]{1,0:T(8,128)(2,1)S(1)} collective-permute-done((bf16[320,512]{1,0:T(8,128)(2,1)S(1)}, bf16[320,512]{1,0:T(8,128)(2,1)S(1)}, u32[]{:S(2)}, u32[]{:S(2)}) %collective-permute-start.33) | collective-permute-done | bytes 327712 | tf_op jit(solution)/shard_map/ppermute | solution.py:330
  358.0 3.8 collective-permute-start.34
  361.8 11.5 %collective-permute-done.17 = bf16[320,512]{1,0:T(8,128)(2,1)S(1)} collective-permute-done((bf16[320,512]{1,0:T(8,128)(2,1)S(1)}, bf16[320,512]{1,0:T(8,128)(2,1)S(1)}, u32[]{:S(2)}, u32[]{:S(2)}) %collective-permute-start.17) | collective-permute-done | bytes 327712 | tf_op jit(solution)/shard_map/ppermute | solution.py:330
  380.0 7.6 %collective-permute-done.18 = bf16[160,512]{1,0:T(8,128)(2,1)S(1)} collective-permute-done((bf16[160,512]{1,0:T(8,128)(2,1)S(1)}, bf16[160,512]{1,0:T(8,128)(2,1)S(1)}, u32[]{:S(2)}, u32[]{:S(2)}) %collective-permute-start.18) | collective-permute-done | bytes 163872 | tf_op jit(solution)/shard_map/ppermute | solution.py:330
  389.3 8.0 %collective-permute-done.26 = bf16[160,512]{1,0:T(8,128)(2,1)S(1)} collective-permute-done((bf16[160,512]{1,0:T(8,128)(2,1)S(1)}, bf16[160,512]{1,0:T(8,128)(2,1)S(1)}, u32[]{:S(2)}, u32[]{:S(2)}) %collective-permute-start.26) | collective-permute-done | bytes 163872 | tf_op jit(solution)/shard_map/ppermute | solution.py:330
  397.5 8.0 %collective-permute-done.10 = bf16[160,512]{1,0:T(8,128)(2,1)S(1)} collective-permute-done((bf16[160,512]{1,0:T(8,128)(2,1)S(1)}, bf16[160,512]{1,0:T(8,128)(2,1)S(1)}, u32[]{:S(2)}, u32[]{:S(2)}) %collective-permute-start.10) | collective-permute-done | bytes 163872 | tf_op jit(solution)/shard_map/ppermute | solution.py:330
  411.0 8.4 %collective-permute-done.11 = bf16[80,512]{1,0:T(8,128)(2,1)S(1)} collective-permute-done((bf16[80,512]{1,0:T(8,128)(2,1)S(1)}, bf16[80,512]{1,0:T(8,128)(2,1)S(1)}, u32[]{:S(2)}, u32[]{:S(2)}) %collective-permute-start.11) | collective-permute-done | bytes 81952 | tf_op jit(solution)/shard_map/ppermute | solution.py:330
  419.5 3.0 collective-permute-start.37
  422.6 10.7 %collective-permute-done.28 = bf16[80,512]{1,0:T(8,128)(2,1)S(1)} collective-permute-done((bf16[80,512]{1,0:T(8,128)(2,1)S(1)}, bf16[80,512]{1,0:T(8,128)(2,1)S(1)}, u32[]{:S(2)}, u32[]{:S(2)}) %collective-permute-start.28) | collective-permute-done | bytes 81952 | tf_op jit(solution)/shard_map/ppermute | solution.py:330
  433.4 5.2 %collective-permute-done.12 = bf16[80,512]{1,0:T(8,128)(2,1)S(1)} collective-permute-done((bf16[80,512]{1,0:T(8,128)(2,1)S(1)}, bf16[80,512]{1,0:T(8,128)(2,1)S(1)}, u32[]{:S(2)}, u32[]{:S(2)}) %collective-permute-start.12) | collective-permute-done | bytes 81952 | tf_op jit(solution)/shard_map/ppermute | solution.py:330
  438.7 4.0 collective-permute-done.37
  452.9 6.1 %collective-permute-done.38 = bf16[320,512]{1,0:T(8,128)(2,1)S(1)} collective-permute-done((bf16[320,512]{1,0:T(8,128)(2,1)S(1)}, bf16[320,512]{1,0:T(8,128)(2,1)S(1)}, u32[]{:S(2)}, u32[]{:S(2)}) %collective-permute-start.38) | collective-permute-done | bytes 327712 | tf_op jit(solution)/shard_map/ppermute | solution.py:330
  472.5 3.4 pad_maximum_fusion.1
  480.0 4.4 maximum_convert_fusion
  484.4 4.4 slice_convert_fusion.1
  (249 shorter events, 95.0 us)
Async XLA Ops:
  7.2 307.2 %reduce-scatter.2.cloned.1.call-start = ((), (), s32[]{:S(2)}) async-start(), calls=%async_computation.1 | async-start | bytes 8912896 | tf_op jit(solution)/shard_map/reduce_scatter | solution.py:449
  7.2 17.4 %collective-permute-start = (bf16[561,512]{1,0:T(8,128)(2,1)}, bf16[561,512]{1,0:T(8,128)(2,1)}, u32[]{:S(2)}, u32[]{:S(2)}) collective-permute-start(bf16[561,512]{1,0:T(8,128)(2,1)} %bitcast.74), channel_id=1, source_target_pairs={{0,1},{1,0},{2,3},{3,2},{4,5},{5,4},{6,7},{7,6},{8,9},{9,8},{10,11... | collective-permute-start | bytes 1723400 | tf_op jit(solution)/shard_map/ppermute | solution.py:391
  11.0 102.8 %collective-permute-start.3 = (f32[4,512]{1,0:T(4,128)S(1)}, f32[4,512]{1,0:T(4,128)S(1)}, u32[]{:S(2)}, u32[]{:S(2)}) collective-permute-start(f32[4,512]{1,0:T(4,128)S(1)} %pad_maximum_fusion.22), channel_id=1, source_target_pairs={{0,1},{1,0},{2,3},{3,2},{4,5},{5,4},{6,7},{7,6},{8,9},{9,8},{10,11... | collective-permute-start | bytes 24584 | tf_op jit(solution)/shard_map/ppermute | solution.py:391
  11.1 102.7 %collective-permute-start.2 = (bf16[512,1024]{1,0:T(8,128)(2,1)}, bf16[512,1024]{1,0:T(8,128)(2,1)}, u32[]{:S(2)}, u32[]{:S(2)}) collective-permute-start(bf16[512,1024]{1,0:T(8,128)(2,1)} %param.16), channel_id=1, source_target_pairs={{0,1},{1,0},{2,3},{3,2},{4,5},{5,4},{6,7},{7,6},{8,9},{9,8},{10,11... | collective-permute-start | bytes 3145736 | tf_op jit(solution)/shard_map/ppermute | solution.py:391
  111.7 13.7 %collective-permute-start.1 = (bf16[561,512]{1,0:T(8,128)(2,1)}, bf16[561,512]{1,0:T(8,128)(2,1)S(1)}, u32[]{:S(2)}, u32[]{:S(2)}) collective-permute-start(bf16[561,512]{1,0:T(8,128)(2,1)} %bitcast.76), channel_id=1, source_target_pairs={{0,1},{1,0},{2,3},{3,2},{4,5},{5,4},{6,7},{7,6},{8,9},{9,8},{10,11... | collective-permute-start | bytes 1723400 | tf_op jit(solution)/shard_map/ppermute | solution.py:391
  133.7 37.7 %collective-permute-start.4 = (bf16[561,1024]{1,0:T(8,128)(2,1)S(1)}, bf16[561,1024]{1,0:T(8,128)(2,1)S(1)}, u32[]{:S(2)}, u32[]{:S(2)}) collective-permute-start(bf16[561,1024]{1,0:T(8,128)(2,1)S(1)} %convolution_convert_fusion.5), channel_id=1, source_target_pairs={{0,1},{1,0},{2,3},{3,2},{4,5},{5,4},{6,7},{7,6},{8,9},{9,8},{10,11... | collective-permute-start | bytes 3446792 | tf_op jit(solution)/shard_map/ppermute | solution.py:399
  135.2 36.1 %collective-permute-start.5 = (bf16[561,512]{1,0:T(8,128)(2,1)S(1)}, bf16[561,512]{1,0:T(8,128)(2,1)S(1)}, u32[]{:S(2)}, u32[]{:S(2)}) collective-permute-start(bf16[561,512]{1,0:T(8,128)(2,1)S(1)} %bitcast.75), channel_id=1, source_target_pairs={{0,1},{1,0},{2,3},{3,2},{4,5},{5,4},{6,7},{7,6},{8,9},{9,8},{10,11... | collective-permute-start | bytes 1723400 | tf_op jit(solution)/shard_map/ppermute | solution.py:391
  191.8 285.4 %all-gather.2.cloned.1.call-start = ((), (), s32[]{:S(2)}) async-start(), calls=%async_computation.2 | async-start | bytes 8912896 | tf_op jit(solution)/shard_map/all_gather | solution.py:469
  210.7 24.5 %collective-permute-start.6 = (bf16[561,1024]{1,0:T(8,128)(2,1)}, bf16[561,1024]{1,0:T(8,128)(2,1)}, u32[]{:S(2)}, u32[]{:S(2)}) collective-permute-start(bf16[561,1024]{1,0:T(8,128)(2,1)} %convolution_convert_fusion.4), channel_id=1, source_target_pairs={{0,1},{1,0},{2,3},{3,2},{4,5},{5,4},{6,7},{7,6},{8,9},{9,8},{10,11... | collective-permute-start | bytes 3446792 | tf_op jit(solution)/shard_map/ppermute | solution.py:399
  318.9 13.3 %collective-permute-start.7 = (bf16[561,512]{1,0:T(8,128)(2,1)}, bf16[561,512]{1,0:T(8,128)(2,1)}, u32[]{:S(2)}, u32[]{:S(2)}) collective-permute-start(bf16[561,512]{1,0:T(8,128)(2,1)} %constant_dynamic-slice_fusion), channel_id=1, source_target_pairs={{0,1},{1,0},{2,3},{3,2},{4,5},{5,4},{6,7},{7,6},{8,9},{9,8},{10,11... | collective-permute-start | bytes 1723400 | tf_op jit(solution)/shard_map/ppermute | solution.py:408
  336.1 21.8 %collective-permute-start.33 = (bf16[320,512]{1,0:T(8,128)(2,1)S(1)}, bf16[320,512]{1,0:T(8,128)(2,1)S(1)}, u32[]{:S(2)}, u32[]{:S(2)}) collective-permute-start(bf16[320,512]{1,0:T(8,128)(2,1)S(1)} %broadcast_select_fusion.14), channel_id=1, source_target_pairs={{0,8},{2,10},{4,12},{6,14},{8,0},{10,2},{12,4},{14,6},{16,24},{18,... | collective-permute-start | bytes 983048 | tf_op jit(solution)/shard_map/ppermute | solution.py:330
  338.0 35.4 %collective-permute-start.17 = (bf16[320,512]{1,0:T(8,128)(2,1)S(1)}, bf16[320,512]{1,0:T(8,128)(2,1)S(1)}, u32[]{:S(2)}, u32[]{:S(2)}) collective-permute-start(bf16[320,512]{1,0:T(8,128)(2,1)S(1)} %broadcast_select_fusion.17), channel_id=1, source_target_pairs={{0,8},{2,10},{4,12},{6,14},{8,0},{10,2},{12,4},{14,6},{16,24},{18,... | collective-permute-start | bytes 983048 | tf_op jit(solution)/shard_map/ppermute | solution.py:330
  338.9 36.5 %collective-permute-start.25 = (bf16[320,512]{1,0:T(8,128)(2,1)S(1)}, bf16[320,512]{1,0:T(8,128)(2,1)S(1)}, u32[]{:S(2)}, u32[]{:S(2)}) collective-permute-start(bf16[320,512]{1,0:T(8,128)(2,1)S(1)} %broadcast_select_fusion.20), channel_id=1, source_target_pairs={{0,4},{2,6},{4,0},{6,2},{8,12},{10,14},{12,8},{14,10},{16,20},{18,... | collective-permute-start | bytes 983048 | tf_op jit(solution)/shard_map/ppermute | solution.py:330
  340.8 37.3 %collective-permute-start.9 = (bf16[320,512]{1,0:T(8,128)(2,1)S(1)}, bf16[320,512]{1,0:T(8,128)(2,1)S(1)}, u32[]{:S(2)}, u32[]{:S(2)}) collective-permute-start(bf16[320,512]{1,0:T(8,128)(2,1)S(1)} %broadcast_select_fusion.23), channel_id=1, source_target_pairs={{0,4},{2,6},{4,0},{6,2},{8,12},{10,14},{12,8},{14,10},{16,20},{18,... | collective-permute-start | bytes 983048 | tf_op jit(solution)/shard_map/ppermute | solution.py:330
  358.0 20.3 %collective-permute-start.34 = (bf16[160,512]{1,0:T(8,128)(2,1)S(1)}, bf16[160,512]{1,0:T(8,128)(2,1)S(1)}, u32[]{:S(2)}, u32[]{:S(2)}) collective-permute-start(bf16[160,512]{1,0:T(8,128)(2,1)S(1)} %broadcast_select_fusion.26), channel_id=1, source_target_pairs={{0,16},{2,18},{4,20},{6,22},{8,24},{10,26},{12,28},{14,30},{16,0},... | collective-permute-start | bytes 491528 | tf_op jit(solution)/shard_map/ppermute | solution.py:330
  373.5 14.1 %collective-permute-start.18 = (bf16[160,512]{1,0:T(8,128)(2,1)S(1)}, bf16[160,512]{1,0:T(8,128)(2,1)S(1)}, u32[]{:S(2)}, u32[]{:S(2)}) collective-permute-start(bf16[160,512]{1,0:T(8,128)(2,1)S(1)} %broadcast_select_fusion.29), channel_id=1, source_target_pairs={{0,16},{2,18},{4,20},{6,22},{8,24},{10,26},{12,28},{14,30},{16,0},... | collective-permute-start | bytes 491528 | tf_op jit(solution)/shard_map/ppermute | solution.py:330
  375.5 21.8 %collective-permute-start.26 = (bf16[160,512]{1,0:T(8,128)(2,1)S(1)}, bf16[160,512]{1,0:T(8,128)(2,1)S(1)}, u32[]{:S(2)}, u32[]{:S(2)}) collective-permute-start(bf16[160,512]{1,0:T(8,128)(2,1)S(1)} %broadcast_select_fusion.32), channel_id=1, source_target_pairs={{0,8},{2,10},{4,12},{6,14},{8,0},{10,2},{12,4},{14,6},{16,24},{18,... | collective-permute-start | bytes 491528 | tf_op jit(solution)/shard_map/ppermute | solution.py:330
  378.2 27.3 %collective-permute-start.10 = (bf16[160,512]{1,0:T(8,128)(2,1)S(1)}, bf16[160,512]{1,0:T(8,128)(2,1)S(1)}, u32[]{:S(2)}, u32[]{:S(2)}) collective-permute-start(bf16[160,512]{1,0:T(8,128)(2,1)S(1)} %broadcast_select_fusion.35), channel_id=1, source_target_pairs={{0,8},{2,10},{4,12},{6,14},{8,0},{10,2},{12,4},{14,6},{16,24},{18,... | collective-permute-start | bytes 491528 | tf_op jit(solution)/shard_map/ppermute | solution.py:330
  378.4 27.3 %collective-permute-start.35 = (bf16[80,512]{1,0:T(8,128)(2,1)S(1)}, bf16[80,512]{1,0:T(8,128)(2,1)S(1)}, u32[]{:S(2)}, u32[]{:S(2)}) collective-permute-start(bf16[80,512]{1,0:T(8,128)(2,1)S(1)} %broadcast_select_fusion.38), channel_id=1, source_target_pairs={{0,4},{2,6},{4,0},{6,2},{8,12},{10,14},{12,8},{14,10},{16,20},{18,... | collective-permute-start | bytes 245768 | tf_op jit(solution)/shard_map/ppermute | solution.py:330
  387.7 19.7 %collective-permute-start.19 = (bf16[80,512]{1,0:T(8,128)(2,1)S(1)}, bf16[80,512]{1,0:T(8,128)(2,1)S(1)}, u32[]{:S(2)}, u32[]{:S(2)}) collective-permute-start(bf16[80,512]{1,0:T(8,128)(2,1)S(1)} %broadcast_select_fusion.41), channel_id=1, source_target_pairs={{0,4},{2,6},{4,0},{6,2},{8,12},{10,14},{12,8},{14,10},{16,20},{18,... | collective-permute-start | bytes 245768 | tf_op jit(solution)/shard_map/ppermute | solution.py:330
  405.6 13.7 %collective-permute-start.11 = (bf16[80,512]{1,0:T(8,128)(2,1)S(1)}, bf16[80,512]{1,0:T(8,128)(2,1)S(1)}, u32[]{:S(2)}, u32[]{:S(2)}) collective-permute-start(bf16[80,512]{1,0:T(8,128)(2,1)S(1)} %broadcast_select_fusion.47), channel_id=1, source_target_pairs={{0,16},{2,18},{4,20},{6,22},{8,24},{10,26},{12,28},{14,30},{16,0},... | collective-permute-start | bytes 245768 | tf_op jit(solution)/shard_map/ppermute | solution.py:330
  405.8 13.7 %collective-permute-start.36 = (bf16[80,512]{1,0:T(8,128)(2,1)S(1)}, bf16[80,512]{1,0:T(8,128)(2,1)S(1)}, u32[]{:S(2)}, u32[]{:S(2)}) collective-permute-start(bf16[80,512]{1,0:T(8,128)(2,1)S(1)} %add_convert_fusion.13), channel_id=1, source_target_pairs={{0,4},{2,6},{4,0},{6,2},{8,12},{10,14},{12,8},{14,10},{16,20},{18,... | collective-permute-start | bytes 245768 | tf_op jit(solution)/shard_map/ppermute | solution.py:330
  407.5 15.0 %collective-permute-start.20 = (bf16[80,512]{1,0:T(8,128)(2,1)S(1)}, bf16[80,512]{1,0:T(8,128)(2,1)S(1)}, u32[]{:S(2)}, u32[]{:S(2)}) collective-permute-start(bf16[80,512]{1,0:T(8,128)(2,1)S(1)} %add_convert_fusion.15), channel_id=1, source_target_pairs={{0,4},{2,6},{4,0},{6,2},{8,12},{10,14},{12,8},{14,10},{16,20},{18,... | collective-permute-start | bytes 245768 | tf_op jit(solution)/shard_map/ppermute | solution.py:330
  410.7 22.6 %collective-permute-start.28 = (bf16[80,512]{1,0:T(8,128)(2,1)S(1)}, bf16[80,512]{1,0:T(8,128)(2,1)S(1)}, u32[]{:S(2)}, u32[]{:S(2)}) collective-permute-start(bf16[80,512]{1,0:T(8,128)(2,1)S(1)} %add_convert_fusion.14), channel_id=1, source_target_pairs={{0,16},{2,18},{4,20},{6,22},{8,24},{10,26},{12,28},{14,30},{16,0},... | collective-permute-start | bytes 245768 | tf_op jit(solution)/shard_map/ppermute | solution.py:330
  419.4 19.2 %collective-permute-start.12 = (bf16[80,512]{1,0:T(8,128)(2,1)S(1)}, bf16[80,512]{1,0:T(8,128)(2,1)S(1)}, u32[]{:S(2)}, u32[]{:S(2)}) collective-permute-start(bf16[80,512]{1,0:T(8,128)(2,1)S(1)} %add_convert_fusion.16), channel_id=1, source_target_pairs={{0,16},{2,18},{4,20},{6,22},{8,24},{10,26},{12,28},{14,30},{16,0},... | collective-permute-start | bytes 245768 | tf_op jit(solution)/shard_map/ppermute | solution.py:330
  419.5 23.2 %collective-permute-start.37 = (bf16[160,512]{1,0:T(8,128)(2,1)S(1)}, bf16[160,512]{1,0:T(8,128)(2,1)S(1)}, u32[]{:S(2)}, u32[]{:S(2)}) collective-permute-start(bf16[160,512]{1,0:T(8,128)(2,1)S(1)} %pad_maximum_fusion.21), channel_id=1, source_target_pairs={{0,16},{2,18},{4,20},{6,22},{8,24},{10,26},{12,28},{14,30},{16,0},... | collective-permute-start | bytes 491528 | tf_op jit(solution)/shard_map/ppermute | solution.py:330
  422.5 22.9 %collective-permute-start.21 = (bf16[160,512]{1,0:T(8,128)(2,1)S(1)}, bf16[160,512]{1,0:T(8,128)(2,1)S(1)}, u32[]{:S(2)}, u32[]{:S(2)}) collective-permute-start(bf16[160,512]{1,0:T(8,128)(2,1)S(1)} %pad_maximum_fusion.19), channel_id=1, source_target_pairs={{0,16},{2,18},{4,20},{6,22},{8,24},{10,26},{12,28},{14,30},{16,0},... | collective-permute-start | bytes 491528 | tf_op jit(solution)/shard_map/ppermute | solution.py:330
  433.4 15.1 %collective-permute-start.29 = (bf16[160,512]{1,0:T(8,128)(2,1)S(1)}, bf16[160,512]{1,0:T(8,128)(2,1)S(1)}, u32[]{:S(2)}, u32[]{:S(2)}) collective-permute-start(bf16[160,512]{1,0:T(8,128)(2,1)S(1)} %pad_maximum_fusion.20), channel_id=1, source_target_pairs={{0,8},{2,10},{4,12},{6,14},{8,0},{10,2},{12,4},{14,6},{16,24},{18,... | collective-permute-start | bytes 491528 | tf_op jit(solution)/shard_map/ppermute | solution.py:330
  438.6 13.3 %collective-permute-start.13 = (bf16[160,512]{1,0:T(8,128)(2,1)S(1)}, bf16[160,512]{1,0:T(8,128)(2,1)S(1)}, u32[]{:S(2)}, u32[]{:S(2)}) collective-permute-start(bf16[160,512]{1,0:T(8,128)(2,1)S(1)} %pad_maximum_fusion.18), channel_id=1, source_target_pairs={{0,8},{2,10},{4,12},{6,14},{8,0},{10,2},{12,4},{14,6},{16,24},{18,... | collective-permute-start | bytes 491528 | tf_op jit(solution)/shard_map/ppermute | solution.py:330
  442.8 16.1 %collective-permute-start.38 = (bf16[320,512]{1,0:T(8,128)(2,1)S(1)}, bf16[320,512]{1,0:T(8,128)(2,1)S(1)}, u32[]{:S(2)}, u32[]{:S(2)}) collective-permute-start(bf16[320,512]{1,0:T(8,128)(2,1)S(1)} %pad_maximum_fusion.17), channel_id=1, source_target_pairs={{0,8},{2,10},{4,12},{6,14},{8,0},{10,2},{12,4},{14,6},{16,24},{18,... | collective-permute-start | bytes 983048 | tf_op jit(solution)/shard_map/ppermute | solution.py:330
  445.5 18.4 %collective-permute-start.22 = (bf16[320,512]{1,0:T(8,128)(2,1)S(1)}, bf16[320,512]{1,0:T(8,128)(2,1)S(1)}, u32[]{:S(2)}, u32[]{:S(2)}) collective-permute-start(bf16[320,512]{1,0:T(8,128)(2,1)S(1)} %pad_maximum_fusion.15), channel_id=1, source_target_pairs={{0,8},{2,10},{4,12},{6,14},{8,0},{10,2},{12,4},{14,6},{16,24},{18,... | collective-permute-start | bytes 983048 | tf_op jit(solution)/shard_map/ppermute | solution.py:330
  448.5 15.8 %collective-permute-start.30 = (bf16[320,512]{1,0:T(8,128)(2,1)S(1)}, bf16[320,512]{1,0:T(8,128)(2,1)S(1)}, u32[]{:S(2)}, u32[]{:S(2)}) collective-permute-start(bf16[320,512]{1,0:T(8,128)(2,1)S(1)} %pad_maximum_fusion.16), channel_id=1, source_target_pairs={{0,4},{2,6},{4,0},{6,2},{8,12},{10,14},{12,8},{14,10},{16,20},{18,... | collective-permute-start | bytes 983048 | tf_op jit(solution)/shard_map/ppermute | solution.py:330
  (46 other events, 776.6 us)
Sparse Core Ops, SparseCore 0:
  191.9 104.1 reduce-scatter.1
  329.6 112.2 all-gather.1

commit v3 on v2

--- a/solution.py
+++ b/solution.py
@@ -323,7 +323,7 @@
     return scale * (scaled - first - unit * second)
 
 
-def exchange_sum(parts, bits, size):
+def exchange_sum(parts, bits, size, beside):
     place = lax.axis_index("dp")
 
     def swap(array, bit):
@@ -345,13 +345,15 @@
     for step in range(len(bits)):
         arrays = [fold(a, order[step]) for a, (_, order) in zip(arrays, parts)]
     for step in reversed(range(len(bits))):
+        if step == 0:
+            arrays, beside = lax.optimization_barrier((arrays, beside))
         arrays = [unfold(a, order[step]) for a, (_, order) in zip(arrays, parts)]
-    return arrays
-
-
-def sum_over_documents(table, size):
+    return arrays, beside
+
+
+def sum_over_documents(table, size, beside):
     if size != 16:
-        return lax.psum(table, "dp")
+        return lax.psum(table, "dp"), beside
     rows = table.shape[0]
     grain = 256
     pieces = 4
@@ -359,7 +361,8 @@
     padded = jnp.pad(table, ((0, pieces * step - rows), (0, 0)))
     orders = ((1, 2, 4, 8), (1, 4, 8, 2))
     parts = [(padded[i * step:(i + 1) * step], orders[i % 2]) for i in range(pieces)]
-    return jnp.concatenate(exchange_sum(parts, orders[0], size), axis=0)[:rows]
+    arrays, beside = exchange_sum(parts, orders[0], size, beside)
+    return jnp.concatenate(arrays, axis=0)[:rows], beside
 
 
 def on_device(
@@ -417,10 +420,12 @@
     weight_qkv = w_qkv.reshape(model_width, 3 * width)
     projected = jnp.dot(rows, weight_qkv, preferred_element_type=F32).astype(BF16)
     norms = join(jnp.concatenate([norm_gains, norm_shifts], axis=0), 1)
-    upstream = join(out_grad.reshape(row_count, width), 1)
+    rows, out_rows = lax.optimization_barrier((rows, out_grad.reshape(row_count, width)))
+    upstream = join(out_rows, 1)
     out_whole = join(w_out, 0)
     projected = projected.reshape(doc_count, slot_count, 3 * width)
     context, probs = attend_forward(lengths, projected, rel_k, rel_q, boxes_col, boxes_row, heads_here)
+    context, upstream, norms, out_whole = lax.optimization_barrier((context, upstream, norms, out_whole))
     context = context.reshape(row_count, width)
 
     attn = jnp.dot(join(context, 1), out_whole, preferred_element_type=F32)
@@ -436,20 +441,12 @@
 
     upstream = upstream.astype(F32)
     grad_second = norm_pull(upstream, unit_second, scale_second, norms[1:2])
-    ffn_grad = grad_second.astype(BF16)
+    grad_second, ffn_grad = lax.optimization_barrier((grad_second, grad_second.astype(BF16)))
     grad_upper = (dot_nt(ffn_grad, w_down) * slope.astype(F32)).astype(BF16)
     hidden_part = dot_nt(grad_upper, w_up).astype(BF16)
-    units = w_up.shape[1]
     down_grad = dot_tn(active, ffn_grad).astype(BF16)
-    early = documents == 16 and units % model_width == 0
-    if early:
-        ffn_table = jnp.concatenate([down_grad] + [
-            dot_tn(h1_low, grad_upper[:, t:t + model_width]).astype(BF16)
-            for t in range(0, units, model_width)], axis=0)
-        ffn_shard = lax.psum_scatter(ffn_table, "dp", scatter_dimension=0, tiled=True)
-    else:
-        up_grad = dot_tn(h1_low, grad_upper).astype(BF16)
-        down_grad, up_grad = lax.psum((down_grad, up_grad), "dp")
+    up_grad = dot_tn(h1_low, grad_upper).astype(BF16)
+    ffn_sums = lax.psum((down_grad, up_grad), "dp")
     grad_hidden = grad_second + total(hidden_part)
     grad_first = norm_pull(grad_hidden, unit_first, scale_first, norms[0:1])
     attn_grad = grad_first.astype(BF16)
@@ -464,12 +461,6 @@
     grad_projected, rel_k_sum, rel_q_sum = attend_backward(
         projected, grad_context, probs, rel_k, rel_q, boxes_col, boxes_row, heads_here
     )
-    if early:
-        grad_projected, ffn_shard = lax.optimization_barrier((grad_projected, ffn_shard))
-        ffn_table = lax.all_gather(ffn_shard, "dp", axis=0, tiled=True)
-        down_grad = ffn_table[:units]
-        up_grad = jnp.concatenate([
-            ffn_table[units + t:units + t + model_width] for t in range(0, units, model_width)], axis=1)
     grad_rows = grad_projected.reshape(row_count, 3 * width)
     input_part = dot_nt(grad_rows, weight_qkv).astype(BF16)
     input_grad = own(grad_first) + own_total(input_part)
@@ -478,7 +469,8 @@
     pieces = qkv_grads + [jnp.sum(rel_k_sum, axis=0), jnp.sum(rel_q_sum, axis=0)]
     pieces += [out_weight_grad[:, t * width:(t + 1) * width] for t in range(shards)]
     pieces += [norm_grads]
-    table = sum_over_documents(jnp.concatenate([p.astype(BF16) for p in pieces], axis=0), documents)
+    table, (down_grad, up_grad) = sum_over_documents(
+        jnp.concatenate([p.astype(BF16) for p in pieces], axis=0), documents, ffn_sums)
     table = table.astype(F32)
     found = []
     at = 0

time: 503 us -> 460 us (0.915)
  waiting for transfers between devices: 176 us -> 147 us
  starting transfers between devices: 47.5 us -> 36 us
    ppermute x5, waiting for transfers between devices: 51.1 us -> 17.5 us  [join(): other = lax.ppermute(array, 'tensor', pair)]
    ppermute x2, waiting for transfers between devices: 22.3 us -> 35.7 us  [total(): lax.ppermute(partial, 'tensor', pair).astype(F32)]
    all_gather x1 -> x0, starting transfers between devices: 11.7 us -> none  [on_device(): ffn_table = lax.all_gather(ffn_shard, 'dp', axis=0, tiled=True)]
    ppermute x32, waiting for transfers between devices: 103 us -> 94 us  [swap(): return lax.ppermute(array, 'dp', [(i, i ^ bit) for i in range(size)])]
    dot_general x4, matrix products: 18.4 us -> 10.5 us  [dot_nt(): lax.dot_general(a, b, (((1,), (1,)), ((), ())), preferred_element_type=F32)]
    unnamed x76 -> x64, local copies, waits for them, and re-layouts: 7.82 us -> 10.7 us
    dot_general x7 -> x6, matrix products: 14.1 us -> 16.1 us  [dot_tn(): lax.dot_general(a, b, (((0,), (0,)), ((), ())), preferred_element_type=F32)]
  transfers between devices with their start and end apart: 42 -> 41, of which waited for: 22 -> 17; matrix products, arithmetic and copies ran while one was open for 11% -> 14% of each run, Pallas kernels for 31% -> 34%
where the time goes in v3:
time: 460 us; the launch traced here: 452 us
  Pallas kernels  152 us (33%)
  waiting for transfers between devices  147 us (32%)
  other arithmetic  43.7 us (10%)
  matrix products  40.2 us (9%)
  starting transfers between devices  36 us (8%)
  local copies, waits for them, and re-layouts  16.6 us (4%)
  between operations  15.9 us (3%)
    ppermute x32, waiting for transfers between devices, swap(): return lax.ppermute(array, 'dp', [(i, i ^ bit) for i in range(size)])  94 us
    pallas_call x1, Pallas kernels, attend_forward(): pl.pallas_call(functools.partial(fwd_kernel, slots, sp), out_shape=[jax.S...  82.5 us
    pallas_call x1, Pallas kernels, attend_backward(): pl.pallas_call(functools.partial(bwd_kernel, slots, sp, width), grid=(doc...  69.8 us
    ppermute x2, waiting for transfers between devices, total(): lax.ppermute(partial, 'tensor', pair).astype(F32)  35.7 us
    ppermute x32, starting transfers between devices, swap(): return lax.ppermute(array, 'dp', [(i, i ^ bit) for i in range(size)])  25.3 us
    ppermute x5, waiting for transfers between devices, join(): other = lax.ppermute(array, 'tensor', pair)  17.5 us
    dot_general x6, matrix products, dot_tn(): lax.dot_general(a, b, (((0,), (0,)), ((), ())), preferred_element_type=F32)  16.1 us
    unnamed x64, local copies, waits for them, and re-layouts  10.7 us
  transfers between devices with their start and end apart: 41, of which 17 were waited for; matrix products, arithmetic and copies ran while one was open for 14% of the time, Pallas kernels for 34%

profile of v3, /device:TPU:0, one launch (start us, length us, event | category | flops | bytes accessed | tf_op | source)
XLA Modules:
  0.0 451.9 jit_solution(12065987277465103347)
XLA Ops:
  7.2 3.1 collective-permute-start
  16.6 3.2 copy.24
  19.8 4.8 %collective-permute-done.2 = f32[4,512]{1,0:T(4,128)S(1)} collective-permute-done((f32[4,512]{1,0:T(4,128)S(1)}, f32[4,512]{1,0:T(4,128)S(1)}, u32[]{:S(2)}, u32[]{:S(2)}) %collective-permute-start.2) | collective-permute-done | bytes 8224 | tf_op jit(solution)/shard_map/ppermute | solution.py:394
  28.4 3.2 fusion.8.q_ref.k_ref.v_ref
  31.6 82.5 %attend_forward.1 = (bf16[1,561,512]{2,1,0:T(8,128)(2,1)}, bf16[1,8,640,640]{3,2,1,0:T(8,128)(2,1)}) custom-call(s32[1]{0:T(128)S(6)} %copy.44.len_ref, bf16[1,561,1536]{2,1,0:T(8,128)(2,1)} %fusion.8.q_ref.k_ref.v_ref, bf16[1,561,1536]{2,1,0:T(8,128)(2,1)} %fusion.8.q_ref.k_ref.v_ref, bf16[1,561,1536]{2,1,0:T(8,128)(2,1)} %fusion.8.q_ref.k_ref.v_ref, ...), custom_call_target="tpu_custom_call" | custom-call | tf_op jit(solution)/shard_map/attend_forward/pallas_call | solution.py:131
  116.8 12.7 %collective-permute-done.4 = bf16[561,512]{1,0:T(8,128)(2,1)S(1)} collective-permute-done((bf16[561,512]{1,0:T(8,128)(2,1)S(1)}, bf16[561,512]{1,0:T(8,128)(2,1)S(1)}, u32[]{:S(2)}, u32[]{:S(2)}) %collective-permute-start.4) | collective-permute-done | bytes 574496 | tf_op jit(solution)/shard_map/ppermute | solution.py:394
  131.7 5.1 %multiply_convert_fusion.1 = (bf16[561,2048]{1,0:T(8,128)(2,1)S(1)}, f32[561,2048]{1,0:T(8,128)}) fusion(bf16[1024,2048]{1,0:T(8,128)(2,1)S(1)} %copy-done.23, f32[561,1024]{1,0:T(8,128)S(1)} %get-tuple-element.132, f32[1024]{0:T(1024)S(1)} %bitcast.88, f32[1024]{0:T(1024)S(1)} %bitcast.76, f32[561]{0:T(1024)S(1)} %get-tuple-element.131, ...), kind=kOutput, calls=%fused_computation.10 | convolution fusion | flops 2361621504 | bytes 13398408 | tf_op jit(solution)/shard_map/dot_general | solution.py:434
  136.8 3.7 convolution_convert_fusion.4
  141.1 24.1 %collective-permute-done.5 = bf16[561,1024]{1,0:T(8,128)(2,1)} collective-permute-done((bf16[561,1024]{1,0:T(8,128)(2,1)}, bf16[561,1024]{1,0:T(8,128)(2,1)}, u32[]{:S(2)}, u32[]{:S(2)}) %collective-permute-start.5) | collective-permute-done | bytes 1148960 | tf_op jit(solution)/shard_map/ppermute | solution.py:402
  165.2 2.8 fusion.37
  173.1 4.3 multiply_convert_fusion
  181.2 5.0 %convolution_convert_fusion.1 = bf16[2048,1024]{1,0:T(8,128)(2,1)} fusion(bf16[561,2048]{1,0:T(8,128)(2,1)S(1)} %copy-done.27, bf16[561,1024]{1,0:T(8,128)(2,1)S(1)} %get-tuple-element.37), kind=kOutput, calls=%fused_computation.13 | convolution fusion | flops 2355101696 | bytes 7641088 | tf_op jit(solution)/shard_map/dot_general | solution.py:309
  186.2 5.8 %convolution_convert_fusion = bf16[1024,2048]{1,0:T(8,128)(2,1)} fusion(bf16[561,2048]{1,0:T(8,128)(2,1)S(1)} %multiply_convert_fusion, f32[561,1024]{1,0:T(8,128)S(1)} %get-tuple-element.132, f32[1024]{0:T(1024)S(1)} %bitcast.90, f32[1024]{0:T(1024)S(1)} %bitcast.78, f32[561]{0:T(1024)S(1)} %get-tuple-element.131, f32[561]{0:T(1024)S(1)} %get-tuple-element.130), kind=kOutput, calls=%fused_computation.12 | convolution fusion | flops 2357974016 | bytes 8802696 | tf_op jit(solution)/shard_map/dot_general | solution.py:309
  192.1 11.6 %collective-permute-done.6 = bf16[561,1024]{1,0:T(8,128)(2,1)} collective-permute-done((bf16[561,1024]{1,0:T(8,128)(2,1)S(1)}, bf16[561,1024]{1,0:T(8,128)(2,1)}, u32[]{:S(2)}, u32[]{:S(2)}) %collective-permute-start.6) | collective-permute-done | bytes 1148960 | tf_op jit(solution)/shard_map/ppermute | solution.py:402
  203.7 3.4 multiply_reduce_fusion
  211.8 69.8 %attend_backward.1 = (bf16[1,561,1536]{2,1,0:T(8,128)(2,1)}, f32[1,384,512]{2,1,0:T(8,128)}, f32[1,384,512]{2,1,0:T(8,128)}) custom-call(bf16[1,561,1536]{2,1,0:T(8,128)(2,1)} %fusion.8.q_ref.k_ref.v_ref, bf16[1,561,1536]{2,1,0:T(8,128)(2,1)} %fusion.8.q_ref.k_ref.v_ref, bf16[1,561,1536]{2,1,0:T(8,128)(2,1)} %fusion.8.q_ref.k_ref.v_ref, ...), custom_call_target="tpu_custom_call" | custom-call | tf_op jit(solution)/shard_map/attend_backward/pallas_call | solution.py:278
  299.6 8.4 %collective-permute-done.30 = bf16[320,512]{1,0:T(8,128)(2,1)S(1)} collective-permute-done((bf16[320,512]{1,0:T(8,128)(2,1)S(1)}, bf16[320,512]{1,0:T(8,128)(2,1)S(1)}, u32[]{:S(2)}, u32[]{:S(2)}) %collective-permute-start.30) | collective-permute-done | bytes 327712 | tf_op jit(solution)/shard_map/ppermute | solution.py:330
  310.4 11.3 %collective-permute-done.16 = bf16[320,512]{1,0:T(8,128)(2,1)S(1)} collective-permute-done((bf16[320,512]{1,0:T(8,128)(2,1)S(1)}, bf16[320,512]{1,0:T(8,128)(2,1)S(1)}, u32[]{:S(2)}, u32[]{:S(2)}) %collective-permute-start.16) | collective-permute-done | bytes 327712 | tf_op jit(solution)/shard_map/ppermute | solution.py:330
  325.5 10.5 %collective-permute-done.17 = bf16[160,512]{1,0:T(8,128)(2,1)S(1)} collective-permute-done((bf16[160,512]{1,0:T(8,128)(2,1)S(1)}, bf16[160,512]{1,0:T(8,128)(2,1)S(1)}, u32[]{:S(2)}, u32[]{:S(2)}) %collective-permute-start.17) | collective-permute-done | bytes 163872 | tf_op jit(solution)/shard_map/ppermute | solution.py:330
  337.1 3.0 collective-permute-start.25
  340.1 4.9 %collective-permute-done.10 = bf16[160,512]{1,0:T(8,128)(2,1)S(1)} collective-permute-done((bf16[160,512]{1,0:T(8,128)(2,1)S(1)}, bf16[160,512]{1,0:T(8,128)(2,1)S(1)}, u32[]{:S(2)}, u32[]{:S(2)}) %collective-permute-start.10) | collective-permute-done | bytes 163872 | tf_op jit(solution)/shard_map/ppermute | solution.py:330
  350.9 5.2 %collective-permute-done.11 = bf16[80,512]{1,0:T(8,128)(2,1)S(1)} collective-permute-done((bf16[80,512]{1,0:T(8,128)(2,1)S(1)}, bf16[80,512]{1,0:T(8,128)(2,1)S(1)}, u32[]{:S(2)}, u32[]{:S(2)}) %collective-permute-start.11) | collective-permute-done | bytes 81952 | tf_op jit(solution)/shard_map/ppermute | solution.py:330
  356.3 3.0 collective-permute-start.34
  359.4 3.1 collective-permute-done.26
  362.7 6.9 %collective-permute-done.12 = bf16[80,512]{1,0:T(8,128)(2,1)S(1)} collective-permute-done((bf16[80,512]{1,0:T(8,128)(2,1)S(1)}, bf16[80,512]{1,0:T(8,128)(2,1)S(1)}, u32[]{:S(2)}, u32[]{:S(2)}) %collective-permute-start.12) | collective-permute-done | bytes 81952 | tf_op jit(solution)/shard_map/ppermute | solution.py:330
  369.7 9.8 %collective-permute-done.34 = bf16[160,512]{1,0:T(8,128)(2,1)S(1)} collective-permute-done((bf16[160,512]{1,0:T(8,128)(2,1)S(1)}, bf16[160,512]{1,0:T(8,128)(2,1)S(1)}, u32[]{:S(2)}, u32[]{:S(2)}) %collective-permute-start.34) | collective-permute-done | bytes 163872 | tf_op jit(solution)/shard_map/ppermute | solution.py:330
  379.6 6.6 %collective-permute-done.20 = bf16[160,512]{1,0:T(8,128)(2,1)S(1)} collective-permute-done((bf16[160,512]{1,0:T(8,128)(2,1)S(1)}, bf16[160,512]{1,0:T(8,128)(2,1)S(1)}, u32[]{:S(2)}, u32[]{:S(2)}) %collective-permute-start.20) | collective-permute-done | bytes 163872 | tf_op jit(solution)/shard_map/ppermute | solution.py:330
  389.4 13.6 %collective-permute-done.35 = bf16[320,512]{1,0:T(8,128)(2,1)S(1)} collective-permute-done((bf16[320,512]{1,0:T(8,128)(2,1)S(1)}, bf16[320,512]{1,0:T(8,128)(2,1)S(1)}, u32[]{:S(2)}, u32[]{:S(2)}) %collective-permute-start.35) | collective-permute-done | bytes 327712 | tf_op jit(solution)/shard_map/ppermute | solution.py:330
  403.1 11.2 %collective-permute-done.21 = bf16[320,512]{1,0:T(8,128)(2,1)S(1)} collective-permute-done((bf16[320,512]{1,0:T(8,128)(2,1)S(1)}, bf16[320,512]{1,0:T(8,128)(2,1)S(1)}, u32[]{:S(2)}, u32[]{:S(2)}) %collective-permute-start.21) | collective-permute-done | bytes 327712 | tf_op jit(solution)/shard_map/ppermute | solution.py:330
  422.1 7.0 %convert_element_type.334 = f32[1024,2048]{1,0:T(8,128)} convert(bf16[1024,2048]{1,0:T(8,128)(2,1)} %get-tuple-element.46) | non-fusion elementwise | flops 2097152 | bytes 12582912 | tf_op jit(solution)/shard_map/convert_element_type | solution.py:490
  429.2 4.4 convert_element_type.335
  441.4 3.4 pad_maximum_fusion
  (234 shorter events, 78.5 us)
Async XLA Ops:
  7.2 410.2 %all-reduce.5.cloned.1.call-start = ((), (), s32[]{:S(2)}) async-start(), calls=%async_computation | async-start | bytes 16777216 | tf_op jit(solution)/shard_map/psum | solution.py:449
  7.2 17.5 %collective-permute-start = (bf16[561,512]{1,0:T(8,128)(2,1)}, bf16[561,512]{1,0:T(8,128)(2,1)}, u32[]{:S(2)}, u32[]{:S(2)}) collective-permute-start(bf16[561,512]{1,0:T(8,128)(2,1)} %bitcast.72), channel_id=1, source_target_pairs={{0,1},{1,0},{2,3},{3,2},{4,5},{5,4},{6,7},{7,6},{8,9},{9,8},{10,11... | collective-permute-start | bytes 1723400 | tf_op jit(solution)/shard_map/ppermute | solution.py:394
  11.0 13.7 %collective-permute-start.2 = (f32[4,512]{1,0:T(4,128)S(1)}, f32[4,512]{1,0:T(4,128)S(1)}, u32[]{:S(2)}, u32[]{:S(2)}) collective-permute-start(f32[4,512]{1,0:T(4,128)S(1)} %pad_maximum_fusion.23), channel_id=1, source_target_pairs={{0,1},{1,0},{2,3},{3,2},{4,5},{5,4},{6,7},{7,6},{8,9},{9,8},{10,11... | collective-permute-start | bytes 24584 | tf_op jit(solution)/shard_map/ppermute | solution.py:394
  11.1 103.0 %collective-permute-start.3 = (bf16[512,1024]{1,0:T(8,128)(2,1)}, bf16[512,1024]{1,0:T(8,128)(2,1)}, u32[]{:S(2)}, u32[]{:S(2)}) collective-permute-start(bf16[512,1024]{1,0:T(8,128)(2,1)} %param.16), channel_id=1, source_target_pairs={{0,1},{1,0},{2,3},{3,2},{4,5},{5,4},{6,7},{7,6},{8,9},{9,8},{10,11... | collective-permute-start | bytes 3145736 | tf_op jit(solution)/shard_map/ppermute | solution.py:394
  26.3 89.4 %collective-permute-start.1 = (bf16[561,512]{1,0:T(8,128)(2,1)S(1)}, bf16[561,512]{1,0:T(8,128)(2,1)S(1)}, u32[]{:S(2)}, u32[]{:S(2)}) collective-permute-start(bf16[561,512]{1,0:T(8,128)(2,1)S(1)} %bitcast.73), channel_id=1, source_target_pairs={{0,1},{1,0},{2,3},{3,2},{4,5},{5,4},{6,7},{7,6},{8,9},{9,8},{10,11... | collective-permute-start | bytes 1723400 | tf_op jit(solution)/shard_map/ppermute | solution.py:394
  116.7 12.7 %collective-permute-start.4 = (bf16[561,512]{1,0:T(8,128)(2,1)S(1)}, bf16[561,512]{1,0:T(8,128)(2,1)S(1)}, u32[]{:S(2)}, u32[]{:S(2)}) collective-permute-start(bf16[561,512]{1,0:T(8,128)(2,1)S(1)} %bitcast.75), channel_id=1, source_target_pairs={{0,1},{1,0},{2,3},{3,2},{4,5},{5,4},{6,7},{7,6},{8,9},{9,8},{10,11... | collective-permute-start | bytes 1723400 | tf_op jit(solution)/shard_map/ppermute | solution.py:394
  140.5 24.7 %collective-permute-start.5 = (bf16[561,1024]{1,0:T(8,128)(2,1)}, bf16[561,1024]{1,0:T(8,128)(2,1)}, u32[]{:S(2)}, u32[]{:S(2)}) collective-permute-start(bf16[561,1024]{1,0:T(8,128)(2,1)} %convolution_convert_fusion.4), channel_id=1, source_target_pairs={{0,1},{1,0},{2,3},{3,2},{4,5},{5,4},{6,7},{7,6},{8,9},{9,8},{10,11... | collective-permute-start | bytes 3446792 | tf_op jit(solution)/shard_map/ppermute | solution.py:402
  180.0 23.7 %collective-permute-start.6 = (bf16[561,1024]{1,0:T(8,128)(2,1)S(1)}, bf16[561,1024]{1,0:T(8,128)(2,1)}, u32[]{:S(2)}, u32[]{:S(2)}) collective-permute-start(bf16[561,1024]{1,0:T(8,128)(2,1)S(1)} %convolution_convert_fusion.3), channel_id=1, source_target_pairs={{0,1},{1,0},{2,3},{3,2},{4,5},{5,4},{6,7},{7,6},{8,9},{9,8},{10,11... | collective-permute-start | bytes 3446792 | tf_op jit(solution)/shard_map/ppermute | solution.py:402
  291.9 127.1 %collective-permute-start.7 = (bf16[561,512]{1,0:T(8,128)(2,1)}, bf16[561,512]{1,0:T(8,128)(2,1)}, u32[]{:S(2)}, u32[]{:S(2)}) collective-permute-start(bf16[561,512]{1,0:T(8,128)(2,1)} %constant_dynamic-slice_fusion), channel_id=1, source_target_pairs={{0,1},{1,0},{2,3},{3,2},{4,5},{5,4},{6,7},{7,6},{8,9},{9,8},{10,11... | collective-permute-start | bytes 1723400 | tf_op jit(solution)/shard_map/ppermute | solution.py:411
  294.3 13.6 %collective-permute-start.30 = (bf16[320,512]{1,0:T(8,128)(2,1)S(1)}, bf16[320,512]{1,0:T(8,128)(2,1)S(1)}, u32[]{:S(2)}, u32[]{:S(2)}) collective-permute-start(bf16[320,512]{1,0:T(8,128)(2,1)S(1)} %broadcast_select_fusion.14), channel_id=1, source_target_pairs={{0,8},{2,10},{4,12},{6,14},{8,0},{10,2},{12,4},{14,6},{16,24},{18,... | collective-permute-start | bytes 983048 | tf_op jit(solution)/shard_map/ppermute | solution.py:330
  295.1 26.6 %collective-permute-start.16 = (bf16[320,512]{1,0:T(8,128)(2,1)S(1)}, bf16[320,512]{1,0:T(8,128)(2,1)S(1)}, u32[]{:S(2)}, u32[]{:S(2)}) collective-permute-start(bf16[320,512]{1,0:T(8,128)(2,1)S(1)} %broadcast_select_fusion.17), channel_id=1, source_target_pairs={{0,8},{2,10},{4,12},{6,14},{8,0},{10,2},{12,4},{14,6},{16,24},{18,... | collective-permute-start | bytes 983048 | tf_op jit(solution)/shard_map/ppermute | solution.py:330
  297.1 24.8 %collective-permute-start.23 = (bf16[320,512]{1,0:T(8,128)(2,1)S(1)}, bf16[320,512]{1,0:T(8,128)(2,1)S(1)}, u32[]{:S(2)}, u32[]{:S(2)}) collective-permute-start(bf16[320,512]{1,0:T(8,128)(2,1)S(1)} %broadcast_select_fusion.20), channel_id=1, source_target_pairs={{0,4},{2,6},{4,0},{6,2},{8,12},{10,14},{12,8},{14,10},{16,20},{18,... | collective-permute-start | bytes 983048 | tf_op jit(solution)/shard_map/ppermute | solution.py:330
  298.0 26.6 %collective-permute-start.9 = (bf16[320,512]{1,0:T(8,128)(2,1)S(1)}, bf16[320,512]{1,0:T(8,128)(2,1)S(1)}, u32[]{:S(2)}, u32[]{:S(2)}) collective-permute-start(bf16[320,512]{1,0:T(8,128)(2,1)S(1)} %broadcast_select_fusion.23), channel_id=1, source_target_pairs={{0,4},{2,6},{4,0},{6,2},{8,12},{10,14},{12,8},{14,10},{16,20},{18,... | collective-permute-start | bytes 983048 | tf_op jit(solution)/shard_map/ppermute | solution.py:330
  308.1 16.7 %collective-permute-start.31 = (bf16[160,512]{1,0:T(8,128)(2,1)S(1)}, bf16[160,512]{1,0:T(8,128)(2,1)S(1)}, u32[]{:S(2)}, u32[]{:S(2)}) collective-permute-start(bf16[160,512]{1,0:T(8,128)(2,1)S(1)} %broadcast_select_fusion.26), channel_id=1, source_target_pairs={{0,16},{2,18},{4,20},{6,22},{8,24},{10,26},{12,28},{14,30},{16,0},... | collective-permute-start | bytes 491528 | tf_op jit(solution)/shard_map/ppermute | solution.py:330
  321.9 14.2 %collective-permute-start.17 = (bf16[160,512]{1,0:T(8,128)(2,1)S(1)}, bf16[160,512]{1,0:T(8,128)(2,1)S(1)}, u32[]{:S(2)}, u32[]{:S(2)}) collective-permute-start(bf16[160,512]{1,0:T(8,128)(2,1)S(1)} %broadcast_select_fusion.29), channel_id=1, source_target_pairs={{0,16},{2,18},{4,20},{6,22},{8,24},{10,26},{12,28},{14,30},{16,0},... | collective-permute-start | bytes 491528 | tf_op jit(solution)/shard_map/ppermute | solution.py:330
  322.1 14.9 %collective-permute-start.24 = (bf16[160,512]{1,0:T(8,128)(2,1)S(1)}, bf16[160,512]{1,0:T(8,128)(2,1)S(1)}, u32[]{:S(2)}, u32[]{:S(2)}) collective-permute-start(bf16[160,512]{1,0:T(8,128)(2,1)S(1)} %broadcast_select_fusion.32), channel_id=1, source_target_pairs={{0,8},{2,10},{4,12},{6,14},{8,0},{10,2},{12,4},{14,6},{16,24},{18,... | collective-permute-start | bytes 491528 | tf_op jit(solution)/shard_map/ppermute | solution.py:330
  324.7 20.3 %collective-permute-start.10 = (bf16[160,512]{1,0:T(8,128)(2,1)S(1)}, bf16[160,512]{1,0:T(8,128)(2,1)S(1)}, u32[]{:S(2)}, u32[]{:S(2)}) collective-permute-start(bf16[160,512]{1,0:T(8,128)(2,1)S(1)} %broadcast_select_fusion.35), channel_id=1, source_target_pairs={{0,8},{2,10},{4,12},{6,14},{8,0},{10,2},{12,4},{14,6},{16,24},{18,... | collective-permute-start | bytes 491528 | tf_op jit(solution)/shard_map/ppermute | solution.py:330
  324.9 22.3 %collective-permute-start.32 = (bf16[80,512]{1,0:T(8,128)(2,1)S(1)}, bf16[80,512]{1,0:T(8,128)(2,1)S(1)}, u32[]{:S(2)}, u32[]{:S(2)}) collective-permute-start(bf16[80,512]{1,0:T(8,128)(2,1)S(1)} %broadcast_select_fusion.38), channel_id=1, source_target_pairs={{0,4},{2,6},{4,0},{6,2},{8,12},{10,14},{12,8},{14,10},{16,20},{18,... | collective-permute-start | bytes 245768 | tf_op jit(solution)/shard_map/ppermute | solution.py:330
  349.4 13.1 %collective-permute-start.26 = (bf16[80,512]{1,0:T(8,128)(2,1)S(1)}, bf16[80,512]{1,0:T(8,128)(2,1)S(1)}, u32[]{:S(2)}, u32[]{:S(2)}) collective-permute-start(bf16[80,512]{1,0:T(8,128)(2,1)S(1)} %add_convert_fusion.14), channel_id=1, source_target_pairs={{0,16},{2,18},{4,20},{6,22},{8,24},{10,26},{12,28},{14,30},{16,0},... | collective-permute-start | bytes 245768 | tf_op jit(solution)/shard_map/ppermute | solution.py:330
  356.2 13.4 %collective-permute-start.12 = (bf16[80,512]{1,0:T(8,128)(2,1)S(1)}, bf16[80,512]{1,0:T(8,128)(2,1)S(1)}, u32[]{:S(2)}, u32[]{:S(2)}) collective-permute-start(bf16[80,512]{1,0:T(8,128)(2,1)S(1)} %add_convert_fusion.16), channel_id=1, source_target_pairs={{0,16},{2,18},{4,20},{6,22},{8,24},{10,26},{12,28},{14,30},{16,0},... | collective-permute-start | bytes 245768 | tf_op jit(solution)/shard_map/ppermute | solution.py:330
  356.3 23.2 %collective-permute-start.34 = (bf16[160,512]{1,0:T(8,128)(2,1)S(1)}, bf16[160,512]{1,0:T(8,128)(2,1)S(1)}, u32[]{:S(2)}, u32[]{:S(2)}) collective-permute-start(bf16[160,512]{1,0:T(8,128)(2,1)S(1)} %pad_maximum_fusion.21), channel_id=1, source_target_pairs={{0,16},{2,18},{4,20},{6,22},{8,24},{10,26},{12,28},{14,30},{16,0},... | collective-permute-start | bytes 491528 | tf_op jit(solution)/shard_map/ppermute | solution.py:330
  359.3 27.0 %collective-permute-start.20 = (bf16[160,512]{1,0:T(8,128)(2,1)S(1)}, bf16[160,512]{1,0:T(8,128)(2,1)S(1)}, u32[]{:S(2)}, u32[]{:S(2)}) collective-permute-start(bf16[160,512]{1,0:T(8,128)(2,1)S(1)} %pad_maximum_fusion.19), channel_id=1, source_target_pairs={{0,16},{2,18},{4,20},{6,22},{8,24},{10,26},{12,28},{14,30},{16,0},... | collective-permute-start | bytes 491528 | tf_op jit(solution)/shard_map/ppermute | solution.py:330
  362.6 23.9 %collective-permute-start.27 = (bf16[160,512]{1,0:T(8,128)(2,1)S(1)}, bf16[160,512]{1,0:T(8,128)(2,1)S(1)}, u32[]{:S(2)}, u32[]{:S(2)}) collective-permute-start(bf16[160,512]{1,0:T(8,128)(2,1)S(1)} %pad_maximum_fusion.20), channel_id=1, source_target_pairs={{0,8},{2,10},{4,12},{6,14},{8,0},{10,2},{12,4},{14,6},{16,24},{18,... | collective-permute-start | bytes 491528 | tf_op jit(solution)/shard_map/ppermute | solution.py:330
  369.6 19.3 %collective-permute-start.13 = (bf16[160,512]{1,0:T(8,128)(2,1)S(1)}, bf16[160,512]{1,0:T(8,128)(2,1)S(1)}, u32[]{:S(2)}, u32[]{:S(2)}) collective-permute-start(bf16[160,512]{1,0:T(8,128)(2,1)S(1)} %pad_maximum_fusion.18), channel_id=1, source_target_pairs={{0,8},{2,10},{4,12},{6,14},{8,0},{10,2},{12,4},{14,6},{16,24},{18,... | collective-permute-start | bytes 491528 | tf_op jit(solution)/shard_map/ppermute | solution.py:330
  379.6 23.4 %collective-permute-start.35 = (bf16[320,512]{1,0:T(8,128)(2,1)S(1)}, bf16[320,512]{1,0:T(8,128)(2,1)S(1)}, u32[]{:S(2)}, u32[]{:S(2)}) collective-permute-start(bf16[320,512]{1,0:T(8,128)(2,1)S(1)} %pad_maximum_fusion.17), channel_id=1, source_target_pairs={{0,8},{2,10},{4,12},{6,14},{8,0},{10,2},{12,4},{14,6},{16,24},{18,... | collective-permute-start | bytes 983048 | tf_op jit(solution)/shard_map/ppermute | solution.py:330
  386.4 28.0 %collective-permute-start.21 = (bf16[320,512]{1,0:T(8,128)(2,1)S(1)}, bf16[320,512]{1,0:T(8,128)(2,1)S(1)}, u32[]{:S(2)}, u32[]{:S(2)}) collective-permute-start(bf16[320,512]{1,0:T(8,128)(2,1)S(1)} %pad_maximum_fusion.15), channel_id=1, source_target_pairs={{0,8},{2,10},{4,12},{6,14},{8,0},{10,2},{12,4},{14,6},{16,24},{18,... | collective-permute-start | bytes 983048 | tf_op jit(solution)/shard_map/ppermute | solution.py:330
  386.6 28.8 %collective-permute-start.28 = (bf16[320,512]{1,0:T(8,128)(2,1)S(1)}, bf16[320,512]{1,0:T(8,128)(2,1)S(1)}, u32[]{:S(2)}, u32[]{:S(2)}) collective-permute-start(bf16[320,512]{1,0:T(8,128)(2,1)S(1)} %pad_maximum_fusion.16), channel_id=1, source_target_pairs={{0,4},{2,6},{4,0},{6,2},{8,12},{10,14},{12,8},{14,10},{16,20},{18,... | collective-permute-start | bytes 983048 | tf_op jit(solution)/shard_map/ppermute | solution.py:330
  389.0 26.4 %collective-permute-start.14 = (bf16[320,512]{1,0:T(8,128)(2,1)S(1)}, bf16[320,512]{1,0:T(8,128)(2,1)S(1)}, u32[]{:S(2)}, u32[]{:S(2)}) collective-permute-start(bf16[320,512]{1,0:T(8,128)(2,1)S(1)} %pad_maximum_fusion.14), channel_id=1, source_target_pairs={{0,4},{2,6},{4,0},{6,2},{8,12},{10,14},{12,8},{14,10},{16,20},{18,... | collective-permute-start | bytes 983048 | tf_op jit(solution)/shard_map/ppermute | solution.py:330
  417.3 16.2 %collective-permute-start.36 = (bf16[640,512]{1,0:T(8,128)(2,1)}, bf16[640,512]{1,0:T(8,128)(2,1)S(1)}, u32[]{:S(2)}, u32[]{:S(2)}) collective-permute-start(bf16[640,512]{1,0:T(8,128)(2,1)} %pad_maximum_fusion.10), channel_id=1, source_target_pairs={{0,2},{2,0},{4,6},{6,4},{8,10},{10,8},{12,14},{14,12},{16,18},{18,... | collective-permute-start | bytes 1966088 | tf_op jit(solution)/shard_map/ppermute | solution.py:330
  418.5 15.5 %collective-permute-start.37 = (bf16[640,512]{1,0:T(8,128)(2,1)}, bf16[640,512]{1,0:T(8,128)(2,1)S(1)}, u32[]{:S(2)}, u32[]{:S(2)}) collective-permute-start(bf16[640,512]{1,0:T(8,128)(2,1)} %pad_maximum_fusion.11), channel_id=1, source_target_pairs={{0,2},{2,0},{4,6},{6,4},{8,10},{10,8},{12,14},{14,12},{16,18},{18,... | collective-permute-start | bytes 1966088 | tf_op jit(solution)/shard_map/ppermute | solution.py:330
  421.6 13.4 %collective-permute-start.38 = (bf16[640,512]{1,0:T(8,128)(2,1)S(1)}, bf16[640,512]{1,0:T(8,128)(2,1)S(1)}, u32[]{:S(2)}, u32[]{:S(2)}) collective-permute-start(bf16[640,512]{1,0:T(8,128)(2,1)S(1)} %copy-done.4), channel_id=1, source_target_pairs={{0,2},{2,0},{4,6},{6,4},{8,10},{10,8},{12,14},{14,12},{16,18},{18,... | collective-permute-start | bytes 1966088 | tf_op jit(solution)/shard_map/ppermute | solution.py:330
  421.6 13.8 %collective-permute-start.39 = (bf16[640,512]{1,0:T(8,128)(2,1)S(1)}, bf16[640,512]{1,0:T(8,128)(2,1)S(1)}, u32[]{:S(2)}, u32[]{:S(2)}) collective-permute-start(bf16[640,512]{1,0:T(8,128)(2,1)S(1)} %pad_maximum_fusion.13), channel_id=1, source_target_pairs={{0,2},{2,0},{4,6},{6,4},{8,10},{10,8},{12,14},{14,12},{16,18},{18,... | collective-permute-start | bytes 1966088 | tf_op jit(solution)/shard_map/ppermute | solution.py:330
  (39 other events, 431.0 us)
Sparse Core Ops, SparseCore 0:
  192.2 225.0 all-reduce.4

commit v4 on v3

--- a/solution.py
+++ b/solution.py
@@ -9,6 +9,7 @@
 BUCKETS = 128
 TEXT = 512
 NEG = -1e30
+LOG2E = math.log2(math.e)
 SCALE = 1.0 / math.sqrt(3 * HEAD_DIM)
 F32 = jnp.float32
 BF16 = jnp.bfloat16
@@ -26,14 +27,31 @@
     return lax.broadcasted_iota(jnp.int32, shape, d)
 
 
-def lane_pick(table, index):
+def pick(table, index):
     return jnp.take_along_axis(table, index, axis=1, mode="promise_in_bounds")
 
 
-def fwd_kernel(slots, sp, len_ref, q_ref, k_ref, v_ref, relk_ref, relq_ref, bc_ref, br_ref,
-               ctx_ref, p_ref, qs, ks, vs, idx, nq, nk, fk):
+def pick(table, index):
+    dims = lax.GatherDimensionNumbers(
+        offset_dims=(), collapsed_slice_dims=(1,), start_index_map=(1,),
+        operand_batching_dims=(0,), start_indices_batching_dims=(0,))
+    return lax.gather(table, index[..., None], dims, slice_sizes=(1, 1),
+                      mode=lax.GatherScatterMode.PROMISE_IN_BOUNDS)
+
+
+LEVELS = 10900.0
+HALF_WORD = 65536.0
+
+
+def tall_block(rows):
+    return next(n for n in (288, 192, 128, 64) if rows % n == 0)
+
+
+def fwd_kernel(slots, sp, rp, len_ref, q_ref, k_ref, v_ref, relk_ref, relq_ref, bc_ref, br_ref,
+               ctx_ref, p_ref, qs, ks, vs, kt, idx, nq, nk, sq, fq, fk, gk, cs):
     pair = pl.program_id(1)
     nb = sp // 128
+    tall = tall_block(rp)
 
     @pl.when(pair == 0)
     def _():
@@ -56,96 +74,143 @@
     qs[0:slots, :] = q_ref[...]
     ks[0:slots, :] = k_ref[...]
     vs[0:slots, :] = v_ref[...]
+    kt[...] = ks[...].astype(F32).T.astype(BF16)
     place = iota((1, sp), 1)
     length = len_ref[pl.program_id(0)]
-    valid = (place < length) | ((place >= TEXT) & (place < slots))
+    barred = jnp.where((place < length) | ((place >= TEXT) & (place < slots)), 0.0, NEG)
     half = iota((1, 128), 1) < 64
 
-    for h in range(2):
-        mine = half if h == 0 else jnp.logical_not(half)
-        qm = jnp.where(mine, qs[...], 0)
-        km = jnp.where(mine, ks[...], 0)
-        nq[...] = nt(qm, relk_ref[...])
-        nk[...] = nt(km, relq_ref[...])
-
-        def key_side(b, c):
-            r0 = pl.multiple_of(b * 128, 128)
-            for ib in range(nb):
-                g = None
+    def longest(rel_ref, h):
+        rel = rel_ref[h * 64:(h + 1) * 64, :].astype(F32)
+        return jnp.max(jnp.sum(rel * rel, axis=0, keepdims=True), axis=1, keepdims=True) * 1.03
+
+    def bound(squares, most):
+        return jnp.maximum(squares * most, 1e-30)
+
+    member = jnp.where((iota((128, 256), 0) < 64) == (iota((128, 256), 1) < 128), 1.0, 0.0).astype(BF16)
+    for side, (rows_ref, rel_ref, table) in enumerate(((qs, relk_ref, nq), (ks, relq_ref, nk))):
+        most = [longest(rel_ref, h) for h in range(2)]
+        if side == 1:
+            most_k = most
+
+        def pack(b, c):
+            r0 = pl.multiple_of(b * tall, tall)
+            here = rows_ref[pl.ds(r0, tall), :]
+            wide = here.astype(F32)
+            squares = nn((wide * wide).astype(BF16), member)
+            words = []
+            for h in range(2):
+                mine = half if h == 0 else jnp.logical_not(half)
+                top = bound(squares[:, h * 128:(h + 1) * 128], most[h])
+                inverse = lax.rsqrt(top)
+                if side == 0:
+                    sq[h, pl.ds(r0, tall), :] = top * inverse * (1.0 / (LEVELS * HALF_WORD))
+                inverse = inverse * LEVELS
+                near = nn(jnp.where(mine, here, 0), rel_ref[...])
+                words.append(jnp.round(near * jnp.concatenate([inverse] * 3, axis=1)).astype(jnp.int32))
+            table[pl.ds(r0, tall), :] = (words[0] << 16) + words[1]
+            return c
+        lax.fori_loop(0, rp // tall, pack, 0)
+
+    turned = kt[...].astype(F32)
+    turned = (turned * turned).astype(BF16)
+    pick_head = jnp.where((iota((16, 128), 0) < 8) == (iota((16, 128), 1) < 64), 1.0, 0.0).astype(BF16)
+    squares = nn(pick_head, turned)
+    step_k = [jnp.sqrt(bound(squares[h * 8:h * 8 + 1, :], most_k[h])) * (1.0 / (LEVELS * HALF_WORD)) for h in range(2)]
+
+    def near(r0, count):
+        for r in range(0, count, 8):
+            here = pl.ds(pl.multiple_of(r0 + r, 8), 8)
+            for jb in range(nb):
+                at = slice(jb * 128, (jb + 1) * 128)
+                sums = [None] * 2
                 for t in range(3):
-                    e = lane_pick(nk[pl.ds(r0, 128), t * 128:(t + 1) * 128],
-                                  idx[t, pl.ds(r0, 128), ib * 128:(ib + 1) * 128])
-                    g = e if g is None else g + e
-                fk[ib * 128:(ib + 1) * 128, pl.ds(r0, 128)] = g.T
-            return c
-        lax.fori_loop(0, nb, key_side, 0)
-
-        def query_side(b, c):
-            r0 = pl.multiple_of(b * 128, 128)
-            q_b = jnp.where(mine, qs[pl.ds(r0, 128), :], 0)
-            s = nt(q_b, ks[...]) + fk[pl.ds(r0, 128), :]
-            parts = []
-            for jb in range(nb):
-                g = s[:, jb * 128:(jb + 1) * 128]
-                for t in range(3):
-                    g = g + lane_pick(nq[pl.ds(r0, 128), t * 128:(t + 1) * 128],
-                                      idx[t, pl.ds(r0, 128), jb * 128:(jb + 1) * 128])
-                parts.append(g)
-            s = jnp.concatenate(parts, axis=1)
-            s = jnp.where(valid, s * SCALE, NEG)
+                    ix = idx[t, here, at]
+                    kind = slice(t * 128, (t + 1) * 128)
+                    for n, table in enumerate((nq, nk)):
+                        e = pick(table[here, kind], ix)
+                        sums[n] = e if sums[n] is None else sums[n] + e
+                fq[here, at] = sums[0]
+                gk[r:r + 8, at] = sums[1]
+        for jb in range(nb):
+            at = slice(jb * 128, (jb + 1) * 128)
+            fk[at, pl.ds(r0, 128)] = gk[:, at].T
+
+    def near_block(b, c):
+        near(pl.multiple_of(b * 128, 128), 128)
+        return c
+    lax.fori_loop(0, rp // 128, near_block, 0)
+    if rp % 128:
+        gk[rp % 128:, :] = jnp.zeros((128 - rp % 128, sp), jnp.int32)
+        near(rp // 128 * 128, rp % 128)
+
+    def soft(b, c):
+        r0 = pl.multiple_of(b * tall, tall)
+        for h in range(2):
+            mine = half if h == 0 else jnp.logical_not(half)
+            q_b = jnp.where(mine, qs[pl.ds(r0, tall), :], 0)
+            from_q = fq[pl.ds(r0, tall), :]
+            from_k = fk[pl.ds(r0, tall), :]
+            if h == 1:
+                from_q = from_q << 16
+                from_k = from_k << 16
+            step_q = jnp.concatenate([sq[h, pl.ds(r0, tall), :]] * nb, axis=1)
+            s = (nn(q_b, kt[...]) + barred) + (from_q.astype(F32) * step_q + from_k.astype(F32) * step_k[h])
             m = jnp.max(s, axis=1, keepdims=True)
-            e = jnp.exp(s - m)
+            e = jnp.exp2((s - m) * (SCALE * LOG2E))
             tot = jnp.sum(e, axis=1, keepdims=True)
             p = (e * (1.0 / tot)).astype(BF16)
-            p_ref[h, pl.ds(r0, 128), :] = p
-            c_b = nn(p, vs[...])
-            fk[pl.ds(r0, 128), 0:128] = c_b
-            return c
-        lax.fori_loop(0, nb, query_side, 0)
-        if h == 0:
-            ctx_ref[...] = fk[0:slots, 0:128].astype(BF16)
-        else:
-            ctx_ref[...] = jnp.where(mine, fk[0:slots, 0:128].astype(BF16), ctx_ref[...])
+            p_ref[h, pl.ds(r0, tall), :] = p
+            got = nn(p, vs[...])
+            if h == 0:
+                first = got
+            else:
+                cs[pl.ds(r0, tall), :] = jnp.where(mine, got, first).astype(BF16)
+        return c
+    lax.fori_loop(0, rp // tall, soft, 0)
+    ctx_ref[...] = cs[0:slots, :]
 
 
 def attend_forward(lengths, qkv, relk, relq, boxes_col, boxes_row, heads):
     docs, slots, width = qkv.shape
     width = width // 3
     sp = boxes_row.shape[2]
+    rp = -(-slots // 64) * 64
     pairs = heads // 2
 
     def part(t):
         return pl.BlockSpec((None, slots, 128), lambda d, p, ln: (d, 0, t * pairs + p))
+    rel = pl.BlockSpec((128, 3 * BUCKETS), lambda d, p, ln: (p, 0))
     grid_spec = pltpu.PrefetchScalarGridSpec(
         num_scalar_prefetch=1, grid=(docs, pairs),
-        in_specs=[part(0), part(1), part(2),
-                  pl.BlockSpec((3 * BUCKETS, 128), lambda d, p, ln: (0, p)),
-                  pl.BlockSpec((3 * BUCKETS, 128), lambda d, p, ln: (0, p)),
+        in_specs=[part(0), part(1), part(2), rel, rel,
                   pl.BlockSpec((None, sp, 2), lambda d, p, ln: (d, 0, 0)),
                   pl.BlockSpec((None, 2, sp), lambda d, p, ln: (d, 0, 0))],
         out_specs=[pl.BlockSpec((None, slots, 128), lambda d, p, ln: (d, 0, p)),
-                   pl.BlockSpec((None, 2, sp, sp), lambda d, p, ln: (d, p, 0, 0))],
-        scratch_shapes=[pltpu.VMEM((sp, 128), BF16)] * 3
-        + [pltpu.VMEM((3, sp, sp), jnp.int32), pltpu.VMEM((sp, 384), F32), pltpu.VMEM((sp, 384), F32),
-           pltpu.VMEM((sp, sp), F32)])
+                   pl.BlockSpec((None, 2, rp, sp), lambda d, p, ln: (d, p, 0, 0))],
+        scratch_shapes=[pltpu.VMEM((sp, 128), BF16)] * 3 + [pltpu.VMEM((128, sp), BF16)]
+        + [pltpu.VMEM((3, sp, sp), jnp.int32), pltpu.VMEM((sp, 384), jnp.int32), pltpu.VMEM((sp, 384), jnp.int32),
+           pltpu.VMEM((2, sp, 128), F32), pltpu.VMEM((sp, sp), jnp.int32), pltpu.VMEM((sp, sp), jnp.int32),
+           pltpu.VMEM((128, sp), jnp.int32), pltpu.VMEM((rp, 128), BF16)])
     return pl.pallas_call(
-        functools.partial(fwd_kernel, slots, sp),
+        functools.partial(fwd_kernel, slots, sp, rp),
         out_shape=[jax.ShapeDtypeStruct((docs, slots, width), BF16),
-                   jax.ShapeDtypeStruct((docs, heads, sp, sp), BF16)],
+                   jax.ShapeDtypeStruct((docs, heads, rp, sp), BF16)],
         grid_spec=grid_spec, name="attend_forward",
         compiler_params=pltpu.CompilerParams(vmem_limit_bytes=56 << 20),
     )(lengths, qkv, qkv, qkv, relk, relq, boxes_col, boxes_row)
 
 
-def bwd_kernel(slots, sp, width, q_ref, k_ref, v_ref, dc_ref, p_ref, relk_ref, relq_ref, bc_ref, br_ref,
+def bwd_kernel(slots, sp, rp, width, q_ref, k_ref, v_ref, dc_ref, p_ref, relk_ref, relq_ref, bc_ref, br_ref,
                dqkv_ref, gk_ref, gq_ref,
-               qs, ks, vs, dcs, base, ex, ey, mx, my, ds, dst, gt, acc):
+               qs, ks, dcs, base, ex, ey, vt, qt, kt, dct, mx, my, ds, dst, w2, o1, hs, dns, gs, gt, acc):
     pair = pl.program_id(1)
     nb = sp // 128
+    tall = tall_block(rp)
 
     @pl.when(pair == 0)
     def _():
-        for r in (qs, ks, vs, dcs, ds, dst):
+        for r in (qs, ks, dcs, ds, dst):
             r[...] = jnp.zeros_like(r)
         lane = iota((sp, 128), 1)
         ax = bc_ref[:, 0:1] >> 4
@@ -169,106 +234,113 @@
             return c
         lax.fori_loop(0, nb, rows, 0)
 
+    qs[0:slots, :] = v_ref[...]
+    vt[...] = qs[...].astype(F32).T.astype(BF16)
     qs[0:slots, :] = q_ref[...]
     ks[0:slots, :] = k_ref[...]
-    vs[0:slots, :] = v_ref[...]
     dcs[0:slots, :] = dc_ref[...]
-    half = iota((1, 128), 1) < 64
-    lane1 = iota((128, 128), 1)
-    row1 = iota((128, 128), 0)
-
-    for h in range(2):
-        mine = half if h == 0 else jnp.logical_not(half)
+    qt[...] = qs[...].astype(F32).T.astype(BF16)
+    kt[...] = ks[...].astype(F32).T.astype(BF16)
+    dct[...] = dcs[...].astype(F32).T.astype(BF16)
+
+    def head(h, carry):
+        mine = (iota((1, 128), 1) < 64) == (h == 0)
+        mine_down = (iota((128, 1), 0) < 64) == (h == 0)
 
         def grad_scores(b, c):
+            r0 = pl.multiple_of(b * tall, tall)
+            d_b = jnp.where(mine, dcs[pl.ds(r0, tall), :], 0)
+            dp = nn(d_b, vt[...])
+            p = p_ref[h, pl.ds(r0, tall), :].astype(F32)
+            inner = jnp.sum(p * dp, axis=1, keepdims=True)
+            ds[pl.ds(r0, tall), 128:128 + sp] = (p * (dp - inner)).astype(BF16)
+            return c
+        lax.fori_loop(0, rp // tall, grad_scores, 0)
+
+        def turn(b, c):
             r0 = pl.multiple_of(b * 128, 128)
-            d_b = jnp.where(mine, dcs[pl.ds(r0, 128), :], 0)
-            dp = nt(d_b, vs[...])
-            p = p_ref[h, pl.ds(r0, 128), :].astype(F32)
-            inner = jnp.sum(p * dp, axis=1, keepdims=True)
-            d = p * (dp - inner)
-            ds[pl.ds(r0, 128), 128:128 + sp] = d.astype(BF16)
             for jb in range(nb):
                 dst[jb * 128:(jb + 1) * 128, pl.ds(pl.multiple_of(r0 + 128, 128), 128)] = \
-                    d[:, jb * 128:(jb + 1) * 128].T.astype(BF16)
+                    ds[pl.ds(r0, 128), (jb + 1) * 128:(jb + 2) * 128].T
             return c
-        lax.fori_loop(0, nb, grad_scores, 0)
-
-        dct = jnp.where(mine, dcs[...], 0).astype(F32).T.astype(BF16)
-        dvt = nn(dct, p_ref[h, :, :])
-        if h == 0:
-            gt[...] = dvt
-        else:
-            gt[...] += dvt
+        lax.fori_loop(0, nb, turn, 0)
+
+        dvt = nn(dct[:, 0:rp], p_ref[h, :, :])
+        gt[...] = jnp.where(mine_down, dvt, gt[...])
 
         for side in range(2):
             mat = ds if side == 0 else dst
             other = ks if side == 0 else qs
-            own = qs if side == 0 else ks
+            own_t = qt if side == 0 else kt
             rel_ref = relk_ref if side == 0 else relq_ref
-            g_ref = gk_ref if side == 0 else gq_ref
             blk = iota((sp, 128), 0) >> 7
             lane_sp = iota((sp, 128), 1) & 63
-            w = jnp.where(mine, other[...].astype(F32), jnp.where(blk == lane_sp, 1.0, 0.0)).astype(BF16)
-            w2 = jnp.concatenate([w, base[...]], axis=1)
-            relm = jnp.where(mine, rel_ref[...], 0)
-            acc[...] = jnp.zeros_like(acc)
-
-            def rows(b, c):
-                r0 = pl.multiple_of(b * 128, 128)
-                d_b = mat[pl.ds(r0, 128), 128:128 + sp]
-                out = nn(d_b, w2)
-                hist = out[:, 128:] + nn(d_b * mx[pl.ds(r0, 128), :], ex[...]) \
-                    + nn(d_b * my[pl.ds(r0, 128), :], ey[...])
-                before = mat[pl.ds(r0, 128), pl.ds(r0, 128)].astype(F32)
-                here = mat[pl.ds(r0, 128), pl.ds(pl.multiple_of(r0 + 128, 128), 128)].astype(F32)
-                after = mat[pl.ds(r0, 128), pl.ds(pl.multiple_of(r0 + 256, 128), 128)].astype(F32)
-                sums = jnp.where(mine, 0.0, out[:, :128])
-                blkno = lane1 & 63
-                low = jnp.where(blkno <= b - 2, sums, 0.0) + jnp.where(lane1 <= row1 + 64, before, 0.0) \
-                    + jnp.where(lane1 <= row1 - 64, here, 0.0)
-                high = jnp.where(blkno >= b + 2, sums, 0.0) + jnp.where(lane1 >= row1 + 63, here, 0.0) \
-                    + jnp.where(lane1 >= row1 - 65, after, 0.0)
+            w2[:, 0:128] = jnp.where(mine, other[...].astype(F32), jnp.where(blk == lane_sp, 1.0, 0.0)).astype(BF16)
+            w2[:, 128:256] = base[...]
+
+            def spread(b, c):
+                r0 = pl.multiple_of(b * tall, tall)
+                d_b = mat[pl.ds(r0, tall), 128:128 + sp]
+                out = nn(d_b, w2[...])
+                o1[pl.ds(r0, tall), :] = out[:, :128]
+                hs[pl.ds(r0, tall), :] = out[:, 128:] + nn(d_b * mx[pl.ds(r0, tall), :], ex[...]) \
+                    + nn(d_b * my[pl.ds(r0, tall), :], ey[...])
+                return c
+            lax.fori_loop(0, rp // tall, spread, 0)
+
+            def buckets(b, r0, n):
+                lane = iota((n, 128), 1)
+                row = iota((n, 128), 0)
+                before = mat[pl.ds(r0, n), pl.ds(r0, 128)].astype(F32)
+                here = mat[pl.ds(r0, n), pl.ds(r0 + 128, 128)].astype(F32)
+                after = mat[pl.ds(r0, n), pl.ds(r0 + 256, 128)].astype(F32)
+                sums = jnp.where(mine, 0.0, o1[pl.ds(r0, n), :])
+                blkno = lane & 63
+                low = jnp.where(blkno <= b - 2, sums, 0.0) + jnp.where(lane <= row + 64, before, 0.0) \
+                    + jnp.where(lane <= row - 64, here, 0.0)
+                high = jnp.where(blkno >= b + 2, sums, 0.0) + jnp.where(lane >= row + 63, here, 0.0) \
+                    + jnp.where(lane >= row - 65, after, 0.0)
                 low = jnp.sum(low, axis=1, keepdims=True)
                 high = jnp.sum(high, axis=1, keepdims=True)
-                at = lane1 + row1 + 64
-                place = at & 127
-                mid = jnp.where(at < 128, lane_pick(before, place),
-                                jnp.where(at < 256, lane_pick(here, place), lane_pick(after, place)))
-                dn0 = jnp.where(lane1 == 0, low, jnp.where(lane1 == 127, high, mid))
-                ax = bc_ref[pl.ds(r0, 128), 0:1] >> 4
-                ay = bc_ref[pl.ds(r0, 128), 1:2] >> 4
-                c1 = lane1 + ax - 63
-                c2 = lane1 + ay - 63
-                dn1 = jnp.where((c1 >= 0) & (c1 < 64), lane_pick(hist, c1 & 127), 0.0)
-                dn2 = jnp.where((c2 >= 0) & (c2 < 64), lane_pick(hist, (c2 + 64) & 127), 0.0)
-                dn = jnp.concatenate([dn0, dn1, dn2], axis=1).astype(BF16)
-                g = (out[:, :128] + nn(dn, relm)) * SCALE
-                o_b = jnp.where(mine, own[pl.ds(r0, 128), :], 0)
-                acc[...] += nn(o_b.astype(F32).T.astype(BF16), dn)
-                return c, g
-            for b in range(nb):
-                _, g = rows(b, 0)
-                n = min(128, slots - b * 128)
-                at = pl.ds(pl.multiple_of(side * width + pair * 128, 128), 128)
-                if h == 0:
-                    dqkv_ref[b * 128:b * 128 + n, at] = g[0:n].astype(BF16)
-                else:
-                    dqkv_ref[b * 128:b * 128 + n, at] = jnp.where(
-                        mine, g[0:n].astype(BF16), dqkv_ref[b * 128:b * 128 + n, at])
-            turned = acc[...].T * SCALE
-            if h == 0:
-                g_ref[...] = turned
-            else:
-                g_ref[...] += turned
-    dv = gt[...].T
-    dqkv_ref[:, pl.ds(pl.multiple_of(2 * width + pair * 128, 128), 128)] = dv[0:slots, :].astype(BF16)
+                near = jnp.where(lane >= row + 64, before, jnp.where(lane <= row - 65, after, here))
+                mid = pick(near, (lane + row + 64) & 127)
+                dn0 = jnp.where(lane == 0, low, jnp.where(lane == 127, high, mid))
+                hist = hs[pl.ds(r0, n), :]
+                c1 = lane + (bc_ref[pl.ds(r0, n), 0:1] >> 4) - 63
+                c2 = lane + (bc_ref[pl.ds(r0, n), 1:2] >> 4) - 63
+                dn1 = jnp.where((c1 >= 0) & (c1 < 64), pick(hist, c1 & 127), 0.0)
+                dn2 = jnp.where((c2 >= 0) & (c2 < 64), pick(hist, (c2 + 64) & 127), 0.0)
+                dns[pl.ds(r0, n), :] = jnp.concatenate([dn0, dn1, dn2], axis=1).astype(BF16)
+
+            def bucket_block(b, c):
+                buckets(b, pl.multiple_of(b * 128, 128), 128)
+                return c
+            lax.fori_loop(0, rp // 128, bucket_block, 0)
+            if rp % 128:
+                buckets(rp // 128, rp // 128 * 128, rp % 128)
+
+            def gather_back(b, c):
+                r0 = pl.multiple_of(b * tall, tall)
+                g = (o1[pl.ds(r0, tall), :] + nn(dns[pl.ds(r0, tall), :], rel_ref[...])) * SCALE
+                gs[side, pl.ds(r0, tall), :] = jnp.where(mine, g, gs[side, pl.ds(r0, tall), :].astype(F32)).astype(BF16)
+                return c
+            lax.fori_loop(0, rp // tall, gather_back, 0)
+            acc[side] = jnp.where(mine_down, nn(own_t[:, 0:rp], dns[...]), acc[side])
+        return carry
+    lax.fori_loop(0, 2, head, 0)
+
+    for side in range(2):
+        dqkv_ref[:, pl.ds(pl.multiple_of(side * width + pair * 128, 128), 128)] = gs[side, 0:slots, :]
+    gk_ref[...] = acc[0].T * SCALE
+    gq_ref[...] = acc[1].T * SCALE
+    dqkv_ref[:, pl.ds(pl.multiple_of(2 * width + pair * 128, 128), 128)] = gt[...].T[0:slots, :].astype(BF16)
 
 
 def attend_backward(qkv, dctx, probs, relk, relq, boxes_col, boxes_row, heads):
     docs, slots, width = qkv.shape
     width = width // 3
     sp = boxes_row.shape[2]
+    rp = -(-slots // 64) * 64
     pairs = heads // 2
 
     def part(t):
@@ -276,11 +348,11 @@
     rel = pl.BlockSpec((3 * BUCKETS, 128), lambda d, p: (0, p))
     grel = pl.BlockSpec((None, 3 * BUCKETS, 128), lambda d, p: (d, 0, p))
     return pl.pallas_call(
-        functools.partial(bwd_kernel, slots, sp, width),
+        functools.partial(bwd_kernel, slots, sp, rp, width),
         grid=(docs, pairs),
         in_specs=[part(0), part(1), part(2),
                   pl.BlockSpec((None, slots, 128), lambda d, p: (d, 0, p)),
-                  pl.BlockSpec((None, 2, sp, sp), lambda d, p: (d, p, 0, 0)),
+                  pl.BlockSpec((None, 2, rp, sp), lambda d, p: (d, p, 0, 0)),
                   rel, rel,
                   pl.BlockSpec((None, sp, 2), lambda d, p: (d, 0, 0)),
                   pl.BlockSpec((None, 2, sp), lambda d, p: (d, 0, 0))],
@@ -288,9 +360,11 @@
         out_shape=[jax.ShapeDtypeStruct((docs, slots, 3 * width), BF16),
                    jax.ShapeDtypeStruct((docs, 3 * BUCKETS, width), F32),
                    jax.ShapeDtypeStruct((docs, 3 * BUCKETS, width), F32)],
-        scratch_shapes=[pltpu.VMEM((sp, 128), BF16)] * 7
+        scratch_shapes=[pltpu.VMEM((sp, 128), BF16)] * 6 + [pltpu.VMEM((128, sp), BF16)] * 4
         + [pltpu.VMEM((sp, sp), BF16)] * 2 + [pltpu.VMEM((sp, sp + 256), BF16)] * 2
-        + [pltpu.VMEM((128, sp), F32), pltpu.VMEM((128, 384), F32)],
+        + [pltpu.VMEM((sp, 256), BF16), pltpu.VMEM((rp, 128), F32), pltpu.VMEM((rp, 128), F32),
+           pltpu.VMEM((rp, 384), BF16), pltpu.VMEM((2, rp, 128), BF16), pltpu.VMEM((128, sp), F32),
+           pltpu.VMEM((2, 128, 384), F32)],
         name="attend_backward",
         compiler_params=pltpu.CompilerParams(vmem_limit_bytes=56 << 20),
     )(qkv, qkv, qkv, dctx, probs, relk, relq, boxes_col, boxes_row)
@@ -424,7 +498,7 @@
     upstream = join(out_rows, 1)
     out_whole = join(w_out, 0)
     projected = projected.reshape(doc_count, slot_count, 3 * width)
-    context, probs = attend_forward(lengths, projected, rel_k, rel_q, boxes_col, boxes_row, heads_here)
+    context, probs = attend_forward(lengths, projected, rel_k.T, rel_q.T, boxes_col, boxes_row, heads_here)
     context, upstream, norms, out_whole = lax.optimization_barrier((context, upstream, norms, out_whole))
     context = context.reshape(row_count, width)
 

time: 460 us -> 425 us (0.924)
  Pallas kernels: 152 us -> 119 us
  waiting for transfers between devices: 147 us -> 137 us
  starting transfers between devices: 36 us -> 40.9 us
    pallas_call x2, Pallas kernels: 152 us -> 119 us  [the longest x1 72.5 us: attend_backward(): pl.pallas_call(functools.partial(bwd_kernel, slots, sp, rp, width), grid=...]
    ppermute x32, waiting for transfers between devices: 94 us -> 87.2 us  [swap(): return lax.ppermute(array, 'dp', [(i, i ^ bit) for i in range(size)])]
  transfers between devices with their start and end apart: 41 -> 41, of which waited for: 17 -> 17; matrix products, arithmetic and copies ran while one was open for 14% -> 16% of each run, Pallas kernels for 34% -> 28%
where the time goes in v4:
time: 425 us; the launch traced here: 416 us
  waiting for transfers between devices  137 us (32%)
  Pallas kernels  119 us (28%)
  other arithmetic  43.7 us (10%)
  starting transfers between devices  40.9 us (10%)
  matrix products  40.3 us (9%)
  local copies, waits for them, and re-layouts  20.3 us (5%)
  between operations  15.9 us (4%)
    ppermute x32, waiting for transfers between devices, swap(): return lax.ppermute(array, 'dp', [(i, i ^ bit) for i in range(size)])  87.2 us
    pallas_call x1, Pallas kernels, attend_backward(): pl.pallas_call(functools.partial(bwd_kernel, slots, sp, rp, width), grid=...  72.5 us
    pallas_call x1, Pallas kernels, attend_forward(): pl.pallas_call(functools.partial(fwd_kernel, slots, sp, rp), out_shape=[j...  46.2 us
    ppermute x2, waiting for transfers between devices, total(): lax.ppermute(partial, 'tensor', pair).astype(F32)  35.8 us
    ppermute x32, starting transfers between devices, swap(): return lax.ppermute(array, 'dp', [(i, i ^ bit) for i in range(size)])  29.1 us
    dot_general x6, matrix products, dot_tn(): lax.dot_general(a, b, (((0,), (0,)), ((), ())), preferred_element_type=F32)  16.1 us
    ppermute x5, waiting for transfers between devices, join(): other = lax.ppermute(array, 'tensor', pair)  13.7 us
    unnamed x64, local copies, waits for them, and re-layouts  10.6 us
  transfers between devices with their start and end apart: 41, of which 17 were waited for; matrix products, arithmetic and copies ran while one was open for 16% of the time, Pallas kernels for 28%

profile of v4, /device:TPU:0, one launch (start us, length us, event | category | flops | bytes accessed | tf_op | source)
XLA Modules:
  0.0 416.5 jit_solution(3418561900870410576)
XLA Ops:
  7.2 3.1 collective-permute-start
  20.4 3.2 copy.26
  28.4 3.2 fusion.8.q_ref.k_ref.v_ref
  31.6 46.2 %attend_forward.1 = (bf16[1,561,512]{2,1,0:T(8,128)(2,1)}, bf16[1,8,576,640]{3,2,1,0:T(8,128)(2,1)}) custom-call(s32[1]{0:T(128)S(6)} %copy.48.len_ref, bf16[1,561,1536]{2,1,0:T(8,128)(2,1)} %fusion.8.q_ref.k_ref.v_ref, bf16[1,561,1536]{2,1,0:T(8,128)(2,1)} %fusion.8.q_ref.k_ref.v_ref, bf16[1,561,1536]{2,1,0:T(8,128)(2,1)} %fusion.8.q_ref.k_ref.v_ref, ...), custom_call_target="tpu_custom_call" | custom-call | tf_op jit(solution)/shard_map/attend_forward/pallas_call | solution.py:195
  80.4 12.7 %collective-permute-done.4 = bf16[561,512]{1,0:T(8,128)(2,1)S(1)} collective-permute-done((bf16[561,512]{1,0:T(8,128)(2,1)S(1)}, bf16[561,512]{1,0:T(8,128)(2,1)S(1)}, u32[]{:S(2)}, u32[]{:S(2)}) %collective-permute-start.4) | collective-permute-done | bytes 574496 | tf_op jit(solution)/shard_map/ppermute | solution.py:468
  95.4 5.1 %multiply_convert_fusion.1 = (bf16[561,2048]{1,0:T(8,128)(2,1)S(1)}, f32[561,2048]{1,0:T(8,128)}) fusion(bf16[1024,2048]{1,0:T(8,128)(2,1)S(1)} %copy-done.23, f32[561,1024]{1,0:T(8,128)S(1)} %get-tuple-element.132, f32[1024]{0:T(1024)S(1)} %bitcast.92, f32[1024]{0:T(1024)S(1)} %bitcast.80, f32[561]{0:T(1024)S(1)} %get-tuple-element.131, ...), kind=kOutput, calls=%fused_computation.10 | convolution fusion | flops 2361621504 | bytes 13398408 | tf_op jit(solution)/shard_map/dot_general | solution.py:508
  100.6 3.7 convolution_convert_fusion.4
  105.3 23.9 %collective-permute-done.5 = bf16[561,1024]{1,0:T(8,128)(2,1)} collective-permute-done((bf16[561,1024]{1,0:T(8,128)(2,1)}, bf16[561,1024]{1,0:T(8,128)(2,1)}, u32[]{:S(2)}, u32[]{:S(2)}) %collective-permute-start.5) | collective-permute-done | bytes 1148960 | tf_op jit(solution)/shard_map/ppermute | solution.py:476
  129.2 2.8 fusion.37
  137.1 4.3 %multiply_convert_fusion = bf16[561,2048]{1,0:T(8,128)(2,1)S(1)} fusion(bf16[561,1024]{1,0:T(8,128)(2,1)S(1)} %get-tuple-element.37, bf16[2048,1024]{1,0:T(8,128)(2,1)S(1)} %copy-done.22, f32[561,2048]{1,0:T(8,128)S(1)} %bitcast.100), kind=kOutput, calls=%fused_computation.9 | convolution fusion | flops 2366791680 | bytes 12236800 | tf_op jit(solution)/shard_map/dot_general | solution.py:379
  145.8 5.0 %convolution_convert_fusion.1 = bf16[2048,1024]{1,0:T(8,128)(2,1)} fusion(bf16[561,2048]{1,0:T(8,128)(2,1)S(1)} %copy-done.27, bf16[561,1024]{1,0:T(8,128)(2,1)S(1)} %get-tuple-element.37), kind=kOutput, calls=%fused_computation.13 | convolution fusion | flops 2355101696 | bytes 7641088 | tf_op jit(solution)/shard_map/dot_general | solution.py:383
  150.8 5.8 %convolution_convert_fusion = bf16[1024,2048]{1,0:T(8,128)(2,1)} fusion(bf16[561,2048]{1,0:T(8,128)(2,1)S(1)} %multiply_convert_fusion, f32[561,1024]{1,0:T(8,128)S(1)} %get-tuple-element.132, f32[1024]{0:T(1024)S(1)} %bitcast.94, f32[1024]{0:T(1024)S(1)} %bitcast.82, f32[561]{0:T(1024)S(1)} %get-tuple-element.131, f32[561]{0:T(1024)S(1)} %get-tuple-element.130), kind=kOutput, calls=%fused_computation.12 | convolution fusion | flops 2357974016 | bytes 8802696 | tf_op jit(solution)/shard_map/dot_general | solution.py:383
  156.7 11.9 %collective-permute-done.6 = bf16[561,1024]{1,0:T(8,128)(2,1)} collective-permute-done((bf16[561,1024]{1,0:T(8,128)(2,1)S(1)}, bf16[561,1024]{1,0:T(8,128)(2,1)}, u32[]{:S(2)}, u32[]{:S(2)}) %collective-permute-start.6) | collective-permute-done | bytes 1148960 | tf_op jit(solution)/shard_map/ppermute | solution.py:476
  168.6 3.4 multiply_reduce_fusion
  176.7 72.5 %attend_backward.1 = (bf16[1,561,1536]{2,1,0:T(8,128)(2,1)}, f32[1,384,512]{2,1,0:T(8,128)}, f32[1,384,512]{2,1,0:T(8,128)}) custom-call(bf16[1,561,1536]{2,1,0:T(8,128)(2,1)} %fusion.8.q_ref.k_ref.v_ref, bf16[1,561,1536]{2,1,0:T(8,128)(2,1)} %fusion.8.q_ref.k_ref.v_ref, bf16[1,561,1536]{2,1,0:T(8,128)(2,1)} %fusion.8.q_ref.k_ref.v_ref, ...), custom_call_target="tpu_custom_call" | custom-call | tf_op jit(solution)/shard_map/attend_backward/pallas_call | solution.py:350
  267.2 5.4 %collective-permute-done.30 = bf16[320,512]{1,0:T(8,128)(2,1)S(1)} collective-permute-done((bf16[320,512]{1,0:T(8,128)(2,1)S(1)}, bf16[320,512]{1,0:T(8,128)(2,1)S(1)}, u32[]{:S(2)}, u32[]{:S(2)}) %collective-permute-start.30) | collective-permute-done | bytes 327712 | tf_op jit(solution)/shard_map/ppermute | solution.py:404
  274.5 12.3 %collective-permute-done.16 = bf16[320,512]{1,0:T(8,128)(2,1)S(1)} collective-permute-done((bf16[320,512]{1,0:T(8,128)(2,1)S(1)}, bf16[320,512]{1,0:T(8,128)(2,1)S(1)}, u32[]{:S(2)}, u32[]{:S(2)}) %collective-permute-start.16) | collective-permute-done | bytes 327712 | tf_op jit(solution)/shard_map/ppermute | solution.py:404
  292.4 8.7 %collective-permute-done.17 = bf16[160,512]{1,0:T(8,128)(2,1)S(1)} collective-permute-done((bf16[160,512]{1,0:T(8,128)(2,1)S(1)}, bf16[160,512]{1,0:T(8,128)(2,1)S(1)}, u32[]{:S(2)}, u32[]{:S(2)}) %collective-permute-start.17) | collective-permute-done | bytes 163872 | tf_op jit(solution)/shard_map/ppermute | solution.py:404
  303.3 2.7 collective-permute-start.25
  306.1 4.2 %collective-permute-done.10 = bf16[160,512]{1,0:T(8,128)(2,1)S(1)} collective-permute-done((bf16[160,512]{1,0:T(8,128)(2,1)S(1)}, bf16[160,512]{1,0:T(8,128)(2,1)S(1)}, u32[]{:S(2)}, u32[]{:S(2)}) %collective-permute-start.10) | collective-permute-done | bytes 163872 | tf_op jit(solution)/shard_map/ppermute | solution.py:404
  310.3 2.7 collective-permute-start.11
  316.9 4.4 %collective-permute-done.11 = bf16[80,512]{1,0:T(8,128)(2,1)S(1)} collective-permute-done((bf16[80,512]{1,0:T(8,128)(2,1)S(1)}, bf16[80,512]{1,0:T(8,128)(2,1)S(1)}, u32[]{:S(2)}, u32[]{:S(2)}) %collective-permute-start.11) | collective-permute-done | bytes 81952 | tf_op jit(solution)/shard_map/ppermute | solution.py:404
  321.5 3.0 collective-permute-start.34
  324.6 3.4 collective-permute-done.26
  328.1 6.9 %collective-permute-done.12 = bf16[80,512]{1,0:T(8,128)(2,1)S(1)} collective-permute-done((bf16[80,512]{1,0:T(8,128)(2,1)S(1)}, bf16[80,512]{1,0:T(8,128)(2,1)S(1)}, u32[]{:S(2)}, u32[]{:S(2)}) %collective-permute-start.12) | collective-permute-done | bytes 81952 | tf_op jit(solution)/shard_map/ppermute | solution.py:404
  335.1 9.7 %collective-permute-done.34 = bf16[160,512]{1,0:T(8,128)(2,1)S(1)} collective-permute-done((bf16[160,512]{1,0:T(8,128)(2,1)S(1)}, bf16[160,512]{1,0:T(8,128)(2,1)S(1)}, u32[]{:S(2)}, u32[]{:S(2)}) %collective-permute-start.34) | collective-permute-done | bytes 163872 | tf_op jit(solution)/shard_map/ppermute | solution.py:404
  345.0 6.5 %collective-permute-done.20 = bf16[160,512]{1,0:T(8,128)(2,1)S(1)} collective-permute-done((bf16[160,512]{1,0:T(8,128)(2,1)S(1)}, bf16[160,512]{1,0:T(8,128)(2,1)S(1)}, u32[]{:S(2)}, u32[]{:S(2)}) %collective-permute-start.20) | collective-permute-done | bytes 163872 | tf_op jit(solution)/shard_map/ppermute | solution.py:404
  355.7 12.4 %collective-permute-done.35 = bf16[320,512]{1,0:T(8,128)(2,1)S(1)} collective-permute-done((bf16[320,512]{1,0:T(8,128)(2,1)S(1)}, bf16[320,512]{1,0:T(8,128)(2,1)S(1)}, u32[]{:S(2)}, u32[]{:S(2)}) %collective-permute-start.35) | collective-permute-done | bytes 327712 | tf_op jit(solution)/shard_map/ppermute | solution.py:404
  368.3 10.6 %collective-permute-done.21 = bf16[320,512]{1,0:T(8,128)(2,1)S(1)} collective-permute-done((bf16[320,512]{1,0:T(8,128)(2,1)S(1)}, bf16[320,512]{1,0:T(8,128)(2,1)S(1)}, u32[]{:S(2)}, u32[]{:S(2)}) %collective-permute-start.21) | collective-permute-done | bytes 327712 | tf_op jit(solution)/shard_map/ppermute | solution.py:404
  386.7 7.0 %convert_element_type.334 = f32[1024,2048]{1,0:T(8,128)} convert(bf16[1024,2048]{1,0:T(8,128)(2,1)} %get-tuple-element.46) | non-fusion elementwise | flops 2097152 | bytes 12582912 | tf_op jit(solution)/shard_map/convert_element_type | solution.py:564
  393.7 4.4 %convert_element_type.335 = f32[2048,1024]{1,0:T(8,128)} convert(bf16[2048,1024]{1,0:T(8,128)(2,1)S(1)} %copy-done.6) | non-fusion elementwise | flops 2097152 | bytes 12582912 | tf_op jit(solution)/shard_map/convert_element_type | solution.py:565
  406.0 3.4 pad_maximum_fusion
  (236 shorter events, 85.9 us)
Async XLA Ops:
  7.2 374.7 %all-reduce.5.cloned.1.call-start = ((), (), s32[]{:S(2)}) async-start(), calls=%async_computation | async-start | bytes 16777216 | tf_op jit(solution)/shard_map/psum | solution.py:523
  7.2 17.5 %collective-permute-start = (bf16[561,512]{1,0:T(8,128)(2,1)}, bf16[561,512]{1,0:T(8,128)(2,1)}, u32[]{:S(2)}, u32[]{:S(2)}) collective-permute-start(bf16[561,512]{1,0:T(8,128)(2,1)} %bitcast.76), channel_id=1, source_target_pairs={{0,1},{1,0},{2,3},{3,2},{4,5},{5,4},{6,7},{7,6},{8,9},{9,8},{10,11... | collective-permute-start | bytes 1723400 | tf_op jit(solution)/shard_map/ppermute | solution.py:468
  11.0 13.7 %collective-permute-start.2 = (f32[4,512]{1,0:T(4,128)S(1)}, f32[4,512]{1,0:T(4,128)S(1)}, u32[]{:S(2)}, u32[]{:S(2)}) collective-permute-start(f32[4,512]{1,0:T(4,128)S(1)} %pad_maximum_fusion.23), channel_id=1, source_target_pairs={{0,1},{1,0},{2,3},{3,2},{4,5},{5,4},{6,7},{7,6},{8,9},{9,8},{10,11... | collective-permute-start | bytes 24584 | tf_op jit(solution)/shard_map/ppermute | solution.py:468
  11.1 66.7 %collective-permute-start.3 = (bf16[512,1024]{1,0:T(8,128)(2,1)}, bf16[512,1024]{1,0:T(8,128)(2,1)}, u32[]{:S(2)}, u32[]{:S(2)}) collective-permute-start(bf16[512,1024]{1,0:T(8,128)(2,1)} %param.16), channel_id=1, source_target_pairs={{0,1},{1,0},{2,3},{3,2},{4,5},{5,4},{6,7},{7,6},{8,9},{9,8},{10,11... | collective-permute-start | bytes 3145736 | tf_op jit(solution)/shard_map/ppermute | solution.py:468
  26.3 53.0 %collective-permute-start.1 = (bf16[561,512]{1,0:T(8,128)(2,1)S(1)}, bf16[561,512]{1,0:T(8,128)(2,1)S(1)}, u32[]{:S(2)}, u32[]{:S(2)}) collective-permute-start(bf16[561,512]{1,0:T(8,128)(2,1)S(1)} %bitcast.77), channel_id=1, source_target_pairs={{0,1},{1,0},{2,3},{3,2},{4,5},{5,4},{6,7},{7,6},{8,9},{9,8},{10,11... | collective-permute-start | bytes 1723400 | tf_op jit(solution)/shard_map/ppermute | solution.py:468
  80.4 12.8 %collective-permute-start.4 = (bf16[561,512]{1,0:T(8,128)(2,1)S(1)}, bf16[561,512]{1,0:T(8,128)(2,1)S(1)}, u32[]{:S(2)}, u32[]{:S(2)}) collective-permute-start(bf16[561,512]{1,0:T(8,128)(2,1)S(1)} %bitcast.79), channel_id=1, source_target_pairs={{0,1},{1,0},{2,3},{3,2},{4,5},{5,4},{6,7},{7,6},{8,9},{9,8},{10,11... | collective-permute-start | bytes 1723400 | tf_op jit(solution)/shard_map/ppermute | solution.py:468
  104.2 24.9 %collective-permute-start.5 = (bf16[561,1024]{1,0:T(8,128)(2,1)}, bf16[561,1024]{1,0:T(8,128)(2,1)}, u32[]{:S(2)}, u32[]{:S(2)}) collective-permute-start(bf16[561,1024]{1,0:T(8,128)(2,1)} %convolution_convert_fusion.4), channel_id=1, source_target_pairs={{0,1},{1,0},{2,3},{3,2},{4,5},{5,4},{6,7},{7,6},{8,9},{9,8},{10,11... | collective-permute-start | bytes 3446792 | tf_op jit(solution)/shard_map/ppermute | solution.py:476
  144.0 24.6 %collective-permute-start.6 = (bf16[561,1024]{1,0:T(8,128)(2,1)S(1)}, bf16[561,1024]{1,0:T(8,128)(2,1)}, u32[]{:S(2)}, u32[]{:S(2)}) collective-permute-start(bf16[561,1024]{1,0:T(8,128)(2,1)S(1)} %convolution_convert_fusion.3), channel_id=1, source_target_pairs={{0,1},{1,0},{2,3},{3,2},{4,5},{5,4},{6,7},{7,6},{8,9},{9,8},{10,11... | collective-permute-start | bytes 3446792 | tf_op jit(solution)/shard_map/ppermute | solution.py:476
  259.4 124.2 %collective-permute-start.7 = (bf16[561,512]{1,0:T(8,128)(2,1)}, bf16[561,512]{1,0:T(8,128)(2,1)}, u32[]{:S(2)}, u32[]{:S(2)}) collective-permute-start(bf16[561,512]{1,0:T(8,128)(2,1)} %constant_dynamic-slice_fusion), channel_id=1, source_target_pairs={{0,1},{1,0},{2,3},{3,2},{4,5},{5,4},{6,7},{7,6},{8,9},{9,8},{10,11... | collective-permute-start | bytes 1723400 | tf_op jit(solution)/shard_map/ppermute | solution.py:485
  262.9 23.9 %collective-permute-start.16 = (bf16[320,512]{1,0:T(8,128)(2,1)S(1)}, bf16[320,512]{1,0:T(8,128)(2,1)S(1)}, u32[]{:S(2)}, u32[]{:S(2)}) collective-permute-start(bf16[320,512]{1,0:T(8,128)(2,1)S(1)} %broadcast_select_fusion.17), channel_id=1, source_target_pairs={{0,8},{2,10},{4,12},{6,14},{8,0},{10,2},{12,4},{14,6},{16,24},{18,... | collective-permute-start | bytes 983048 | tf_op jit(solution)/shard_map/ppermute | solution.py:404
  264.7 23.1 %collective-permute-start.23 = (bf16[320,512]{1,0:T(8,128)(2,1)S(1)}, bf16[320,512]{1,0:T(8,128)(2,1)S(1)}, u32[]{:S(2)}, u32[]{:S(2)}) collective-permute-start(bf16[320,512]{1,0:T(8,128)(2,1)S(1)} %broadcast_select_fusion.20), channel_id=1, source_target_pairs={{0,4},{2,6},{4,0},{6,2},{8,12},{10,14},{12,8},{14,10},{16,20},{18,... | collective-permute-start | bytes 983048 | tf_op jit(solution)/shard_map/ppermute | solution.py:404
  265.7 24.8 %collective-permute-start.9 = (bf16[320,512]{1,0:T(8,128)(2,1)S(1)}, bf16[320,512]{1,0:T(8,128)(2,1)S(1)}, u32[]{:S(2)}, u32[]{:S(2)}) collective-permute-start(bf16[320,512]{1,0:T(8,128)(2,1)S(1)} %broadcast_select_fusion.23), channel_id=1, source_target_pairs={{0,4},{2,6},{4,0},{6,2},{8,12},{10,14},{12,8},{14,10},{16,20},{18,... | collective-permute-start | bytes 983048 | tf_op jit(solution)/shard_map/ppermute | solution.py:404
  272.7 18.0 %collective-permute-start.31 = (bf16[160,512]{1,0:T(8,128)(2,1)S(1)}, bf16[160,512]{1,0:T(8,128)(2,1)S(1)}, u32[]{:S(2)}, u32[]{:S(2)}) collective-permute-start(bf16[160,512]{1,0:T(8,128)(2,1)S(1)} %broadcast_select_fusion.26), channel_id=1, source_target_pairs={{0,16},{2,18},{4,20},{6,22},{8,24},{10,26},{12,28},{14,30},{16,0},... | collective-permute-start | bytes 491528 | tf_op jit(solution)/shard_map/ppermute | solution.py:404
  287.0 14.2 %collective-permute-start.17 = (bf16[160,512]{1,0:T(8,128)(2,1)S(1)}, bf16[160,512]{1,0:T(8,128)(2,1)S(1)}, u32[]{:S(2)}, u32[]{:S(2)}) collective-permute-start(bf16[160,512]{1,0:T(8,128)(2,1)S(1)} %broadcast_select_fusion.29), channel_id=1, source_target_pairs={{0,16},{2,18},{4,20},{6,22},{8,24},{10,26},{12,28},{14,30},{16,0},... | collective-permute-start | bytes 491528 | tf_op jit(solution)/shard_map/ppermute | solution.py:404
  287.9 15.3 %collective-permute-start.24 = (bf16[160,512]{1,0:T(8,128)(2,1)S(1)}, bf16[160,512]{1,0:T(8,128)(2,1)S(1)}, u32[]{:S(2)}, u32[]{:S(2)}) collective-permute-start(bf16[160,512]{1,0:T(8,128)(2,1)S(1)} %broadcast_select_fusion.32), channel_id=1, source_target_pairs={{0,8},{2,10},{4,12},{6,14},{8,0},{10,2},{12,4},{14,6},{16,24},{18,... | collective-permute-start | bytes 491528 | tf_op jit(solution)/shard_map/ppermute | solution.py:404
  290.6 19.6 %collective-permute-start.10 = (bf16[160,512]{1,0:T(8,128)(2,1)S(1)}, bf16[160,512]{1,0:T(8,128)(2,1)S(1)}, u32[]{:S(2)}, u32[]{:S(2)}) collective-permute-start(bf16[160,512]{1,0:T(8,128)(2,1)S(1)} %broadcast_select_fusion.35), channel_id=1, source_target_pairs={{0,8},{2,10},{4,12},{6,14},{8,0},{10,2},{12,4},{14,6},{16,24},{18,... | collective-permute-start | bytes 491528 | tf_op jit(solution)/shard_map/ppermute | solution.py:404
  290.8 22.2 %collective-permute-start.32 = (bf16[80,512]{1,0:T(8,128)(2,1)S(1)}, bf16[80,512]{1,0:T(8,128)(2,1)S(1)}, u32[]{:S(2)}, u32[]{:S(2)}) collective-permute-start(bf16[80,512]{1,0:T(8,128)(2,1)S(1)} %broadcast_select_fusion.38), channel_id=1, source_target_pairs={{0,4},{2,6},{4,0},{6,2},{8,12},{10,14},{12,8},{14,10},{16,20},{18,... | collective-permute-start | bytes 245768 | tf_op jit(solution)/shard_map/ppermute | solution.py:404
  301.3 13.5 %collective-permute-start.18 = (bf16[80,512]{1,0:T(8,128)(2,1)S(1)}, bf16[80,512]{1,0:T(8,128)(2,1)S(1)}, u32[]{:S(2)}, u32[]{:S(2)}) collective-permute-start(bf16[80,512]{1,0:T(8,128)(2,1)S(1)} %broadcast_select_fusion.41), channel_id=1, source_target_pairs={{0,4},{2,6},{4,0},{6,2},{8,12},{10,14},{12,8},{14,10},{16,20},{18,... | collective-permute-start | bytes 245768 | tf_op jit(solution)/shard_map/ppermute | solution.py:404
  315.3 12.6 %collective-permute-start.26 = (bf16[80,512]{1,0:T(8,128)(2,1)S(1)}, bf16[80,512]{1,0:T(8,128)(2,1)S(1)}, u32[]{:S(2)}, u32[]{:S(2)}) collective-permute-start(bf16[80,512]{1,0:T(8,128)(2,1)S(1)} %add_convert_fusion.14), channel_id=1, source_target_pairs={{0,16},{2,18},{4,20},{6,22},{8,24},{10,26},{12,28},{14,30},{16,0},... | collective-permute-start | bytes 245768 | tf_op jit(solution)/shard_map/ppermute | solution.py:404
  321.3 13.7 %collective-permute-start.12 = (bf16[80,512]{1,0:T(8,128)(2,1)S(1)}, bf16[80,512]{1,0:T(8,128)(2,1)S(1)}, u32[]{:S(2)}, u32[]{:S(2)}) collective-permute-start(bf16[80,512]{1,0:T(8,128)(2,1)S(1)} %add_convert_fusion.16), channel_id=1, source_target_pairs={{0,16},{2,18},{4,20},{6,22},{8,24},{10,26},{12,28},{14,30},{16,0},... | collective-permute-start | bytes 245768 | tf_op jit(solution)/shard_map/ppermute | solution.py:404
  321.5 23.4 %collective-permute-start.34 = (bf16[160,512]{1,0:T(8,128)(2,1)S(1)}, bf16[160,512]{1,0:T(8,128)(2,1)S(1)}, u32[]{:S(2)}, u32[]{:S(2)}) collective-permute-start(bf16[160,512]{1,0:T(8,128)(2,1)S(1)} %pad_maximum_fusion.21), channel_id=1, source_target_pairs={{0,16},{2,18},{4,20},{6,22},{8,24},{10,26},{12,28},{14,30},{16,0},... | collective-permute-start | bytes 491528 | tf_op jit(solution)/shard_map/ppermute | solution.py:404
  324.5 27.1 %collective-permute-start.20 = (bf16[160,512]{1,0:T(8,128)(2,1)S(1)}, bf16[160,512]{1,0:T(8,128)(2,1)S(1)}, u32[]{:S(2)}, u32[]{:S(2)}) collective-permute-start(bf16[160,512]{1,0:T(8,128)(2,1)S(1)} %pad_maximum_fusion.19), channel_id=1, source_target_pairs={{0,16},{2,18},{4,20},{6,22},{8,24},{10,26},{12,28},{14,30},{16,0},... | collective-permute-start | bytes 491528 | tf_op jit(solution)/shard_map/ppermute | solution.py:404
  328.0 23.7 %collective-permute-start.27 = (bf16[160,512]{1,0:T(8,128)(2,1)S(1)}, bf16[160,512]{1,0:T(8,128)(2,1)S(1)}, u32[]{:S(2)}, u32[]{:S(2)}) collective-permute-start(bf16[160,512]{1,0:T(8,128)(2,1)S(1)} %pad_maximum_fusion.20), channel_id=1, source_target_pairs={{0,8},{2,10},{4,12},{6,14},{8,0},{10,2},{12,4},{14,6},{16,24},{18,... | collective-permute-start | bytes 491528 | tf_op jit(solution)/shard_map/ppermute | solution.py:404
  335.0 19.0 %collective-permute-start.13 = (bf16[160,512]{1,0:T(8,128)(2,1)S(1)}, bf16[160,512]{1,0:T(8,128)(2,1)S(1)}, u32[]{:S(2)}, u32[]{:S(2)}) collective-permute-start(bf16[160,512]{1,0:T(8,128)(2,1)S(1)} %pad_maximum_fusion.18), channel_id=1, source_target_pairs={{0,8},{2,10},{4,12},{6,14},{8,0},{10,2},{12,4},{14,6},{16,24},{18,... | collective-permute-start | bytes 491528 | tf_op jit(solution)/shard_map/ppermute | solution.py:404
  344.9 23.2 %collective-permute-start.35 = (bf16[320,512]{1,0:T(8,128)(2,1)S(1)}, bf16[320,512]{1,0:T(8,128)(2,1)S(1)}, u32[]{:S(2)}, u32[]{:S(2)}) collective-permute-start(bf16[320,512]{1,0:T(8,128)(2,1)S(1)} %pad_maximum_fusion.17), channel_id=1, source_target_pairs={{0,8},{2,10},{4,12},{6,14},{8,0},{10,2},{12,4},{14,6},{16,24},{18,... | collective-permute-start | bytes 983048 | tf_op jit(solution)/shard_map/ppermute | solution.py:404
  351.6 27.3 %collective-permute-start.21 = (bf16[320,512]{1,0:T(8,128)(2,1)S(1)}, bf16[320,512]{1,0:T(8,128)(2,1)S(1)}, u32[]{:S(2)}, u32[]{:S(2)}) collective-permute-start(bf16[320,512]{1,0:T(8,128)(2,1)S(1)} %pad_maximum_fusion.15), channel_id=1, source_target_pairs={{0,8},{2,10},{4,12},{6,14},{8,0},{10,2},{12,4},{14,6},{16,24},{18,... | collective-permute-start | bytes 983048 | tf_op jit(solution)/shard_map/ppermute | solution.py:404
  351.8 28.1 %collective-permute-start.28 = (bf16[320,512]{1,0:T(8,128)(2,1)S(1)}, bf16[320,512]{1,0:T(8,128)(2,1)S(1)}, u32[]{:S(2)}, u32[]{:S(2)}) collective-permute-start(bf16[320,512]{1,0:T(8,128)(2,1)S(1)} %pad_maximum_fusion.16), channel_id=1, source_target_pairs={{0,4},{2,6},{4,0},{6,2},{8,12},{10,14},{12,8},{14,10},{16,20},{18,... | collective-permute-start | bytes 983048 | tf_op jit(solution)/shard_map/ppermute | solution.py:404
  354.2 25.8 %collective-permute-start.14 = (bf16[320,512]{1,0:T(8,128)(2,1)S(1)}, bf16[320,512]{1,0:T(8,128)(2,1)S(1)}, u32[]{:S(2)}, u32[]{:S(2)}) collective-permute-start(bf16[320,512]{1,0:T(8,128)(2,1)S(1)} %pad_maximum_fusion.14), channel_id=1, source_target_pairs={{0,4},{2,6},{4,0},{6,2},{8,12},{10,14},{12,8},{14,10},{16,20},{18,... | collective-permute-start | bytes 983048 | tf_op jit(solution)/shard_map/ppermute | solution.py:404
  381.9 16.2 %collective-permute-start.36 = (bf16[640,512]{1,0:T(8,128)(2,1)}, bf16[640,512]{1,0:T(8,128)(2,1)S(1)}, u32[]{:S(2)}, u32[]{:S(2)}) collective-permute-start(bf16[640,512]{1,0:T(8,128)(2,1)} %pad_maximum_fusion.10), channel_id=1, source_target_pairs={{0,2},{2,0},{4,6},{6,4},{8,10},{10,8},{12,14},{14,12},{16,18},{18,... | collective-permute-start | bytes 1966088 | tf_op jit(solution)/shard_map/ppermute | solution.py:404
  383.0 15.5 %collective-permute-start.37 = (bf16[640,512]{1,0:T(8,128)(2,1)}, bf16[640,512]{1,0:T(8,128)(2,1)S(1)}, u32[]{:S(2)}, u32[]{:S(2)}) collective-permute-start(bf16[640,512]{1,0:T(8,128)(2,1)} %pad_maximum_fusion.11), channel_id=1, source_target_pairs={{0,2},{2,0},{4,6},{6,4},{8,10},{10,8},{12,14},{14,12},{16,18},{18,... | collective-permute-start | bytes 1966088 | tf_op jit(solution)/shard_map/ppermute | solution.py:404
  386.2 13.4 %collective-permute-start.38 = (bf16[640,512]{1,0:T(8,128)(2,1)S(1)}, bf16[640,512]{1,0:T(8,128)(2,1)S(1)}, u32[]{:S(2)}, u32[]{:S(2)}) collective-permute-start(bf16[640,512]{1,0:T(8,128)(2,1)S(1)} %copy-done.4), channel_id=1, source_target_pairs={{0,2},{2,0},{4,6},{6,4},{8,10},{10,8},{12,14},{14,12},{16,18},{18,... | collective-permute-start | bytes 1966088 | tf_op jit(solution)/shard_map/ppermute | solution.py:404
  386.2 13.8 %collective-permute-start.39 = (bf16[640,512]{1,0:T(8,128)(2,1)S(1)}, bf16[640,512]{1,0:T(8,128)(2,1)S(1)}, u32[]{:S(2)}, u32[]{:S(2)}) collective-permute-start(bf16[640,512]{1,0:T(8,128)(2,1)S(1)} %pad_maximum_fusion.13), channel_id=1, source_target_pairs={{0,2},{2,0},{4,6},{6,4},{8,10},{10,8},{12,14},{14,12},{16,18},{18,... | collective-permute-start | bytes 1966088 | tf_op jit(solution)/shard_map/ppermute | solution.py:404
  (39 other events, 346.7 us)
Sparse Core Ops, SparseCore 0:
  156.8 224.6 all-reduce.4
